TPU v7x, 32 devices: a whole 2x2x4 slice. The times are simulated.
32 devices in a mesh: grp: 4 (over x, core), ep: 8 (over z, y).
Axes of the slice: x: 2, y: 2, z: 4, core: 2. Of those that a mesh axis runs over, the one named last changes fastest.
Arguments:
- tokens: bfloat16 [32768, 512], P(('grp', 'ep')), may hold values from -6 to 6
- segments: int32 [128, 256], P(('grp', 'ep')), may hold values from 0 to 7, never falling along the last dimension, each value on 1 to 128 neighbouring positions
- patch_mask: int32 [128, 256], P(('grp', 'ep')), may hold values 0 or 1
- choices: int32 [32768, 2], P(('grp', 'ep')), may hold values from 0 to 7, all different within a row
- priority: int32 [32, 1024], P(('grp', 'ep')), may hold values from 0 to 1023, each once within a row
- first_gain: bfloat16 [512], P(('grp', 'ep')), may hold values from 0.5 to 1.5
- joint_weight: bfloat16 [512, 1536], P(('grp', 'ep')), may hold values from -0.25 to 0.25
- output_weight: bfloat16 [512, 512], P(('grp', 'ep')), may hold values from -1 to 1
- second_gain: bfloat16 [512], P(('grp', 'ep')), may hold values from 0.5 to 1.5
- router_weight: bfloat16 [512, 8], P(('grp', 'ep')), may hold values from -0.19921875 to 0.19921875
- expert_up: bfloat16 [8, 512, 2048], P('ep'), may hold values from -0.25 to 0.25
- expert_down: bfloat16 [8, 2048, 512], P('ep'), may hold values from -0.75 to 0.75
- out_grad: bfloat16 [32768, 512], P(('grp', 'ep')), may hold values from -6 to 6
Outputs:
- output: bfloat16 [32768, 512], P(('grp', 'ep'))
- tokens_grad: float32 [32768, 512], P(('grp', 'ep'))
- first_gain_grad: float32 [512], P(('grp', 'ep'))
- joint_weight_grad: float32 [512, 1536], P(('grp', 'ep'))
- output_weight_grad: float32 [512, 512], P(('grp', 'ep'))
- second_gain_grad: float32 [512], P(('grp', 'ep'))
- router_weight_grad: float32 [512, 8], P(('grp', 'ep'))
- expert_up_grad: float32 [8, 512, 2048], P('ep')
- expert_down_grad: float32 [8, 2048, 512], P('ep')
Inputs may be any that keep to these rules, and one draw needn't show every extreme that they name: `segments`: within a sequence the ids never fall. `choices`: a token's two experts differ. `priority`: each row holds every number below 1024 once.
All inputs are finite; a program needn't handle non-finite values. No bound on the sum of `patch_mask` on one device may be relied on, other than what follows from the above.
Results may differ from a plain program's by a relative error of at most 0.013.
Values may be sent and summed in bfloat16 or wider, within the bound.
A program may use at most 192 MiB of HBM per device.

v0:
```python
import jax
import jax.numpy as jnp
from jax import lax
from jax.sharding import PartitionSpec as P

HEADS = 8


EPSILON = 1e-06
NEGATIVE = -1e30


def normalize(values, gain):
    mean = jnp.mean(values, axis=-1, keepdims=True)
    centred = values - mean
    inverse = lax.rsqrt(jnp.mean(centred * centred, axis=-1, keepdims=True) + EPSILON)
    unit = centred * inverse
    return (unit * gain, unit, inverse)


def normalize_back(incoming, gain, unit, inverse):
    scaled = incoming * gain
    inner = (
        scaled
        - jnp.mean(scaled, axis=-1, keepdims=True)
        - unit * jnp.mean(scaled * unit, axis=-1, keepdims=True)
    )
    return (inverse * inner, jnp.sum(incoming * unit, axis=0))


def outer(left, right):
    return lax.dot_general(
        left, right, (((0,), (0,)), ((), ())), preferred_element_type=jnp.float32
    )


def times_t(left, right):
    return lax.dot_general(
        left, right, (((1,), (1,)), ((), ())), preferred_element_type=jnp.float32
    )


def gelu_slope(values):
    normal_cdf = 0.5 * (1.0 + lax.erf(values * 0.7071067811865476))
    density = jnp.exp(-0.5 * values * values) * 0.3989422804014327
    return normal_cdf + values * density


def route(picks, live, ranks, expert_count, capacity):
    row_count = picks.shape[0]
    labels = lax.broadcasted_iota(jnp.int32, (row_count, expert_count), 1)
    first = (picks[:, 0:1] == labels).astype(jnp.int32)
    second = (picks[:, 1:2] == labels).astype(jnp.int32)
    live_col = live[:, None]
    earlier = (ranks[None, :] < ranks[:, None]).astype(jnp.int32)
    first_live = first * live_col
    second_live = second * live_col
    place_one = jnp.sum(
        jnp.dot(earlier, first_live, preferred_element_type=jnp.int32) * first, axis=1
    )
    ahead = (
        jnp.dot(earlier, second_live, preferred_element_type=jnp.int32)
        + jnp.sum(first_live, axis=0)[None, :]
    )
    place_two = jnp.sum(ahead * second, axis=1)
    keep_one = (live > 0) & (place_one < capacity)
    keep_two = (live > 0) & (place_two < capacity)
    dummy = expert_count * capacity
    slot_one = jnp.where(keep_one, picks[:, 0] * capacity + place_one, dummy)
    slot_two = jnp.where(keep_two, picks[:, 1] * capacity + place_two, dummy)
    pick_one = (first * keep_one[:, None].astype(jnp.int32)).astype(jnp.float32)
    pick_two = (second * keep_two[:, None].astype(jnp.int32)).astype(jnp.float32)
    return (slot_one, slot_two, pick_one, pick_two)


def visible(group, live):
    rows = group.shape[0]
    index = lax.broadcasted_iota(jnp.int32, (rows, rows), 0)
    other = lax.broadcasted_iota(jnp.int32, (rows, rows), 1)
    return (group[:, None] == group[None, :]) & ((live[None, :] > 0) | (index == other))


def attend_forward(query, key, value, allowed, factor):
    scores = jnp.einsum("qhd,khd->hqk", query, key, preferred_element_type=jnp.float32) * factor
    masked = jnp.where(allowed[None], scores, NEGATIVE)
    top = jnp.max(masked, axis=-1, keepdims=True)
    weights = jnp.exp(masked - top)
    total = jnp.sum(weights, axis=-1, keepdims=True)
    probs = (weights / total).astype(jnp.bfloat16)
    mixed = jnp.einsum("hqk,khd->qhd", probs, value, preferred_element_type=jnp.float32)
    return (mixed, top + jnp.log(total))


def attend_backward(query, key, value, allowed, log_total, grad_mixed, factor):
    scores = jnp.einsum("qhd,khd->hqk", query, key, preferred_element_type=jnp.float32) * factor
    masked = jnp.where(allowed[None], scores, NEGATIVE)
    probs = jnp.exp(masked - log_total)
    grad_value = jnp.einsum(
        "hqk,qhd->khd", probs.astype(jnp.bfloat16), grad_mixed, preferred_element_type=jnp.float32
    )
    grad_probs = jnp.einsum("qhd,khd->hqk", grad_mixed, value, preferred_element_type=jnp.float32)
    delta = jnp.sum(probs * grad_probs, axis=-1, keepdims=True)
    grad_scores = (probs * (grad_probs - delta)).astype(jnp.bfloat16)
    grad_query = (
        jnp.einsum("hqk,khd->qhd", grad_scores, key, preferred_element_type=jnp.float32) * factor
    )
    grad_key = (
        jnp.einsum("hqk,qhd->khd", grad_scores, query, preferred_element_type=jnp.float32) * factor
    )
    return jnp.stack([grad_query, grad_key, grad_value], axis=1)


def per_device(
    tokens,
    segments,
    patch_mask,
    choices,
    priority,
    first_gain,
    joint_weight,
    output_weight,
    second_gain,
    router_weight,
    expert_up,
    expert_down,
    out_grad,
):
    row_count, width = tokens.shape
    head_size = width // HEADS
    factor = head_size ** (-0.5)
    expert_count = router_weight.shape[1]
    length = segments.shape[1]
    capacity = (21 * choices.shape[1] * row_count + 20 * expert_count - 1) // (20 * expert_count)
    block_rows = min(row_count, 512)
    gain_one, joint_full, output_full, gain_two, router_full = (
        lax.all_gather(first_gain, ("grp", "ep"), axis=0, tiled=True),
        lax.all_gather(joint_weight, ("grp", "ep"), axis=0, tiled=True),
        lax.all_gather(output_weight, ("grp", "ep"), axis=0, tiled=True),
        lax.all_gather(second_gain, ("grp", "ep"), axis=0, tiled=True),
        lax.all_gather(router_weight, ("grp", "ep"), axis=0, tiled=True),
    )
    inputs = tokens.astype(jnp.float32)
    gain_one = gain_one.astype(jnp.float32)
    gain_two = gain_two.astype(jnp.float32)
    normed_f, unit_one, inverse_one = normalize(inputs, gain_one)
    normed = normed_f.astype(jnp.bfloat16)
    joint = jnp.dot(normed, joint_full, preferred_element_type=jnp.float32).astype(jnp.bfloat16)
    joint = joint.reshape(row_count, 3, HEADS, head_size)
    live = patch_mask.reshape(row_count)
    position = lax.broadcasted_iota(jnp.int32, (row_count,), 0)
    group = position // length * length + segments.reshape(row_count)
    masks = []
    mixed_parts = []
    log_parts = []
    for start in range(0, row_count, block_rows):
        allowed = visible(group[start : start + block_rows], live[start : start + block_rows])
        block = joint[start : start + block_rows]
        mixed_block, log_total = attend_forward(
            block[:, 0], block[:, 1], block[:, 2], allowed, factor
        )
        masks.append(allowed)
        mixed_parts.append(mixed_block)
        log_parts.append(log_total)
    mixed = jnp.concatenate(mixed_parts, axis=0).reshape(row_count, width).astype(jnp.bfloat16)
    state = inputs + jnp.dot(mixed, output_full, preferred_element_type=jnp.float32)
    normed_two_f, unit_two, inverse_two = normalize(state, gain_two)
    normed_two = normed_two_f.astype(jnp.bfloat16)
    logits = jnp.dot(normed_two, router_full, preferred_element_type=jnp.float32)
    gate = jax.nn.softmax(logits, axis=-1)
    slot_one, slot_two, pick_one, pick_two = route(
        choices, live, priority.reshape(row_count), expert_count, capacity
    )
    gate_one = jnp.sum(gate * pick_one, axis=1)
    gate_two = jnp.sum(gate * pick_two, axis=1)
    empty = jnp.zeros((expert_count * capacity + 1, width), jnp.bfloat16)
    outgoing = empty.at[slot_one].add(normed_two).at[slot_two].add(normed_two)
    outgoing = outgoing[: expert_count * capacity].reshape(expert_count, capacity, width)
    arrived = lax.all_to_all(outgoing, "ep", split_axis=0, concat_axis=1, tiled=True)
    pre = jnp.einsum("erd,edf->erf", arrived, expert_up, preferred_element_type=jnp.float32)
    act = jax.nn.gelu(pre, approximate=False).astype(jnp.bfloat16)
    produced = jnp.einsum(
        "erf,efd->erd", act, expert_down, preferred_element_type=jnp.float32
    ).astype(jnp.bfloat16)
    returned = lax.all_to_all(produced, "ep", split_axis=1, concat_axis=0, tiled=True)
    zero_row = jnp.zeros((1, width), jnp.bfloat16)
    flat = jnp.concatenate([returned.reshape(expert_count * capacity, width), zero_row], axis=0)
    got_one = flat[slot_one].astype(jnp.float32)
    got_two = flat[slot_two].astype(jnp.float32)
    output = (state + gate_one[:, None] * got_one + gate_two[:, None] * got_two).astype(
        jnp.bfloat16
    )
    grad = out_grad.astype(jnp.float32)
    grad_gate = (
        pick_one * jnp.sum(grad * got_one, axis=1)[:, None]
        + pick_two * jnp.sum(grad * got_two, axis=1)[:, None]
    )
    grad_logits = (gate * (grad_gate - jnp.sum(gate * grad_gate, axis=1, keepdims=True))).astype(
        jnp.bfloat16
    )
    grad_router = outer(normed_two, grad_logits)
    grad_normed_two = times_t(grad_logits, router_full)
    weighted_one = (gate_one[:, None] * grad).astype(jnp.bfloat16)
    weighted_two = (gate_two[:, None] * grad).astype(jnp.bfloat16)
    grad_out_rows = empty.at[slot_one].add(weighted_one).at[slot_two].add(weighted_two)
    grad_out_rows = grad_out_rows[: expert_count * capacity].reshape(expert_count, capacity, width)
    grad_arrived = lax.all_to_all(grad_out_rows, "ep", split_axis=0, concat_axis=1, tiled=True)
    rows_now = lax.all_to_all(outgoing, "ep", split_axis=0, concat_axis=1, tiled=True)
    pre_now = jnp.einsum("erd,edf->erf", rows_now, expert_up, preferred_element_type=jnp.float32)
    act_now = jax.nn.gelu(pre_now, approximate=False).astype(jnp.bfloat16)
    grad_down = jnp.einsum(
        "erf,erd->efd", act_now, grad_arrived, preferred_element_type=jnp.float32
    )
    grad_act = jnp.einsum(
        "erd,efd->erf", grad_arrived, expert_down, preferred_element_type=jnp.float32
    )
    grad_pre = (grad_act * gelu_slope(pre_now)).astype(jnp.bfloat16)
    grad_up = jnp.einsum("erd,erf->edf", rows_now, grad_pre, preferred_element_type=jnp.float32)
    grad_rows = jnp.einsum(
        "erf,edf->erd", grad_pre, expert_up, preferred_element_type=jnp.float32
    ).astype(jnp.bfloat16)
    grad_back = lax.all_to_all(grad_rows, "ep", split_axis=1, concat_axis=0, tiled=True)
    flat_grad = jnp.concatenate(
        [grad_back.reshape(expert_count * capacity, width), zero_row], axis=0
    )
    grad_normed_two = (
        grad_normed_two
        + flat_grad[slot_one].astype(jnp.float32)
        + flat_grad[slot_two].astype(jnp.float32)
    )
    grad_state_in, grad_gain_two = normalize_back(grad_normed_two, gain_two, unit_two, inverse_two)
    grad_state = grad + grad_state_in
    grad_branch = grad_state.astype(jnp.bfloat16)
    grad_output_w = outer(mixed, grad_branch)
    grad_mixed = (
        times_t(grad_branch, output_full).astype(jnp.bfloat16).reshape(row_count, HEADS, head_size)
    )
    grad_parts = []
    for number, start in enumerate(range(0, row_count, block_rows)):
        block = joint[start : start + block_rows]
        grad_parts.append(
            attend_backward(
                block[:, 0],
                block[:, 1],
                block[:, 2],
                masks[number],
                log_parts[number],
                grad_mixed[start : start + block_rows],
                factor,
            )
        )
    grad_joint = (
        jnp.concatenate(grad_parts, axis=0).reshape(row_count, 3 * width).astype(jnp.bfloat16)
    )
    grad_joint_w = outer(normed, grad_joint)
    grad_normed = times_t(grad_joint, joint_full)
    grad_inputs_in, grad_gain_one = normalize_back(grad_normed, gain_one, unit_one, inverse_one)
    tokens_grad = grad_state + grad_inputs_in
    shares = (
        lax.psum_scatter(grad_gain_one, ("grp", "ep"), scatter_dimension=0, tiled=True),
        lax.psum_scatter(grad_joint_w, ("grp", "ep"), scatter_dimension=0, tiled=True),
        lax.psum_scatter(grad_output_w, ("grp", "ep"), scatter_dimension=0, tiled=True),
        lax.psum_scatter(grad_gain_two, ("grp", "ep"), scatter_dimension=0, tiled=True),
        lax.psum_scatter(grad_router, ("grp", "ep"), scatter_dimension=0, tiled=True),
    )
    grad_up, grad_down = (
        lax.psum(grad_up.astype(jnp.bfloat16), "grp").astype(jnp.float32),
        lax.psum(grad_down.astype(jnp.bfloat16), "grp").astype(jnp.float32),
    )
    return (
        output,
        tokens_grad,
        shares[0],
        shares[1],
        shares[2],
        shares[3],
        shares[4],
        grad_up,
        grad_down,
    )


def solution(mesh):
    in_specs = (
        P(("grp", "ep"), None),
        P(("grp", "ep"), None),
        P(("grp", "ep"), None),
        P(("grp", "ep"), None),
        P(("grp", "ep"), None),
        P(("grp", "ep")),
        P(("grp", "ep"), None),
        P(("grp", "ep"), None),
        P(("grp", "ep")),
        P(("grp", "ep"), None),
        P("ep", None, None),
        P("ep", None, None),
        P(("grp", "ep"), None),
    )
    out_specs = (
        P(("grp", "ep"), None),
        P(("grp", "ep"), None),
        P(("grp", "ep")),
        P(("grp", "ep"), None),
        P(("grp", "ep"), None),
        P(("grp", "ep")),
        P(("grp", "ep"), None),
        P("ep", None, None),
        P("ep", None, None),
    )
    return jax.shard_map(
        per_device, mesh=mesh, in_specs=in_specs, out_specs=out_specs, check_vma=False
    )
```

profile of v0, /device:TPU:0, one launch (start us, length us, event | category | flops | bytes accessed | tf_op | source)
XLA Modules:
  0.0 1114.1 jit_solution(8089762748541029859)
XLA Ops:
  11.2 42.1 %all-reduce.7 = (bf16[512]{0:T(512)(128)(2,1)S(1)}, bf16[512]{0:T(512)(128)(2,1)S(1)}) all-reduce(bf16[512]{0:T(512)(128)(2,1)S(1)} %dynamic-update-slice, bf16[512]{0:T(512)(128)(2,1)S(1)} %dynamic-update-slice.1), channel_id=1, replica_groups=mesh['grp'=4,'ep'=8] {'grp','ep'}, use_global_device_ids=true, to_apply=%add.2 | all-reduce | flops 1024 | bytes 4096
  65.6 74.1 %all_gather.17 = bf16[512,512]{1,0:T(8,128)(2,1)} all-gather(bf16[16,512]{1,0:T(8,128)(2,1)S(1)} %copy-done.51), channel_id=1, replica_groups=mesh['grp'=4,'ep'=8] {'grp','ep'}, dimensions={0}, use_global_device_ids=true | all-gather | bytes 540672 | tf_op jit(solution)/shard_map/all_gather | solution.py:138
  173.4 9.2 scatter_custom_fusion
  182.6 10.6 scatter_fusion
  196.4 3.6 reshape.421
  200.0 53.0 %all_to_all.16 = bf16[8,269,512]{2,1,0:T(8,128)(2,1)} all-to-all(bf16[8,269,512]{2,1,0:T(8,128)(2,1)} %reshape.421), channel_id=1, replica_groups=mesh['grp'=4,'ep'=8] {'ep'}, dimensions={0} | all-to-all | bytes 4407296 | tf_op jit(solution)/shard_map/all_to_all | solution.py:178
  253.0 3.6 reshape.422
  256.7 43.5 %fusion.2 = (bf16[2152,2048]{1,0:T(8,128)(2,1)S(1)}, f32[2152,2048]{1,0:T(8,128)}) fusion(bf16[2152,512]{1,0:T(8,128)(2,1)} %reshape.422, bf16[1,512,2048]{2,1,0:T(8,128)(2,1)S(1)} %copy-done), kind=kOutput, calls=%fused_computation.12 | convolution fusion | flops 4799545344 | bytes 30744576 | tf_op jit(solution)/shard_map/erd,edf->erf/dot_general | solution.py:179
  300.2 5.7 fusion.32
  305.9 16.4 %copy.139 = bf16[1,2152,512]{2,0,1:T(2,128)(2,1)} copy(bf16[1,2152,512]{2,1,0:T(8,128)(2,1)S(1)} %fusion.32) | data formatting | bytes 4407296 | tf_op jit(solution)/shard_map/convert_element_type | solution.py:183
  322.8 16.5 %reduce = bf16[2152,512]{1,0:T(8,128)(2,1)} reduce(bf16[2152,1,512]{2,1,0:T(2,128)(2,1)} %bitcast.160, bf16[]{:T(256)} %broadcast.495), dimensions={1}, to_apply=%bitcast.153.reduce_sub_computation | reduce | bytes 4407298
  339.4 3.8 reshape.505
  343.2 4.4 all-to-all-start.1
  349.1 102.5 %all-gather = bf16[32,16,8]{1,2,0:T(8,128)(2,1)S(1)} all-gather(bf16[1,16,8]{1,2,0:T(8,128)(2,1)S(1)} %bitcast.205), channel_id=1, replica_groups=mesh['grp'=4,'ep'=8] {'grp','ep'}, dimensions={0}, use_global_device_ids=true | all-gather | bytes 8448 | tf_op jit(solution)/shard_map/all_gather | solution.py:140
  453.4 7.9 reshape.506
  465.7 7.0 gather_fusion.1
  475.0 7.0 gather_fusion
  492.9 9.0 scatter_custom_fusion.2
  501.9 10.6 scatter_fusion.1
  515.6 3.6 reshape.426
  519.3 52.0 %all_to_all.17 = bf16[8,269,512]{2,1,0:T(8,128)(2,1)} all-to-all(bf16[8,269,512]{2,1,0:T(8,128)(2,1)} %reshape.426), channel_id=1, replica_groups=mesh['grp'=4,'ep'=8] {'ep'}, dimensions={0} | all-to-all | bytes 4407296 | tf_op jit(solution)/shard_map/all_to_all | solution.py:206
  571.3 3.6 reshape.427
  574.9 13.4 %fusion.8 = bf16[2152,2048]{1,0:T(8,128)(2,1)S(1)} fusion(f32[2152,2048]{1,0:T(8,128)} %get-tuple-element.87, bf16[2152,512]{1,0:T(8,128)(2,1)} %reshape.427, bf16[1,2048,512]{2,1,0:T(8,128)(2,1)} %param.24), kind=kOutput, calls=%fused_computation.18 | convolution fusion | flops 4557144064 | bytes 30744576 | tf_op jit(solution)/shard_map/erd,efd->erf/dot_general | solution.py:213
  588.3 5.3 fusion.33
  593.7 16.4 %copy.138 = bf16[1,2152,512]{2,0,1:T(2,128)(2,1)} copy(bf16[1,2152,512]{2,1,0:T(8,128)(2,1)S(1)} %fusion.33) | data formatting | bytes 4407296 | tf_op jit(solution)/shard_map/convert_element_type | solution.py:220
  610.1 16.1 %reduce.1 = bf16[2152,512]{1,0:T(8,128)(2,1)} reduce(bf16[2152,1,512]{2,1,0:T(2,128)(2,1)} %bitcast.161, bf16[]{:T(256)} %broadcast.495), dimensions={1}, to_apply=%bitcast.152.reduce_sub_computation | reduce | bytes 4407298
  626.2 3.9 reshape.507
  630.1 4.4 all-to-all-start.3
  637.0 9.8 fusion.35
  646.9 9.9 fusion.34
  656.8 26.4 %all-to-all-done.3 = bf16[8,2,68864]{2,1,0:T(2,128)(2,1)} async-done(((bf16[8,2,68864]{2,1,0:T(2,128)(2,1)}), bf16[8,2,68864]{2,1,0:T(2,128)(2,1)}, u32[]{:S(2)}, u32[]{:S(2)}) %all-to-all-start.3) | async-done | bytes 2203680 | tf_op jit(solution)/shard_map/all_to_all | solution.py:221
  683.2 7.9 reshape.508
  695.5 7.0 gather_fusion.2
  702.6 7.0 gather_fusion.3
  714.2 3.4 multiply_reduce_fusion.2
  732.9 5.6 multiply_reduce_fusion
  746.5 3.8 fusion.77
  750.2 4.8 fusion.84
  755.0 4.9 fusion.81
  762.2 3.5 fusion.117
  765.7 12.3 %reduce-scatter.10.cloned.1.call-done = f32[16,8]{1,0:T(8,128)} async-done(((f32[512,8]{1,0:T(8,128)}), f32[16,8]{1,0:T(8,128)}) %reduce-scatter.10.cloned.1.call-update) | async-done | bytes 528
  779.4 85.5 %all-reduce.11.cloned.1.call-done = (bf16[1,512,2048]{2,1,0:T(8,128)(2,1)}, bf16[1,2048,512]{2,1,0:T(8,128)(2,1)}) async-done(((bf16[1,512,2048]{2,1,0:T(8,128)(2,1)}, bf16[1,2048,512]{2,1,0:T(8,128)(2,1)}), (bf16[1,512,2048]{2,1,0:T(8,128)(2,1)}, bf16[1,2048,512]{2,1,0:T(8,128)(2,1)})) %all-reduce.11.cloned.1.call-update) | async-done | bytes 4194320 | tf_op jit(solution)/shard_map/psum | solution.py:266
  864.9 4.3 convert_element_type.178
  873.1 3.5 fusion.47
  876.5 39.7 %all-reduce.6 = (f32[512]{0:T(512)S(1)}, f32[512]{0:T(512)S(1)}) all-reduce(f32[512]{0:T(512)S(1)} %get-tuple-element.47, f32[512]{0:T(512)S(1)} %get-tuple-element.45), channel_id=2, replica_groups=mesh['grp'=4,'ep'=8] {'grp','ep'}, use_global_device_ids=true, to_apply=%region_29.30.clone | all-reduce | flops 1024 | bytes 8192
  917.4 4.2 fusion.46
  925.9 77.0 %reduce-scatter.8.cloned.1.call-done = f32[16,512]{1,0:T(8,128)} async-done(((f32[512,512]{1,0:T(8,128)}), f32[16,512]{1,0:T(8,128)}) %reduce-scatter.8.cloned.1.call-update) | async-done | bytes 32784 | tf_op jit(solution)/shard_map/reduce_scatter | solution.py:261
  1002.9 104.5 %reduce-scatter.6.cloned.1.call-done = f32[16,1536]{1,0:T(8,128)} async-done(((f32[512,1536]{1,0:T(8,128)}), f32[16,1536]{1,0:T(8,128)}) %reduce-scatter.6.cloned.1.call-update) | async-done | bytes 98320 | tf_op jit(solution)/shard_map/reduce_scatter | solution.py:260
  (245 shorter events, 124.5 us)
Async XLA Ops:
  7.2 249.5 %copy-start = (bf16[1,512,2048]{2,1,0:T(8,128)(2,1)S(1)}, bf16[1,512,2048]{2,1,0:T(8,128)(2,1)}, u32[]{:S(2)}) copy-start(bf16[1,512,2048]{2,1,0:T(8,128)(2,1)} %param.23) | copy-start | bytes 6291460
  7.2 57.0 %copy-start.46 = (s32[1024,2]{0,1:T(2,128)S(1)}, s32[1024,2]{0,1:T(2,128)}, u32[]{:S(2)}) copy-start(s32[1024,2]{0,1:T(2,128)} %param.16) | copy-start | bytes 24580
  7.2 58.4 %copy-start.51 = (bf16[16,512]{1,0:T(8,128)(2,1)S(1)}, bf16[16,512]{1,0:T(8,128)(2,1)}, u32[]{:S(2)}) copy-start(bf16[16,512]{1,0:T(8,128)(2,1)} %param.20) | copy-start | bytes 49156
  7.2 132.5 %all-gather.3.cloned.1.call-start = ((), (), s32[]{:S(2)}) async-start(), calls=%async_computation.7 | async-start | bytes 1622016 | tf_op jit(solution)/shard_map/all_gather | solution.py:137
  9.5 159.7 %copy-start.7 = (bf16[1024,512]{0,1:T(8,128)(2,1)}, bf16[1024,512]{0,1:T(8,128)(2,1)S(1)}, u32[]{:S(2)}) copy-start(bf16[1024,512]{0,1:T(8,128)(2,1)S(1)} %copy.92) | copy-start | bytes 3145732
  53.3 89.8 %copy-start.58 = (f32[512]{0:T(512)}, f32[512]{0:T(512)S(1)}, u32[]{:S(2)}) copy-start(f32[512]{0:T(512)S(1)} %convert_element_type.142) | copy-start | bytes 6148
  54.8 115.5 %copy-start.47 = (f32[512]{0:T(512)}, f32[512]{0:T(512)S(1)}, u32[]{:S(2)}) copy-start(f32[512]{0:T(512)S(1)} %convert_element_type.148) | copy-start | bytes 6148
  55.5 8.7 copy-start.42
  57.0 7.2 copy-start.38
  57.0 8.6 copy-start.44
  60.4 3.9 copy-start.54
  63.8 79.3 %copy-start.40 = (f32[1024]{0:T(1024)}, f32[1024]{0:T(1024)S(1)}, u32[]{:S(2)}) copy-start(f32[1024]{0:T(1024)S(1)} %broadcast_multiply_fusion.5) | copy-start | bytes 12292
  64.1 79.0 %copy-start.49 = (f32[1024]{0:T(1024)}, f32[1024]{0:T(1024)S(1)}, u32[]{:S(2)}) copy-start(f32[1024]{0:T(1024)S(1)} %add_rsqrt_fusion.1) | copy-start | bytes 12292
  64.2 109.2 %copy-start.52 = (s32[1024,1]{0,1:T(1,128)}, s32[1024,1]{0,1:T(1,128)S(1)}, u32[]{:S(2)}) copy-start(s32[1024,1]{0,1:T(1,128)S(1)} %get-tuple-element.73) | copy-start | bytes 12292
  172.1 21.1 %copy-start.9 = (bf16[1024,512]{0,1:T(8,128)(2,1)}, bf16[1024,512]{0,1:T(8,128)(2,1)S(1)}, u32[]{:S(2)}) copy-start(bf16[1024,512]{0,1:T(8,128)(2,1)S(1)} %multiply_convert_fusion.2) | copy-start | bytes 3145732
  256.7 43.5 %copy-start.61 = (bf16[1,2048,512]{2,1,0:T(8,128)(2,1)S(1)}, bf16[1,2048,512]{2,1,0:T(8,128)(2,1)}, u32[]{:S(2)}) copy-start(bf16[1,2048,512]{2,1,0:T(8,128)(2,1)} %param.24) | copy-start | bytes 6291460
  300.2 5.7 copy-start.64
  343.2 5.9 copy-start.60
  343.2 108.5 %copy-start.53 = (s32[1024,1]{0,1:T(1,128)S(1)}, s32[1024,1]{0,1:T(1,128)}, u32[]{:S(2)}) copy-start(s32[1024,1]{0,1:T(1,128)} %copy-done.52) | copy-start | bytes 12292
  343.2 108.6 %copy-start.43 = (s32[1,2,4,128]{3,1,2,0:T(2,128)S(1)}, s32[1,2,4,128]{3,1,2,0:T(2,128)}, u32[]{:S(2)}) copy-start(s32[1,2,4,128]{3,1,2,0:T(2,128)} %copy-done.42) | copy-start | bytes 12292
  343.2 108.6 %copy-start.55 = (s32[1024]{0:T(1024)S(1)}, s32[1024]{0:T(1024)}, u32[]{:S(2)}) copy-start(s32[1024]{0:T(1024)} %copy-done.54) | copy-start | bytes 12292
  343.2 108.6 %copy-start.57 = (s32[1024]{0:T(1024)S(1)}, s32[1024]{0:T(1024)}, u32[]{:S(2)}) copy-start(s32[1024]{0:T(1024)} %copy-done.56) | copy-start | bytes 12292
  343.2 110.1 %all-to-all-start.1 = ((bf16[8,2,68864]{2,1,0:T(2,128)(2,1)}), bf16[8,2,68864]{2,1,0:T(2,128)(2,1)}, u32[]{:S(2)}, u32[]{:S(2)}) async-start(bf16[8,2,68864]{2,1,0:T(2,128)(2,1)} %reshape.505), calls=%async_computation.1 | async-start | bytes 4407296 | tf_op jit(solution)/shard_map/all_to_all | solution.py:184
  482.0 4.4 copy-start.39
  482.0 4.5 copy-start.45
  588.3 5.3 copy-start.63
  626.2 8.4 copy-start.27
  626.2 8.4 copy-start.35
  626.2 8.4 copy-start.29
  626.2 8.4 copy-start.37
  630.1 53.2 %all-to-all-start.3 = ((bf16[8,2,68864]{2,1,0:T(2,128)(2,1)}), bf16[8,2,68864]{2,1,0:T(2,128)(2,1)}, u32[]{:S(2)}, u32[]{:S(2)}) async-start(bf16[8,2,68864]{2,1,0:T(2,128)(2,1)} %reshape.507), calls=%async_computation.3 | async-start | bytes 4407296 | tf_op jit(solution)/shard_map/all_to_all | solution.py:221
  634.5 143.6 %reduce-scatter.10.cloned.1.call-start = ((), (), s32[]{:S(2)}) async-start(), calls=%async_computation.10 | async-start | bytes 270336
  637.0 227.9 %all-reduce.11.cloned.1.call-start = ((), (), s32[]{:S(2)}) async-start(), calls=%async_computation.11 | async-start | bytes 8388608 | tf_op jit(solution)/shard_map/psum | solution.py:266
  637.0 9.8 copy-start.20
  656.8 346.1 %reduce-scatter.8.cloned.1.call-start = ((), (), s32[]{:S(2)}) async-start(), calls=%async_computation.9 | async-start | bytes 1081344 | tf_op jit(solution)/shard_map/reduce_scatter | solution.py:261
  709.6 4.6 copy-start.31
  709.6 4.6 copy-start.33
  709.6 4.6 copy-start.48
  717.7 4.7 slice-start.1
  720.0 11.2 %copy-start.6 = (f32[1024,512]{0,1:T(8,128)}, f32[1024,512]{0,1:T(8,128)S(1)}, u32[]{:S(2)}) copy-start(f32[1024,512]{0,1:T(8,128)S(1)} %get-tuple-element.66) | copy-start | bytes 6291460
  732.9 5.6 slice-start.2
  732.9 6.0 slice-start.3
  746.4 361.0 %reduce-scatter.6.cloned.1.call-start = ((), (), s32[]{:S(2)}) async-start(), calls=%async_computation.8 | async-start | bytes 3244032 | tf_op jit(solution)/shard_map/reduce_scatter | solution.py:260
  755.0 5.0 copy-start.22
  755.0 5.0 copy-start.23
  755.0 5.0 copy-start.24
  864.9 4.3 copy-start.21
  869.2 3.9 copy-start.62
  (28 other events, 70.6 us)
Sparse Core Ops, SparseCore 0:
  10.9 57.7 all-gather.2
  637.5 140.4 reduce-scatter.9
  781.2 83.6 all-reduce.10
  867.6 135.2 reduce-scatter.7
  1009.6 97.7 reduce-scatter.5
where the time goes:
time: 1120 us; the launch traced here: 1110 us
  blocking collectives  363 us (32%)
  waiting for transfers between devices  307 us (27%)
  local copies, waits for them, and re-layouts  164 us (15%)
  matrix products  154 us (14%)
  other arithmetic  102 us (9%)
  between operations  15 us (1%)
    reduce_scatter x1, waiting for transfers between devices, per_device(): lax.psum_scatter(grad_joint_w, ('grp', 'ep'), scatter_dimension=0, tiled=...  105 us
    all_gather x1, blocking collectives, per_device(): lax.all_gather(router_weight, ('grp', 'ep'), axis=0, tiled=True)  102 us
    psum x1, waiting for transfers between devices, per_device(): lax.psum(grad_up.astype(jnp.bfloat16), 'grp').astype(jnp.float32)  85.5 us
    unnamed x2, blocking collectives  81.8 us
    reduce_scatter x1, waiting for transfers between devices, per_device(): lax.psum_scatter(grad_output_w, ('grp', 'ep'), scatter_dimension=0, tiled...  77 us
    all_gather x1, blocking collectives, per_device(): lax.all_gather(output_weight, ('grp', 'ep'), axis=0, tiled=True)  74.1 us
    unnamed x160, local copies, waits for them, and re-layouts  56.1 us
    all_to_all x1, blocking collectives, per_device(): lax.all_to_all(outgoing, 'ep', split_axis=0, concat_axis=1, tiled=True)  53 us
  transfers between devices with their start and end apart: 7, of which 5 were waited for; matrix products, arithmetic and copies ran while one was open for 12% of the time, Pallas kernels for 0%

commit v1 on v0

--- a/solution.py
+++ b/solution.py
@@ -1,7 +1,14 @@
+import functools
+
 import jax
 import jax.numpy as jnp
 from jax import lax
+from jax.experimental import pallas as pl
+from jax.experimental.pallas import tpu as pltpu
 from jax.sharding import PartitionSpec as P
+
+MESH = pl.DeviceIdType.MESH
+MIB = 1 << 20
 
 HEADS = 8
 
@@ -38,12 +45,6 @@
     return lax.dot_general(
         left, right, (((1,), (1,)), ((), ())), preferred_element_type=jnp.float32
     )
-
-
-def gelu_slope(values):
-    normal_cdf = 0.5 * (1.0 + lax.erf(values * 0.7071067811865476))
-    density = jnp.exp(-0.5 * values * values) * 0.3989422804014327
-    return normal_cdf + values * density
 
 
 def route(picks, live, ranks, expert_count, capacity):
@@ -65,12 +66,11 @@
     place_two = jnp.sum(ahead * second, axis=1)
     keep_one = (live > 0) & (place_one < capacity)
     keep_two = (live > 0) & (place_two < capacity)
-    dummy = expert_count * capacity
-    slot_one = jnp.where(keep_one, picks[:, 0] * capacity + place_one, dummy)
-    slot_two = jnp.where(keep_two, picks[:, 1] * capacity + place_two, dummy)
-    pick_one = (first * keep_one[:, None].astype(jnp.int32)).astype(jnp.float32)
-    pick_two = (second * keep_two[:, None].astype(jnp.int32)).astype(jnp.float32)
-    return (slot_one, slot_two, pick_one, pick_two)
+    stride = -(-capacity // 16) * 16
+    dummy = expert_count * stride
+    slot_one = jnp.where(keep_one, picks[:, 0] * stride + place_one, dummy)
+    slot_two = jnp.where(keep_two, picks[:, 1] * stride + place_two, dummy)
+    return (slot_one, slot_two)
 
 
 def visible(group, live):
@@ -108,6 +108,229 @@
         jnp.einsum("hqk,qhd->khd", grad_scores, query, preferred_element_type=jnp.float32) * factor
     )
     return jnp.stack([grad_query, grad_key, grad_value], axis=1)
+
+
+def partner(me, step, count):
+    other, bit = 0, 1
+    while bit < count:
+        other = other + bit * lax.rem(lax.div(me, bit) + lax.div(step, bit), 2)
+        bit *= 2
+    return other
+
+
+def expert_kernel(
+    count,
+    experts,
+    sent_rows,
+    sent_grads,
+    up_ref,
+    down_ref,
+    router_ref,
+    back_ref,
+    ret_ref,
+    grad_up_ref,
+    grad_down_ref,
+    grad_router_ref,
+    rows,
+    grads,
+    gated,
+    act,
+    grad_pre,
+    logit_grads,
+    out_grads,
+    out_ret,
+    turned,
+    sems,
+    local_sem,
+):
+    me = lax.axis_index("ep")
+    block, width = rows.shape[1:]
+    hidden = up_ref.shape[1]
+    chunk = 512
+    barrier = pltpu.get_barrier_semaphore()
+
+    def greet(step, carry):
+        pl.semaphore_signal(
+            barrier, inc=1, device_id={"ep": partner(me, step, count)}, device_id_type=MESH
+        )
+        return carry
+
+    lax.fori_loop(1, count, greet, 0)
+    pl.semaphore_wait(barrier, count - 1)
+
+    def remote(kind, source, target, step):
+        return pltpu.make_async_remote_copy(
+            src_ref=source,
+            dst_ref=target,
+            send_sem=sems.at[2 * kind, step],
+            recv_sem=sems.at[2 * kind + 1, step],
+            device_id={"ep": partner(me, step, count)},
+            device_id_type=MESH,
+        )
+
+    def send_rows(step):
+        return remote(0, sent_rows.at[partner(me, step, count)], rows.at[step], step)
+
+    def send_grads(step):
+        return remote(1, sent_grads.at[partner(me, step, count)], grads.at[step], step)
+
+    def send_back(step):
+        return remote(2, out_grads.at[step], back_ref.at[me], step)
+
+    def send_ret(step):
+        return remote(3, out_ret.at[step], ret_ref.at[me], step)
+
+    own = [
+        pltpu.make_async_copy(sent_rows.at[me], rows.at[0], local_sem.at[0]),
+        pltpu.make_async_copy(sent_grads.at[me], grads.at[0], local_sem.at[1]),
+        pltpu.make_async_copy(out_grads.at[0], back_ref.at[me], local_sem.at[2]),
+        pltpu.make_async_copy(out_ret.at[0], ret_ref.at[me], local_sem.at[3]),
+    ]
+    own[0].start()
+    own[1].start()
+
+    def start(step, carry):
+        send_rows(step).start()
+        send_grads(step).start()
+        return carry
+
+    lax.fori_loop(1, count, start, 0)
+    own[0].wait()
+    own[1].wait()
+    lanes = lax.broadcasted_iota(jnp.int32, (block, router_ref.shape[1]), 1)
+
+    def one_block(step, carry):
+        @pl.when(step > 0)
+        def _():
+            send_rows(step).wait_recv()
+            send_grads(step).wait_recv()
+
+        mine = rows[step]
+        cotangent = grads[step].astype(jnp.float32)
+        place = pl.ds(pl.multiple_of(step * block, 16), block)
+        logits = jnp.dot(mine, router_ref[...], preferred_element_type=jnp.float32)
+        logits = jnp.where(lanes < experts, logits, NEGATIVE)
+        weights = jnp.exp(logits - jnp.max(logits, axis=1, keepdims=True))
+        gate_all = weights / jnp.sum(weights, axis=1, keepdims=True)
+        here = (lanes == me).astype(jnp.float32)
+        gate = jnp.sum(gate_all * here, axis=1, keepdims=True)
+        pair = (gate * cotangent).astype(jnp.bfloat16)
+        gated[place, :] = pair
+        ret = jnp.zeros((block, width), jnp.float32)
+        back = jnp.zeros((block, width), jnp.float32)
+        for first in range(0, hidden, chunk):
+            span = slice(first, first + chunk)
+            pre = jnp.dot(mine, up_ref[:, span], preferred_element_type=jnp.float32)
+            cdf = 0.5 * (1.0 + lax.erf(pre * 0.7071067811865476))
+            density = jnp.exp(-0.5 * pre * pre) * 0.3989422804014327
+            low = (pre * cdf).astype(jnp.bfloat16)
+            act[place, span] = low
+            ret = ret + jnp.dot(low, down_ref[span, :], preferred_element_type=jnp.float32)
+            grad_act = times_t(pair, down_ref[span, :])
+            slope = (grad_act * (cdf + pre * density)).astype(jnp.bfloat16)
+            grad_pre[place, span] = slope
+            back = back + times_t(slope, up_ref[:, span])
+        ret = ret.astype(jnp.bfloat16).astype(jnp.float32)
+        out_ret[step] = (gate * ret).astype(jnp.bfloat16)
+        gate_grad = jnp.sum(cotangent * ret, axis=1, keepdims=True)
+        low_logits = (gate * gate_grad * (here - gate_all)).astype(jnp.bfloat16)
+        logit_grads[place, :] = low_logits
+        back = back + times_t(low_logits, router_ref[...])
+        out_grads[step] = back.astype(jnp.bfloat16)
+
+        @pl.when(step > 0)
+        def _():
+            send_back(step).start()
+
+        @pl.when(step == 0)
+        def _():
+            own[2].start()
+
+        return carry
+
+    lax.fori_loop(0, count, one_block, 0)
+    own[3].start()
+
+    def start_ret(step, carry):
+        send_ret(step).start()
+        return carry
+
+    lax.fori_loop(1, count, start_ret, 0)
+    turned[...] = jnp.transpose(rows[...].reshape(count * block, width))
+    grad_router_ref[...] = jnp.dot(
+        turned[...], logit_grads[...], preferred_element_type=jnp.float32
+    )
+
+    def up_chunk(index, carry):
+        span = pl.ds(pl.multiple_of(index * chunk, chunk), chunk)
+        grad_up_ref[:, span] = jnp.dot(
+            turned[...], grad_pre[:, span], preferred_element_type=jnp.float32
+        ).astype(jnp.bfloat16)
+        return carry
+
+    lax.fori_loop(0, hidden // chunk, up_chunk, 0)
+    turned[...] = jnp.transpose(gated[...])
+
+    def down_chunk(index, carry):
+        span = pl.ds(pl.multiple_of(index * chunk, chunk), chunk)
+        part = jnp.dot(turned[...], act[:, span], preferred_element_type=jnp.float32)
+        grad_down_ref[span, :] = jnp.transpose(part).astype(jnp.bfloat16)
+        return carry
+
+    lax.fori_loop(0, hidden // chunk, down_chunk, 0)
+
+    def finish(step, carry):
+        send_rows(step).wait_send()
+        send_grads(step).wait_send()
+        send_back(step).wait()
+        send_ret(step).wait()
+        return carry
+
+    lax.fori_loop(1, count, finish, 0)
+    own[2].wait()
+    own[3].wait()
+
+
+def experts_both_ways(sent_rows, sent_grads, up, down, router):
+    count, block, width = sent_rows.shape
+    experts = router.shape[1]
+    hidden = up.shape[1]
+    router = jnp.pad(router, ((0, 0), (0, 128 - experts)))
+    any_space = pl.BlockSpec(memory_space=pl.ANY)
+    vmem = pl.BlockSpec(memory_space=pltpu.VMEM)
+    low = jnp.bfloat16
+    slots = count * block
+    return pl.pallas_call(
+        functools.partial(expert_kernel, count, experts),
+        out_shape=(
+            jax.ShapeDtypeStruct((count, block, width), low),
+            jax.ShapeDtypeStruct((count, block, width), low),
+            jax.ShapeDtypeStruct((width, hidden), low),
+            jax.ShapeDtypeStruct((hidden, width), low),
+            jax.ShapeDtypeStruct((width, 128), jnp.float32),
+        ),
+        in_specs=[any_space, any_space, vmem, vmem, vmem],
+        out_specs=(any_space, any_space, vmem, vmem, vmem),
+        scratch_shapes=[
+            pltpu.VMEM((count, block, width), low),
+            pltpu.VMEM((count, block, width), low),
+            pltpu.VMEM((slots, width), low),
+            pltpu.VMEM((slots, hidden), low),
+            pltpu.VMEM((slots, hidden), low),
+            pltpu.VMEM((slots, 128), low),
+            pltpu.VMEM((count, block, width), low),
+            pltpu.VMEM((count, block, width), low),
+            pltpu.VMEM((width, slots), low),
+            pltpu.SemaphoreType.DMA((8, count)),
+            pltpu.SemaphoreType.DMA((4,)),
+        ],
+        compiler_params=pltpu.CompilerParams(
+            collective_id=1, has_side_effects=True, vmem_limit_bytes=58 * MIB
+        ),
+        cost_estimate=pl.CostEstimate(
+            flops=12 * slots * width * hidden, bytes_accessed=16 * MIB, transcendentals=0
+        ),
+    )(sent_rows, sent_grads, up, down, router)
 
 
 def per_device(
@@ -165,68 +388,26 @@
     state = inputs + jnp.dot(mixed, output_full, preferred_element_type=jnp.float32)
     normed_two_f, unit_two, inverse_two = normalize(state, gain_two)
     normed_two = normed_two_f.astype(jnp.bfloat16)
-    logits = jnp.dot(normed_two, router_full, preferred_element_type=jnp.float32)
-    gate = jax.nn.softmax(logits, axis=-1)
-    slot_one, slot_two, pick_one, pick_two = route(
+    slot_one, slot_two = route(
         choices, live, priority.reshape(row_count), expert_count, capacity
     )
-    gate_one = jnp.sum(gate * pick_one, axis=1)
-    gate_two = jnp.sum(gate * pick_two, axis=1)
-    empty = jnp.zeros((expert_count * capacity + 1, width), jnp.bfloat16)
-    outgoing = empty.at[slot_one].add(normed_two).at[slot_two].add(normed_two)
-    outgoing = outgoing[: expert_count * capacity].reshape(expert_count, capacity, width)
-    arrived = lax.all_to_all(outgoing, "ep", split_axis=0, concat_axis=1, tiled=True)
-    pre = jnp.einsum("erd,edf->erf", arrived, expert_up, preferred_element_type=jnp.float32)
-    act = jax.nn.gelu(pre, approximate=False).astype(jnp.bfloat16)
-    produced = jnp.einsum(
-        "erf,efd->erd", act, expert_down, preferred_element_type=jnp.float32
-    ).astype(jnp.bfloat16)
-    returned = lax.all_to_all(produced, "ep", split_axis=1, concat_axis=0, tiled=True)
-    zero_row = jnp.zeros((1, width), jnp.bfloat16)
-    flat = jnp.concatenate([returned.reshape(expert_count * capacity, width), zero_row], axis=0)
-    got_one = flat[slot_one].astype(jnp.float32)
-    got_two = flat[slot_two].astype(jnp.float32)
-    output = (state + gate_one[:, None] * got_one + gate_two[:, None] * got_two).astype(
-        jnp.bfloat16
-    )
+    block = -(-capacity // 16) * 16
+    slots = expert_count * block
+    index = lax.broadcasted_iota(jnp.int32, (slots, row_count), 0)
+    chosen = ((index == slot_one[None, :]) | (index == slot_two[None, :])).astype(jnp.bfloat16)
+    spread = lambda values: (
+        jnp.dot(chosen, values, preferred_element_type=jnp.float32)
+        .astype(jnp.bfloat16)
+        .reshape(expert_count, block, width)
+    )
+    collect = lambda values: outer(chosen, values.reshape(slots, width))
     grad = out_grad.astype(jnp.float32)
-    grad_gate = (
-        pick_one * jnp.sum(grad * got_one, axis=1)[:, None]
-        + pick_two * jnp.sum(grad * got_two, axis=1)[:, None]
-    )
-    grad_logits = (gate * (grad_gate - jnp.sum(gate * grad_gate, axis=1, keepdims=True))).astype(
-        jnp.bfloat16
-    )
-    grad_router = outer(normed_two, grad_logits)
-    grad_normed_two = times_t(grad_logits, router_full)
-    weighted_one = (gate_one[:, None] * grad).astype(jnp.bfloat16)
-    weighted_two = (gate_two[:, None] * grad).astype(jnp.bfloat16)
-    grad_out_rows = empty.at[slot_one].add(weighted_one).at[slot_two].add(weighted_two)
-    grad_out_rows = grad_out_rows[: expert_count * capacity].reshape(expert_count, capacity, width)
-    grad_arrived = lax.all_to_all(grad_out_rows, "ep", split_axis=0, concat_axis=1, tiled=True)
-    rows_now = lax.all_to_all(outgoing, "ep", split_axis=0, concat_axis=1, tiled=True)
-    pre_now = jnp.einsum("erd,edf->erf", rows_now, expert_up, preferred_element_type=jnp.float32)
-    act_now = jax.nn.gelu(pre_now, approximate=False).astype(jnp.bfloat16)
-    grad_down = jnp.einsum(
-        "erf,erd->efd", act_now, grad_arrived, preferred_element_type=jnp.float32
-    )
-    grad_act = jnp.einsum(
-        "erd,efd->erf", grad_arrived, expert_down, preferred_element_type=jnp.float32
-    )
-    grad_pre = (grad_act * gelu_slope(pre_now)).astype(jnp.bfloat16)
-    grad_up = jnp.einsum("erd,erf->edf", rows_now, grad_pre, preferred_element_type=jnp.float32)
-    grad_rows = jnp.einsum(
-        "erf,edf->erd", grad_pre, expert_up, preferred_element_type=jnp.float32
-    ).astype(jnp.bfloat16)
-    grad_back = lax.all_to_all(grad_rows, "ep", split_axis=1, concat_axis=0, tiled=True)
-    flat_grad = jnp.concatenate(
-        [grad_back.reshape(expert_count * capacity, width), zero_row], axis=0
-    )
-    grad_normed_two = (
-        grad_normed_two
-        + flat_grad[slot_one].astype(jnp.float32)
-        + flat_grad[slot_two].astype(jnp.float32)
-    )
+    back, returned, grad_up, grad_down, grad_router = experts_both_ways(
+        spread(normed_two), spread(out_grad), expert_up[0], expert_down[0], router_full
+    )
+    output = (state + collect(returned)).astype(jnp.bfloat16)
+    grad_router = grad_router[:, :expert_count]
+    grad_normed_two = collect(back)
     grad_state_in, grad_gain_two = normalize_back(grad_normed_two, gain_two, unit_two, inverse_two)
     grad_state = grad + grad_state_in
     grad_branch = grad_state.astype(jnp.bfloat16)
@@ -263,8 +444,8 @@
         lax.psum_scatter(grad_router, ("grp", "ep"), scatter_dimension=0, tiled=True),
     )
     grad_up, grad_down = (
-        lax.psum(grad_up.astype(jnp.bfloat16), "grp").astype(jnp.float32),
-        lax.psum(grad_down.astype(jnp.bfloat16), "grp").astype(jnp.float32),
+        lax.psum(grad_up, "grp").astype(jnp.float32)[None],
+        lax.psum(grad_down, "grp").astype(jnp.float32)[None],
     )
     return (
         output,

time: 1120 us -> 923 us (0.82)
  Pallas kernels: 0 us -> 193 us
  blocking collectives: 363 us -> 221 us
  local copies, waits for them, and re-layouts: 164 us -> 31.3 us
  other arithmetic: 102 us -> 20.7 us
  matrix products: 154 us -> 79 us
  waiting for transfers between devices: 307 us -> 358 us
    pallas_call x0 -> x1, Pallas kernels: none -> 193 us  [experts_both_ways(): pl.pallas_call(functools.partial(expert_kernel, count, experts), out_shap...]
    all_to_all x2 -> x0, blocking collectives: 105 us -> none  [the longest x1 53 us: per_device(): lax.all_to_all(outgoing, 'ep', split_axis=0, concat_axis=1, tiled=True)]
    dot_general x7 -> x2, matrix products: 89.1 us -> 8.3 us  [per_device(): jnp.dot(chosen, values, preferred_element_type=jnp.float32)]
    reduce_scatter x1, waiting for transfers between devices: 77 us -> 131 us  [per_device(): lax.psum_scatter(grad_output_w, ('grp', 'ep'), scatter_dimension=0, tiled...]
    scatter-add x4 -> x0, other arithmetic: 39.4 us -> none  [the longest x2 19.8 us: per_device(): outgoing = empty.at[slot_one].add(normed_two).at[slot_two].add(normed_two)]
    convert_element_type x5 -> x0, local copies, waits for them, and re-layouts: 38.8 us -> none  [the longest x1 16.4 us: per_device(): grad_rows = jnp.einsum('erf,edf->erd', grad_pre, expert_up, preferred_ele...]
    reduce_scatter x0 -> x1, waiting for transfers between devices: none -> 37.3 us  [per_device(): lax.psum_scatter(grad_router, ('grp', 'ep'), scatter_dimension=0, tiled=T...]
    gather x8 -> x0, local copies, waits for them, and re-layouts: 37.2 us -> none  [the longest x2 9.35 us: per_device(): flat_grad[slot_one].astype(jnp.float32)]
  transfers between devices with their start and end apart: 7 -> 5, of which waited for: 5 -> 4; matrix products, arithmetic and copies ran while one was open for 12% -> 8% of each run, Pallas kernels for 0% -> 0%
where the time goes in v1:
time: 923 us; the launch traced here: 918 us
  waiting for transfers between devices  358 us (39%)
  blocking collectives  221 us (24%)
  Pallas kernels  193 us (21%)
  matrix products  79 us (9%)
  local copies, waits for them, and re-layouts  31.3 us (3%)
  other arithmetic  20.7 us (2%)
  between operations  14.6 us (2%)
    pallas_call x1, Pallas kernels, experts_both_ways(): pl.pallas_call(functools.partial(expert_kernel, count, experts), out_shap...  193 us
    reduce_scatter x1, waiting for transfers between devices, per_device(): lax.psum_scatter(grad_output_w, ('grp', 'ep'), scatter_dimension=0, tiled...  131 us
    reduce_scatter x1, waiting for transfers between devices, per_device(): lax.psum_scatter(grad_joint_w, ('grp', 'ep'), scatter_dimension=0, tiled=...  104 us
    unnamed x2, blocking collectives  87.8 us
    psum x1, waiting for transfers between devices, per_device(): lax.psum(grad_up, 'grp').astype(jnp.float32)[None]  83.4 us
    all_gather x1, blocking collectives, per_device(): lax.all_gather(output_weight, ('grp', 'ep'), axis=0, tiled=True)  67.1 us
    all_gather x1, blocking collectives, per_device(): lax.all_gather(router_weight, ('grp', 'ep'), axis=0, tiled=True)  66.3 us
    reduce_scatter x1, waiting for transfers between devices, per_device(): lax.psum_scatter(grad_router, ('grp', 'ep'), scatter_dimension=0, tiled=T...  37.3 us
  transfers between devices with their start and end apart: 5, of which 4 were waited for; matrix products, arithmetic and copies ran while one was open for 8% of the time, Pallas kernels for 0%

profile of v1, /device:TPU:0, one launch (start us, length us, event | category | flops | bytes accessed | tf_op | source)
XLA Modules:
  0.0 917.9 jit_solution(14824715793012241623)
XLA Ops:
  8.0 1.5 copy.60
  11.2 42.1 %all-reduce.6 = (bf16[512]{0:T(512)(128)(2,1)S(1)}, bf16[512]{0:T(512)(128)(2,1)S(1)}) all-reduce(bf16[512]{0:T(512)(128)(2,1)S(1)} %dynamic-update-slice, bf16[512]{0:T(512)(128)(2,1)S(1)} %dynamic-update-slice.1), channel_id=1, replica_groups=mesh['grp'=4,'ep'=8] {'grp','ep'}, use_global_device_ids=true, to_apply=%add.1 | all-reduce | flops 1024 | bytes 4096
  56.3 66.3 %all-gather = bf16[32,16,8]{1,2,0:T(8,128)(2,1)S(1)} all-gather(bf16[1,16,8]{1,2,0:T(8,128)(2,1)S(1)} %bitcast.145), channel_id=1, replica_groups=mesh['grp'=4,'ep'=8] {'grp','ep'}, dimensions={0}, use_global_device_ids=true | all-gather | bytes 8448 | tf_op jit(solution)/shard_map/all_gather | solution.py:363
  124.8 2.4 fusion.78
  127.2 2.4 fusion.75
  130.3 1.4 fusion.86
  131.6 67.1 %all_gather.17 = bf16[512,512]{1,0:T(8,128)(2,1)S(1)} all-gather(bf16[16,512]{1,0:T(8,128)(2,1)S(1)} %copy-done.21), channel_id=1, replica_groups=mesh['grp'=4,'ep'=8] {'grp','ep'}, dimensions={0}, use_global_device_ids=true | all-gather | bytes 540672 | tf_op jit(solution)/shard_map/all_gather | solution.py:361
  198.7 4.0 convolution_convert_fusion
  202.7 3.3 convolution_convert_fusion.2
  206.1 1.9 fusion.111
  207.9 1.7 copy.63
  209.7 2.7 fusion.115
  213.6 2.0 copy-done
  215.6 2.4 fusion.65
  217.9 1.9 copy.61
  219.9 1.5 fusion.116
  222.6 2.1 copy-done.1
  224.7 1.6 fusion.64
  227.7 4.3 convolution_convert_fusion.1
  232.0 193.1 %shard_map.196 = (bf16[8,272,512]{2,1,0:T(8,128)(2,1)}, bf16[8,272,512]{2,1,0:T(8,128)(2,1)}, bf16[512,2048]{1,0:T(8,128)(2,1)}, bf16[2048,512]{1,0:T(8,128)(2,1)}, f32[512,128]{1,0:T(8,128)}) custom-call(bf16[8,272,512]{2,1,0:T(8,128)(2,1)} %bitcast.153, bf16[8,272,512]{2,1,0:T(8,128)(2,1)} %bitcast.151, bf16[512,2048]{1,0:T(8,128)(2,1)} %bitcast.146, ...), custom_call_target="tpu_custom_call" | custom-call | flops 27380416512 | bytes 16777216 | tf_op jit(solution)/shard_map/pallas_call | solution.py:303
  425.1 5.0 multiply_reduce_fusion.2
  432.8 5.1 multiply_reduce_fusion
  438.8 2.5 multiply_convert_fusion
  441.4 2.2 fusion.54
  443.6 1.6 fusion.55
  446.0 3.0 fusion.88
  449.0 5.7 multiply_reduce_fusion.1
  455.1 2.5 multiply_convert_fusion.1
  457.7 2.0 copy-done.2
  459.7 3.2 fusion.56
  463.2 3.2 fusion.57
  466.4 4.9 fusion.58
  471.3 5.0 fusion.61
  476.8 1.7 copy-done.14
  478.5 3.6 fusion.93
  482.1 5.8 add_convert_fusion
  487.9 2.3 copy.74
  490.2 4.6 fusion.34
  494.8 2.0 fusion.33
  496.7 2.9 copy.75
  499.6 45.7 %all-reduce.5 = (f32[512]{0:T(512)S(1)}, f32[512]{0:T(512)S(1)}) all-reduce(f32[512]{0:T(512)S(1)} %get-tuple-element.48, f32[512]{0:T(512)S(1)} %get-tuple-element.46), channel_id=2, replica_groups=mesh['grp'=4,'ep'=8] {'grp','ep'}, use_global_device_ids=true, to_apply=%region_18.19.clone | all-reduce | flops 1024 | bytes 8192
  546.5 37.3 %reduce-scatter.8.cloned.1.call-done = f32[16,8]{1,0:T(8,128)} async-done(((f32[512,8]{1,0:T(8,128)}), f32[16,8]{1,0:T(8,128)}) %reduce-scatter.8.cloned.1.call-update) | async-done | bytes 528 | tf_op jit(solution)/shard_map/reduce_scatter | solution.py:444
  583.8 1.4 copy.76
  585.2 83.4 %all-reduce.10.cloned.1.call-done = (bf16[1,512,2048]{2,1,0:T(8,128)(2,1)}, bf16[1,2048,512]{2,1,0:T(8,128)(2,1)}) async-done(((bf16[1,512,2048]{2,1,0:T(8,128)(2,1)}, bf16[1,2048,512]{2,1,0:T(8,128)(2,1)}), (bf16[1,512,2048]{2,1,0:T(8,128)(2,1)}, bf16[1,2048,512]{2,1,0:T(8,128)(2,1)})) %all-reduce.10.cloned.1.call-update) | async-done | bytes 4194320 | tf_op jit(solution)/shard_map/psum | solution.py:447
  668.6 4.3 broadcast_in_dim.79
  672.9 2.6 broadcast_in_dim.81
  675.5 131.2 %reduce-scatter.6.cloned.1.call-done = f32[16,512]{1,0:T(8,128)} async-done(((f32[512,512]{1,0:T(8,128)}), f32[16,512]{1,0:T(8,128)}) %reduce-scatter.6.cloned.1.call-update) | async-done | bytes 32784 | tf_op jit(solution)/shard_map/reduce_scatter | solution.py:442
  806.7 104.5 %reduce-scatter.4.cloned.1.call-done = f32[16,1536]{1,0:T(8,128)} async-done(((f32[512,1536]{1,0:T(8,128)}), f32[16,1536]{1,0:T(8,128)}) %reduce-scatter.4.cloned.1.call-update) | async-done | bytes 98320 | tf_op jit(solution)/shard_map/reduce_scatter | solution.py:441
  (108 shorter events, 18.7 us)
Async XLA Ops:
  7.2 49.1 %copy-start.22 = (bf16[16,8]{0,1:T(8,128)(2,1)S(1)}, bf16[16,8]{0,1:T(8,128)(2,1)}, u32[]{:S(2)}) copy-start(bf16[16,8]{0,1:T(8,128)(2,1)} %param.22) | copy-start | bytes 772
  7.2 115.5 %copy-start.19 = (bf16[1024,512]{1,0:T(8,128)(2,1)S(1)}, bf16[1024,512]{1,0:T(8,128)(2,1)}, u32[]{:S(2)}) copy-start(bf16[1024,512]{1,0:T(8,128)(2,1)} %param.25) | copy-start | bytes 3145732
  7.2 195.5 %all-gather.3.cloned.1.call-start = ((), (), s32[]{:S(2)}) async-start(), calls=%async_computation.3 | async-start | bytes 1622016 | tf_op jit(solution)/shard_map/all_gather | solution.py:360
  7.9 575.9 %reduce-scatter.8.cloned.1.call-start = ((), (), s32[]{:S(2)}) async-start(), calls=%async_computation.6 | async-start | bytes 270336 | tf_op jit(solution)/shard_map/reduce_scatter | solution.py:444
  8.0 116.8 %copy-start.23 = (s32[1,1024]{1,0:T(1,128)S(1)}, s32[1,1024]{1,0:T(1,128)}, u32[]{:S(2)}) copy-start(s32[1,1024]{1,0:T(1,128)} %param.17) | copy-start | bytes 12292
  124.8 6.8 copy-start.21
  198.7 27.7 %copy-start.11 = (bf16[512,512]{1,0:T(8,128)(2,1)}, bf16[512,512]{1,0:T(8,128)(2,1)S(1)}, u32[]{:S(2)}) copy-start(bf16[512,512]{1,0:T(8,128)(2,1)S(1)} %all_gather.17) | copy-start | bytes 1572868
  209.6 3.9 copy-start.5
  212.3 3.2 copy-start
  219.8 2.7 copy-start.4
  221.4 3.3 copy-start.1
  224.7 1.6 copy-start.20
  226.4 1.0 copy-start.7
  227.4 202.7 %copy-start.3 = (f32[1024,512]{0,1:T(8,128)}, f32[1024,512]{0,1:T(8,128)S(1)}, u32[]{:S(2)}) copy-start(f32[1024,512]{0,1:T(8,128)S(1)} %get-tuple-element.75) | copy-start | bytes 6291460
  425.0 5.1 copy-start.13
  430.1 1.0 copy-start.12
  431.2 1.6 copy-start.6
  432.7 5.1 copy-start.9
  432.7 5.1 slice-start
  432.7 6.1 slice-start.1
  445.2 223.4 %all-reduce.10.cloned.1.call-start = ((), (), s32[]{:S(2)}) async-start(), calls=%async_computation.7 | async-start | bytes 8388608 | tf_op jit(solution)/shard_map/psum | solution.py:447
  445.9 360.7 %reduce-scatter.6.cloned.1.call-start = ((), (), s32[]{:S(2)}) async-start(), calls=%async_computation.5 | async-start | bytes 1081344 | tf_op jit(solution)/shard_map/reduce_scatter | solution.py:442
  449.0 5.8 slice-start.2
  449.0 6.2 slice-start.3
  457.7 2.0 copy-start.2
  462.9 448.2 %reduce-scatter.4.cloned.1.call-start = ((), (), s32[]{:S(2)}) async-start(), calls=%async_computation.4 | async-start | bytes 3244032 | tf_op jit(solution)/shard_map/reduce_scatter | solution.py:441
  463.2 3.2 copy-start.10
  466.4 4.9 copy-start.8
  471.3 5.0 copy-start.16
  471.3 5.0 copy-start.17
  471.3 5.0 copy-start.18
  476.8 1.7 copy-start.14
  668.6 4.3 copy-start.15
Sparse Core Ops, SparseCore 0:
  10.9 57.8 all-gather.2
  445.3 138.4 reduce-scatter.7
  586.4 82.1 all-reduce.9
  671.3 135.3 reduce-scatter.5
  813.4 97.6 reduce-scatter.3

commit v2 on v1

--- a/solution.py
+++ b/solution.py
@@ -289,6 +289,925 @@
     lax.fori_loop(1, count, finish, 0)
     own[2].wait()
     own[3].wait()
+
+
+def column(values, lane):
+    lanes = lax.broadcasted_iota(jnp.int32, values.shape, 1)
+    return jnp.sum(jnp.where(lanes == lane, values, 0), axis=1, keepdims=True)
+
+
+def core_peer(grp):
+    return grp + 1 - 2 * lax.rem(grp, 2)
+
+
+def x_peer(grp):
+    return lax.rem(grp + 2, 4)
+
+
+def flags(condition):
+    return jnp.where(condition, 1.0, 0.0).astype(jnp.bfloat16)
+
+
+def remote_copy(source, target, send_sem, recv_sem, device):
+    return pltpu.make_async_remote_copy(
+        src_ref=source,
+        dst_ref=target,
+        send_sem=send_sem,
+        recv_sem=recv_sem,
+        device_id=device,
+        device_id_type=MESH,
+    )
+
+
+def greet_all(count, me, grp):
+    barrier = pltpu.get_barrier_semaphore()
+
+    def greet(step, carry):
+        pl.semaphore_signal(
+            barrier, inc=1, device_id={"ep": partner(me, step, count)}, device_id_type=MESH
+        )
+        return carry
+
+    lax.fori_loop(1, count, greet, 0)
+    for peer in (core_peer(grp), x_peer(grp)):
+        pl.semaphore_signal(barrier, inc=1, device_id={"grp": peer}, device_id_type=MESH)
+    pl.semaphore_wait(barrier, count + 1)
+
+
+def seen(segment_row, live_row, segment_col):
+    length = segment_row.shape[1]
+    index = lax.broadcasted_iota(jnp.int32, (length, length), 0)
+    other = lax.broadcasted_iota(jnp.int32, (length, length), 1)
+    return (segment_col == segment_row) & ((live_row > 0) | (index == other))
+
+
+def forward_kernel(
+    count,
+    capacity,
+    tokens,
+    segments,
+    live,
+    picks,
+    ranks,
+    out_grad,
+    joint_shard,
+    output_shard,
+    pack_shard,
+    weights,
+    joint,
+    mixed,
+    state,
+    sent_rows,
+    logs,
+    slots,
+    grads,
+    own_grads,
+    normed_two,
+    int_columns,
+    ep_sems,
+    x_sems,
+    core_sems,
+    grad_sems,
+    local_sems,
+):
+    me, grp = lax.axis_index("ep"), lax.axis_index("grp")
+    row_count, width = tokens.shape
+    sequences, length = segments.shape
+    block = sent_rows.shape[1]
+    joint_width = joint.shape[1]
+    head_size = width // HEADS
+    factor = head_size ** (-0.5)
+    mate, across = core_peer(grp), x_peer(grp)
+    greet_all(count, me, grp)
+
+    def shard(owner_grp, owner):
+        return weights.at[owner_grp * count + owner]
+
+    def to_ep(step):
+        place = shard(grp, me)
+        other = partner(me, step, count)
+        return remote_copy(place, place, ep_sems.at[0, step], ep_sems.at[1, step], {"ep": other})
+
+    def to_x(step):
+        place = shard(grp, partner(me, step, count))
+        return remote_copy(place, place, x_sems.at[0, step], x_sems.at[1, step], {"grp": across})
+
+    def to_core(owner_grp, part, step):
+        place = shard(owner_grp, partner(me, step, count))
+        sems = core_sems.at[0, part, step], core_sems.at[1, part, step]
+        return remote_copy(place, place, *sems, {"grp": mate})
+
+    def send_grads(step):
+        return remote_copy(
+            own_grads.at[step],
+            grads.at[step],
+            grad_sems.at[0, step],
+            grad_sems.at[1, step],
+            {"ep": partner(me, step, count)},
+        )
+
+    mine = grp * count + me
+    fill = [
+        pltpu.make_async_copy(
+            joint_shard, weights.at[mine, :, pl.ds(0, joint_width)], local_sems.at[0]
+        ),
+        pltpu.make_async_copy(
+            output_shard, weights.at[mine, :, pl.ds(joint_width, width)], local_sems.at[1]
+        ),
+        pltpu.make_async_copy(
+            pack_shard, weights.at[mine, :, pl.ds(joint_width + width, 128)], local_sems.at[2]
+        ),
+    ]
+    for copy in fill:
+        copy.start()
+    for copy in fill:
+        copy.wait()
+
+    def first_hop(step, carry):
+        to_ep(step).start()
+        return carry
+
+    lax.fori_loop(1, count, first_hop, 0)
+    to_x(0).start()
+    to_core(grp, 0, 0).start()
+
+    ints = jnp.concatenate([segments[...], live[...]], axis=0).astype(jnp.float32)
+    turned = jnp.transpose(ints)
+    int_columns[...] = turned.astype(jnp.int32)
+    live_col = jnp.concatenate(
+        [turned[:, sequences + i : sequences + i + 1] for i in range(sequences)], axis=0
+    )
+    rank_row = ranks[...].astype(jnp.float32)
+    rank_col = jnp.transpose(jnp.broadcast_to(rank_row, (8, row_count)))[:, 0:1]
+    earlier = flags(rank_row < rank_col)
+    first, second = picks[:, 0:1], picks[:, 1:2]
+    lanes = lax.broadcasted_iota(jnp.int32, (row_count, 128), 1)
+    one = jnp.where(lanes == first, 1.0, 0.0)
+    two = jnp.where(lanes == second + count, 1.0, 0.0)
+    counts = jnp.dot(
+        earlier, ((one + two) * live_col).astype(jnp.bfloat16), preferred_element_type=jnp.float32
+    )
+    ahead = jnp.sum(jnp.where(lanes == first + count, live_col, 0.0), axis=0, keepdims=True)
+    place_one = jnp.sum(counts * one, axis=1, keepdims=True)
+    place_two = jnp.sum((counts + ahead) * two, axis=1, keepdims=True)
+    nowhere = 1.0 * count * block
+    slot_one = jnp.where(
+        (live_col > 0) & (place_one < capacity),
+        first.astype(jnp.float32) * block + place_one,
+        nowhere,
+    )
+    slot_two = jnp.where(
+        (live_col > 0) & (place_two < capacity),
+        second.astype(jnp.float32) * block + place_two,
+        nowhere,
+    )
+    both = jnp.where(lanes == 0, slot_one, jnp.where(lanes == 1, slot_two, nowhere))
+    slots[...] = both.astype(jnp.int32)
+    slot_rows = jnp.transpose(both)[0:8].astype(jnp.int32)
+    row_one, row_two = slot_rows[0:1], slot_rows[1:2]
+
+    def rows_of(expert, values):
+        index = lax.broadcasted_iota(jnp.int32, (block, row_count), 0) + expert * block
+        chosen = flags((index == row_one) | (index == row_two))
+        return jnp.dot(chosen, values[...], preferred_element_type=jnp.float32).astype(jnp.bfloat16)
+
+    def spread_grads(step, carry):
+        own_grads[step] = rows_of(partner(me, step, count), out_grad)
+
+        @pl.when(step > 0)
+        def _():
+            send_grads(step).start()
+
+        return carry
+
+    lax.fori_loop(0, count, spread_grads, 0)
+    keep = pltpu.make_async_copy(own_grads.at[0], grads.at[0], local_sems.at[3])
+    keep.start()
+
+    def pass_on(step, carry):
+        to_ep(step).wait_recv()
+        to_x(step).start()
+        to_core(grp, 0, step).start()
+        return carry
+
+    lax.fori_loop(1, count, pass_on, 0)
+
+    def pass_further(step, carry):
+        to_x(step).wait_recv()
+        to_core(across, 1, step).start()
+        return carry
+
+    lax.fori_loop(0, count, pass_further, 0)
+
+    def arrive(step, carry):
+        to_core(mate, 0, step).wait_recv()
+        to_core(x_peer(mate), 1, step).wait_recv()
+        return carry
+
+    lax.fori_loop(0, count, arrive, 0)
+
+    devices = weights.shape[0]
+    total = devices * weights.shape[1]
+    pack = weights[:, :, joint_width + width :].reshape(total, 128)
+    gains = jnp.transpose(pack.astype(jnp.float32))
+    gain_one = gains[count : count + 1]
+    gain_two = gains[count + 1 : count + 2]
+    half = lax.broadcasted_iota(jnp.int32, (length, 128), 1) < head_size
+    halves = (flags(half), flags(jnp.logical_not(half)))
+
+    def attend(number, carry):
+        rows = pl.ds(pl.multiple_of(number * length, length), length)
+        values = tokens[rows, :].astype(jnp.float32)
+        normed = normalize(values, gain_one)[0].astype(jnp.bfloat16)
+        joint[rows, :] = jnp.dot(
+            normed,
+            weights[:, :, :joint_width].reshape(total, joint_width),
+            preferred_element_type=jnp.float32,
+        ).astype(jnp.bfloat16)
+        allowed = seen(
+            segments[pl.ds(number, 1), :], live[pl.ds(number, 1), :], column(int_columns[...], number)
+        )
+        log_all = jnp.zeros((length, 128), jnp.float32)
+        log_lanes = lax.broadcasted_iota(jnp.int32, (length, 128), 1)
+        for pair in range(HEADS // 2):
+            at = pair * 128
+            query = joint[rows, at : at + 128]
+            key = joint[rows, width + at : width + at + 128]
+            value = joint[rows, 2 * width + at : 2 * width + at + 128]
+            results = []
+            for side in range(2):
+                scores = times_t(query * halves[side], key) * factor
+                masked = jnp.where(allowed, scores, NEGATIVE)
+                top = jnp.max(masked, axis=-1, keepdims=True)
+                powers = jnp.exp(masked - top)
+                added = jnp.sum(powers, axis=-1, keepdims=True)
+                probs = (powers * (1.0 / added)).astype(jnp.bfloat16)
+                results.append(jnp.dot(probs, value, preferred_element_type=jnp.float32))
+                log_all = jnp.where(log_lanes == 2 * pair + side, top + jnp.log(added), log_all)
+            mixed[rows, at : at + 128] = jnp.where(half, results[0], results[1]).astype(jnp.bfloat16)
+        logs[rows, :] = log_all
+        after = values + jnp.dot(
+            mixed[rows, :],
+            weights[:, :, joint_width : joint_width + width].reshape(total, width),
+            preferred_element_type=jnp.float32,
+        )
+        state[rows, :] = after
+        normed_two[rows, :] = normalize(after, gain_two)[0].astype(jnp.bfloat16)
+        return carry
+
+    lax.fori_loop(0, sequences, attend, 0)
+
+    def spread_rows(expert, carry):
+        sent_rows[expert] = rows_of(expert, normed_two)
+        return carry
+
+    lax.fori_loop(0, count, spread_rows, 0)
+    keep.wait()
+    to_x(0).wait_send()
+    to_core(grp, 0, 0).wait_send()
+    to_core(across, 1, 0).wait_send()
+
+    def finish(step, carry):
+        to_ep(step).wait_send()
+        to_x(step).wait_send()
+        to_core(grp, 0, step).wait_send()
+        to_core(across, 1, step).wait_send()
+        send_grads(step).wait()
+        return carry
+
+    lax.fori_loop(1, count, finish, 0)
+
+
+def forward(
+    count, capacity, block, tokens, segments, live, picks, ranks, out_grad, joint, output, pack
+):
+    row_count, width = tokens.shape
+    devices = width // joint.shape[0]
+    all_width = joint.shape[1] + width + 128
+    any_space = pl.BlockSpec(memory_space=pl.ANY)
+    vmem = pl.BlockSpec(memory_space=pltpu.VMEM)
+    low = jnp.bfloat16
+    return pl.pallas_call(
+        functools.partial(forward_kernel, count, capacity),
+        out_shape=(
+            jax.ShapeDtypeStruct((devices, joint.shape[0], all_width), low),
+            jax.ShapeDtypeStruct((row_count, joint.shape[1]), low),
+            jax.ShapeDtypeStruct((row_count, width), low),
+            jax.ShapeDtypeStruct((row_count, width), jnp.float32),
+            jax.ShapeDtypeStruct((count, block, width), low),
+            jax.ShapeDtypeStruct((row_count, 128), jnp.float32),
+            jax.ShapeDtypeStruct((row_count, 128), jnp.int32),
+            jax.ShapeDtypeStruct((count, block, width), low),
+        ),
+        in_specs=[vmem] * 6 + [any_space] * 3,
+        out_specs=(vmem,) * 7 + (any_space,),
+        scratch_shapes=[
+            pltpu.VMEM((count, block, width), low),
+            pltpu.VMEM((row_count, width), low),
+            pltpu.VMEM((segments.shape[1], 2 * segments.shape[0]), jnp.int32),
+            pltpu.SemaphoreType.DMA((2, count)),
+            pltpu.SemaphoreType.DMA((2, count)),
+            pltpu.SemaphoreType.DMA((2, 2, count)),
+            pltpu.SemaphoreType.DMA((2, count)),
+            pltpu.SemaphoreType.DMA((4,)),
+        ],
+        compiler_params=pltpu.CompilerParams(
+            collective_id=2, has_side_effects=True, vmem_limit_bytes=48 * MIB
+        ),
+    )(tokens, segments, live, picks, ranks, out_grad, joint, output, pack)
+
+
+def middle_kernel(
+    count,
+    sent_rows,
+    grads,
+    up_ref,
+    down_ref,
+    router_ref,
+    back_ref,
+    out_ret,
+    grad_up_ref,
+    grad_down_ref,
+    grad_router_ref,
+    rows,
+    gated,
+    act,
+    grad_pre,
+    logit_grads,
+    out_grads,
+    turned,
+    part_up,
+    part_down,
+    mate_up,
+    mate_down,
+    half_up,
+    half_down,
+    far_up,
+    far_down,
+    sems,
+    sum_sems,
+    local_sem,
+):
+    me, grp = lax.axis_index("ep"), lax.axis_index("grp")
+    mate, across = core_peer(grp), x_peer(grp)
+    core = lax.rem(grp, 2)
+    block, width = rows.shape[1:]
+    hidden = up_ref.shape[1]
+    chunk = 512
+    greet_all(count, me, grp)
+
+    def send_rows(step):
+        other = partner(me, step, count)
+        return remote_copy(
+            sent_rows.at[other], rows.at[step], sems.at[0, step], sems.at[1, step], {"ep": other}
+        )
+
+    def send_back(step):
+        other = partner(me, step, count)
+        return remote_copy(
+            out_grads.at[step], back_ref.at[me], sems.at[2, step], sems.at[3, step], {"ep": other}
+        )
+
+    own = [
+        pltpu.make_async_copy(sent_rows.at[me], rows.at[0], local_sem.at[0]),
+        pltpu.make_async_copy(out_grads.at[0], back_ref.at[me], local_sem.at[1]),
+    ]
+    own[0].start()
+
+    def start(step, carry):
+        send_rows(step).start()
+        return carry
+
+    lax.fori_loop(1, count, start, 0)
+    own[0].wait()
+    lanes = lax.broadcasted_iota(jnp.int32, (block, router_ref.shape[1]), 1)
+
+    def one_block(step, carry):
+        @pl.when(step > 0)
+        def _():
+            send_rows(step).wait_recv()
+
+        mine = rows[step]
+        cotangent = grads[step].astype(jnp.float32)
+        place = pl.ds(pl.multiple_of(step * block, 16), block)
+        logits = jnp.dot(mine, router_ref[...], preferred_element_type=jnp.float32)
+        logits = jnp.where(lanes < count, logits, NEGATIVE)
+        weights = jnp.exp(logits - jnp.max(logits, axis=1, keepdims=True))
+        gate_all = weights / jnp.sum(weights, axis=1, keepdims=True)
+        here = (lanes == me).astype(jnp.float32)
+        gate = jnp.sum(gate_all * here, axis=1, keepdims=True)
+        pair = (gate * cotangent).astype(jnp.bfloat16)
+        gated[place, :] = pair
+        ret = jnp.zeros((block, width), jnp.float32)
+        back = jnp.zeros((block, width), jnp.float32)
+        for first in range(0, hidden, chunk):
+            span = slice(first, first + chunk)
+            pre = jnp.dot(mine, up_ref[:, span], preferred_element_type=jnp.float32)
+            cdf = 0.5 * (1.0 + lax.erf(pre * 0.7071067811865476))
+            density = jnp.exp(-0.5 * pre * pre) * 0.3989422804014327
+            low = (pre * cdf).astype(jnp.bfloat16)
+            act[place, span] = low
+            ret = ret + jnp.dot(low, down_ref[span, :], preferred_element_type=jnp.float32)
+            grad_act = times_t(pair, down_ref[span, :])
+            slope = (grad_act * (cdf + pre * density)).astype(jnp.bfloat16)
+            grad_pre[place, span] = slope
+            back = back + times_t(slope, up_ref[:, span])
+        ret = ret.astype(jnp.bfloat16).astype(jnp.float32)
+        out_ret[step] = (gate * ret).astype(jnp.bfloat16)
+        gate_grad = jnp.sum(cotangent * ret, axis=1, keepdims=True)
+        low_logits = (gate * gate_grad * (here - gate_all)).astype(jnp.bfloat16)
+        logit_grads[place, :] = low_logits
+        back = back + times_t(low_logits, router_ref[...])
+        out_grads[step] = back.astype(jnp.bfloat16)
+
+        @pl.when(step > 0)
+        def _():
+            send_back(step).start()
+
+        @pl.when(step == 0)
+        def _():
+            own[1].start()
+
+        return carry
+
+    lax.fori_loop(0, count, one_block, 0)
+    turned[...] = jnp.transpose(rows[...].reshape(count * block, width))
+    grad_router_ref[...] = jnp.dot(
+        turned[...], logit_grads[...], preferred_element_type=jnp.float32
+    )
+
+    up_rows, down_rows = half_up.shape[0], half_down.shape[0]
+    groups = (
+        (part_up, mate_up, half_up, far_up, grad_up_ref, up_rows),
+        (part_down, mate_down, half_down, far_down, grad_down_ref, down_rows),
+    )
+
+    def half_of(which, size):
+        return pl.ds(pl.multiple_of(which * size, size), size)
+
+    def to_mate(layer):
+        part, landing, _, _, _, size = groups[layer]
+        sem = sum_sems.at[0, layer], sum_sems.at[1, layer]
+        return remote_copy(part.at[half_of(1 - core, size)], landing, *sem, {"grp": mate})
+
+    def to_across(layer):
+        _, _, half, far, _, _ = groups[layer]
+        sem = sum_sems.at[2, layer], sum_sems.at[3, layer]
+        return remote_copy(half, far, *sem, {"grp": across})
+
+    def to_mate_again(layer):
+        result, size = groups[layer][4:]
+        sem = sum_sems.at[4, layer], sum_sems.at[5, layer]
+        place = result.at[half_of(core, size)]
+        return remote_copy(place, place, *sem, {"grp": mate})
+
+    def add_mate(layer):
+        part, landing, half, _, _, size = groups[layer]
+        to_mate(layer).wait_recv()
+        kept = part[half_of(core, size), :].astype(jnp.float32)
+        half[...] = (kept + landing[...].astype(jnp.float32)).astype(jnp.bfloat16)
+        to_across(layer).start()
+
+    def add_across(layer):
+        _, _, half, far, result, size = groups[layer]
+        to_across(layer).wait_recv()
+        result[half_of(core, size), :] = (
+            half[...].astype(jnp.float32) + far[...].astype(jnp.float32)
+        ).astype(jnp.bfloat16)
+        to_mate_again(layer).start()
+
+    def up_chunk(index, carry):
+        span = pl.ds(pl.multiple_of(index * chunk, chunk), chunk)
+        part_up[:, span] = jnp.dot(
+            turned[...], grad_pre[:, span], preferred_element_type=jnp.float32
+        ).astype(jnp.bfloat16)
+        return carry
+
+    lax.fori_loop(0, hidden // chunk, up_chunk, 0)
+    to_mate(0).start()
+    turned[...] = jnp.transpose(gated[...])
+
+    def down_chunk(index, carry):
+        span = pl.ds(pl.multiple_of(index * chunk, chunk), chunk)
+        part = jnp.dot(turned[...], act[:, span], preferred_element_type=jnp.float32)
+        part_down[span, :] = jnp.transpose(part).astype(jnp.bfloat16)
+        return carry
+
+    lax.fori_loop(0, hidden // chunk, down_chunk, 0)
+    to_mate(1).start()
+    add_mate(0)
+    add_mate(1)
+    add_across(0)
+    add_across(1)
+    for layer in range(2):
+        to_mate(layer).wait_send()
+        to_across(layer).wait_send()
+        to_mate_again(layer).wait()
+
+    def finish(step, carry):
+        send_rows(step).wait_send()
+        send_back(step).wait()
+        return carry
+
+    lax.fori_loop(1, count, finish, 0)
+    own[1].wait()
+
+
+def middle(sent_rows, grads, up, down, router):
+    count, block, width = sent_rows.shape
+    hidden = up.shape[1]
+    any_space = pl.BlockSpec(memory_space=pl.ANY)
+    vmem = pl.BlockSpec(memory_space=pltpu.VMEM)
+    low = jnp.bfloat16
+    slots = count * block
+    return pl.pallas_call(
+        functools.partial(middle_kernel, count),
+        out_shape=(
+            jax.ShapeDtypeStruct((count, block, width), low),
+            jax.ShapeDtypeStruct((count, block, width), low),
+            jax.ShapeDtypeStruct((width, hidden), low),
+            jax.ShapeDtypeStruct((hidden, width), low),
+            jax.ShapeDtypeStruct((width, 128), jnp.float32),
+        ),
+        in_specs=[any_space, vmem, vmem, vmem, vmem],
+        out_specs=(any_space, vmem, vmem, vmem, vmem),
+        scratch_shapes=[
+            pltpu.VMEM((count, block, width), low),
+            pltpu.VMEM((slots, width), low),
+            pltpu.VMEM((slots, hidden), low),
+            pltpu.VMEM((slots, hidden), low),
+            pltpu.VMEM((slots, 128), low),
+            pltpu.VMEM((count, block, width), low),
+            pltpu.VMEM((width, slots), low),
+            pltpu.VMEM((width, hidden), low),
+            pltpu.VMEM((hidden, width), low),
+            pltpu.VMEM((width // 2, hidden), low),
+            pltpu.VMEM((hidden // 2, width), low),
+            pltpu.VMEM((width // 2, hidden), low),
+            pltpu.VMEM((hidden // 2, width), low),
+            pltpu.VMEM((width // 2, hidden), low),
+            pltpu.VMEM((hidden // 2, width), low),
+            pltpu.SemaphoreType.DMA((4, count)),
+            pltpu.SemaphoreType.DMA((6, 2)),
+            pltpu.SemaphoreType.DMA((2,)),
+        ],
+        compiler_params=pltpu.CompilerParams(
+            collective_id=3, has_side_effects=True, vmem_limit_bytes=60 * MIB
+        ),
+        cost_estimate=pl.CostEstimate(
+            flops=12 * slots * width * hidden, bytes_accessed=16 * MIB, transcendentals=0
+        ),
+    )(sent_rows, grads, up, down, router)
+
+
+def backward_kernel(
+    count,
+    tokens,
+    segments,
+    live,
+    out_grad,
+    weights,
+    joint,
+    mixed,
+    state,
+    logs,
+    slots,
+    back,
+    out_ret,
+    grad_router,
+    output,
+    tokens_grad,
+    shares,
+    returned,
+    grad_joint,
+    normed_all,
+    branch_all,
+    part,
+    mate_part,
+    pair_part,
+    far_part,
+    x_part,
+    ep_part,
+    turned,
+    ret_sems,
+    mate_sems,
+    x_sems,
+    ep_sems,
+    local_sems,
+):
+    me, grp = lax.axis_index("ep"), lax.axis_index("grp")
+    row_count, width = tokens.shape
+    sequences, length = segments.shape
+    block = back.shape[1]
+    slot_count = count * block
+    joint_width = joint.shape[1]
+    head_size = width // HEADS
+    factor = head_size ** (-0.5)
+    mate, across = core_peer(grp), x_peer(grp)
+    core, side_x = lax.rem(grp, 2), lax.div(grp, 2)
+    devices = weights.shape[0]
+    total = devices * weights.shape[1]
+    greet_all(count, me, grp)
+
+    def send_ret(step):
+        return remote_copy(
+            out_ret.at[step],
+            returned.at[me],
+            ret_sems.at[0, step],
+            ret_sems.at[1, step],
+            {"ep": partner(me, step, count)},
+        )
+
+    keep = pltpu.make_async_copy(out_ret.at[0], returned.at[me], local_sems.at[0])
+    keep.start()
+
+    def start(step, carry):
+        send_ret(step).start()
+        return carry
+
+    lax.fori_loop(1, count, start, 0)
+    pack = weights[:, :, joint_width + width :].reshape(total, 128)
+    gains = jnp.transpose(pack.astype(jnp.float32))
+    gain_one = gains[count : count + 1]
+    gain_two = gains[count + 1 : count + 2]
+    half = lax.broadcasted_iota(jnp.int32, (length, 128), 1) < head_size
+    halves = (flags(half), flags(jnp.logical_not(half)))
+    ints = jnp.transpose(segments[...].astype(jnp.float32)).astype(jnp.int32)
+
+    def chosen_of(rows):
+        index = lax.broadcasted_iota(jnp.int32, (length, slot_count), 1)
+        pair = slots[rows, :]
+        return flags((index == pair[:, 0:1]) | (index == pair[:, 1:2]))
+
+    def one_sequence(number, carry):
+        grad_one, grad_two = carry
+        rows = pl.ds(pl.multiple_of(number * length, length), length)
+        grad_normed_two = jnp.dot(
+            chosen_of(rows),
+            back[...].reshape(slot_count, width),
+            preferred_element_type=jnp.float32,
+        )
+        _, unit, inverse = normalize(state[rows, :], gain_two)
+        inner, share = normalize_back(grad_normed_two, gain_two, unit, inverse)
+        grad_two = grad_two + share[None, :]
+        grad_state = out_grad[rows, :].astype(jnp.float32) + inner
+        branch = grad_state.astype(jnp.bfloat16)
+        branch_all[rows, :] = branch
+        grad_mixed = times_t(
+            branch, weights[:, :, joint_width : joint_width + width].reshape(total, width)
+        ).astype(jnp.bfloat16)
+        allowed = seen(segments[pl.ds(number, 1), :], live[pl.ds(number, 1), :], column(ints, number))
+        log_all = logs[rows, :]
+        for pair in range(HEADS // 2):
+            at = pair * 128
+            query = joint[rows, at : at + 128]
+            key = joint[rows, width + at : width + at + 128]
+            value = joint[rows, 2 * width + at : 2 * width + at + 128]
+            grad_out = grad_mixed[:, at : at + 128]
+            results = []
+            for side in range(2):
+                scores = times_t(query * halves[side], key) * factor
+                head = 2 * pair + side
+                masked = jnp.where(allowed, scores, NEGATIVE)
+                probs = jnp.exp(masked - log_all[:, head : head + 1])
+                grad_value = outer(probs.astype(jnp.bfloat16), grad_out)
+                grad_probs = times_t(grad_out * halves[side], value)
+                delta = jnp.sum(probs * grad_probs, axis=-1, keepdims=True)
+                grad_scores = (probs * (grad_probs - delta)).astype(jnp.bfloat16)
+                grad_query = jnp.dot(grad_scores, key, preferred_element_type=jnp.float32) * factor
+                grad_key = outer(grad_scores, query) * factor
+                results.append((grad_query, grad_key, grad_value))
+            for third in range(3):
+                grad_joint[rows, third * width + at : third * width + at + 128] = jnp.where(
+                    half, results[0][third], results[1][third]
+                ).astype(jnp.bfloat16)
+        grad_normed = times_t(
+            grad_joint[rows, :], weights[:, :, :joint_width].reshape(total, joint_width)
+        )
+        normed, unit, inverse = normalize(tokens[rows, :].astype(jnp.float32), gain_one)
+        normed_all[rows, :] = normed.astype(jnp.bfloat16)
+        inner, share = normalize_back(grad_normed, gain_one, unit, inverse)
+        grad_one = grad_one + share[None, :]
+        tokens_grad[rows, :] = grad_state + inner
+        return grad_one, grad_two
+
+    nothing = jnp.zeros((1, width), jnp.float32)
+    grad_one, grad_two = lax.fori_loop(0, sequences, one_sequence, (nothing, nothing))
+
+    shape = (devices, total // devices)
+    turned[...] = jnp.transpose(mixed[...])
+    part[:, :, joint_width : joint_width + width] = (
+        jnp.dot(turned[...], branch_all[...], preferred_element_type=jnp.float32)
+        .astype(jnp.bfloat16)
+        .reshape(*shape, width)
+    )
+    lines = lax.broadcasted_iota(jnp.int32, (128, width), 0)
+    gain_lines = jnp.where(
+        lines == count, grad_one, jnp.where(lines == count + 1, grad_two, 0.0)
+    )
+    part[:, :, joint_width + width :] = (
+        (grad_router[...] + jnp.transpose(gain_lines)).astype(jnp.bfloat16).reshape(*shape, 128)
+    )
+    turned[...] = jnp.transpose(normed_all[...])
+    for third in range(3):
+        span = slice(third * width, (third + 1) * width)
+        part[:, :, span] = (
+            jnp.dot(turned[...], grad_joint[:, span], preferred_element_type=jnp.float32)
+            .astype(jnp.bfloat16)
+            .reshape(*shape, width)
+        )
+
+    def to_mate(which):
+        owner = 2 * which + 1 - core
+        return remote_copy(
+            part.at[pl.ds(owner * count, count)],
+            mate_part.at[which],
+            mate_sems.at[0, which],
+            mate_sems.at[1, which],
+            {"grp": mate},
+        )
+
+    to_x = remote_copy(pair_part, x_part, x_sems.at[0], x_sems.at[1], {"grp": across})
+
+    def to_ep(step):
+        other = partner(me, step, count)
+        return remote_copy(
+            far_part.at[other], ep_part.at[step], ep_sems.at[0, step], ep_sems.at[1, step], {"ep": other}
+        )
+
+    def summed(which, landing):
+        owner = 2 * which + core
+        return part[pl.ds(owner * count, count)].astype(jnp.float32) + landing.astype(jnp.float32)
+
+    to_mate(1 - side_x).start()
+    to_mate(side_x).start()
+    to_mate(1 - side_x).wait_recv()
+    pair_part[...] = summed(1 - side_x, mate_part[1 - side_x]).astype(jnp.bfloat16)
+    to_x.start()
+    to_mate(side_x).wait_recv()
+    to_x.wait_recv()
+    far_part[...] = (summed(side_x, mate_part[side_x]) + x_part[...].astype(jnp.float32)).astype(
+        jnp.bfloat16
+    )
+
+    def to_all(step, carry):
+        to_ep(step).start()
+        return carry
+
+    lax.fori_loop(1, count, to_all, 0)
+    keep.wait()
+
+    def from_all(step, carry):
+        send_ret(step).wait()
+        return carry
+
+    lax.fori_loop(1, count, from_all, 0)
+
+    def combine(number, carry):
+        rows = pl.ds(pl.multiple_of(number * length, length), length)
+        gathered = jnp.dot(
+            chosen_of(rows),
+            returned[...].reshape(slot_count, width),
+            preferred_element_type=jnp.float32,
+        )
+        output[rows, :] = (state[rows, :] + gathered).astype(jnp.bfloat16)
+        return carry
+
+    lax.fori_loop(0, sequences, combine, 0)
+
+    def add_share(step, added):
+        to_ep(step).wait_recv()
+        return added + ep_part[step].astype(jnp.float32)
+
+    shares[...] = lax.fori_loop(1, count, add_share, far_part[me].astype(jnp.float32))
+    to_mate(0).wait_send()
+    to_mate(1).wait_send()
+    to_x.wait_send()
+
+    def finish(step, carry):
+        to_ep(step).wait_send()
+        return carry
+
+    lax.fori_loop(1, count, finish, 0)
+
+
+def backward(
+    tokens, segments, live, out_grad, weights, joint, mixed, state, logs, slots, back, ret, router
+):
+    row_count, width = tokens.shape
+    count = back.shape[0]
+    devices, shard_rows, all_width = weights.shape
+    any_space = pl.BlockSpec(memory_space=pl.ANY)
+    vmem = pl.BlockSpec(memory_space=pltpu.VMEM)
+    low = jnp.bfloat16
+    quarter = (count, shard_rows, all_width)
+    return pl.pallas_call(
+        functools.partial(backward_kernel, count),
+        out_shape=(
+            jax.ShapeDtypeStruct((row_count, width), low),
+            jax.ShapeDtypeStruct((row_count, width), jnp.float32),
+            jax.ShapeDtypeStruct((shard_rows, all_width), jnp.float32),
+        ),
+        in_specs=[vmem] * 11 + [any_space, vmem],
+        out_specs=(vmem,) * 3,
+        scratch_shapes=[
+            pltpu.VMEM(back.shape, low),
+            pltpu.VMEM(joint.shape, low),
+            pltpu.VMEM((row_count, width), low),
+            pltpu.VMEM((row_count, width), low),
+            pltpu.VMEM(weights.shape, low),
+            pltpu.VMEM((2,) + quarter, low),
+            pltpu.VMEM(quarter, low),
+            pltpu.VMEM(quarter, low),
+            pltpu.VMEM(quarter, low),
+            pltpu.VMEM(quarter, low),
+            pltpu.VMEM((width, row_count), low),
+            pltpu.SemaphoreType.DMA((2, count)),
+            pltpu.SemaphoreType.DMA((2, 2)),
+            pltpu.SemaphoreType.DMA((2,)),
+            pltpu.SemaphoreType.DMA((2, count)),
+            pltpu.SemaphoreType.DMA((1,)),
+        ],
+        compiler_params=pltpu.CompilerParams(
+            collective_id=4, has_side_effects=True, vmem_limit_bytes=56 * MIB
+        ),
+    )(tokens, segments, live, out_grad, weights, joint, mixed, state, logs, slots, back, ret, router)
+
+
+def per_device_fused(
+    tokens,
+    segments,
+    patch_mask,
+    choices,
+    priority,
+    first_gain,
+    joint_weight,
+    output_weight,
+    second_gain,
+    router_weight,
+    expert_up,
+    expert_down,
+    out_grad,
+):
+    row_count, width = tokens.shape
+    experts = router_weight.shape[1]
+    capacity = (21 * choices.shape[1] * row_count + 20 * experts - 1) // (20 * experts)
+    block = -(-capacity // 16) * 16
+    shard_rows = first_gain.shape[0]
+    pack = jnp.concatenate(
+        [
+            router_weight,
+            first_gain[:, None],
+            second_gain[:, None],
+            jnp.zeros((shard_rows, 128 - experts - 2), jnp.bfloat16),
+        ],
+        axis=1,
+    )
+    weights, joint, mixed, state, sent_rows, logs, slots, grads = forward(
+        experts,
+        capacity,
+        block,
+        tokens,
+        segments,
+        patch_mask,
+        choices,
+        priority,
+        out_grad,
+        joint_weight,
+        output_weight,
+        pack,
+    )
+    router = weights[:, :, joint.shape[1] + width :].reshape(width, 128)
+    back, ret, grad_up, grad_down, grad_router = middle(
+        sent_rows, grads, expert_up[0], expert_down[0], router
+    )
+    output, tokens_grad, shares = backward(
+        tokens,
+        segments,
+        patch_mask,
+        out_grad,
+        weights,
+        joint,
+        mixed,
+        state,
+        logs,
+        slots,
+        back,
+        ret,
+        grad_router,
+    )
+    start = joint.shape[1] + width
+    return (
+        output,
+        tokens_grad,
+        shares[:, start + experts],
+        shares[:, : joint.shape[1]],
+        shares[:, joint.shape[1] : start],
+        shares[:, start + experts + 1],
+        shares[:, start : start + experts],
+        grad_up.astype(jnp.float32)[None],
+        grad_down.astype(jnp.float32)[None],
+    )
 
 
 def experts_both_ways(sent_rows, sent_grads, up, down, router):
@@ -487,6 +1406,7 @@
         P("ep", None, None),
         P("ep", None, None),
     )
+    fused = mesh.shape["grp"] == 4 and mesh.shape["ep"] == 8
     return jax.shard_map(
-        per_device, mesh=mesh, in_specs=in_specs, out_specs=out_specs, check_vma=False
-    )
+        per_device_fused if fused else per_device, mesh=mesh, in_specs=in_specs, out_specs=out_specs, check_vma=False
+    )

time: 923 us -> 316 us (0.34)
  waiting for transfers between devices: 358 us -> 0 us
  blocking collectives: 221 us -> 0 us
  Pallas kernels: 193 us -> 287 us
  matrix products: 79 us -> 0 us
  other arithmetic: 20.7 us -> 5.23 us
  between operations: 14.6 us -> 0.72 us
    reduce_scatter x3 -> x0, waiting for transfers between devices: 273 us -> none  [the longest x1 131 us: per_device(): lax.psum_scatter(grad_output_w, ('grp', 'ep'), scatter_dimension=0, tiled...]
    all_gather x2 -> x0, blocking collectives: 133 us -> none  [the longest x1 67.1 us: per_device(): lax.all_gather(output_weight, ('grp', 'ep'), axis=0, tiled=True)]
    pallas_call x1 -> x3, Pallas kernels: 193 us -> 287 us  [the longest x1 126 us: middle(): pl.pallas_call(functools.partial(middle_kernel, count), out_shape=(jax.Sh...]
    unnamed x2 -> x0, blocking collectives: 87.8 us -> none
    psum x1 -> x0, waiting for transfers between devices: 83.4 us -> none  [per_device(): lax.psum(grad_up, 'grp').astype(jnp.float32)[None]]
    dot_general x24 -> x0, matrix products: 79 us -> none  [the longest x4 17.4 us: outer(): lax.dot_general(left, right, (((0,), (0,)), ((), ())), preferred_element_...]
    unnamed x69 -> x33, local copies, waits for them, and re-layouts: 23.3 us -> 14.2 us
  transfers between devices with their start and end apart: 5 -> 0, of which waited for: 4 -> 0; matrix products, arithmetic and copies ran while one was open for 8% -> 0% of each run, Pallas kernels for 0% -> 0%
where the time goes in v2:
time: 316 us; the launch traced here: 315 us
  Pallas kernels  287 us (91%)
  local copies, waits for them, and re-layouts  22.4 us (7%)
  other arithmetic  5.23 us (2%)
    pallas_call x1, Pallas kernels, middle(): pl.pallas_call(functools.partial(middle_kernel, count), out_shape=(jax.Sh...  126 us
    pallas_call x1, Pallas kernels, backward(): pl.pallas_call(functools.partial(backward_kernel, count), out_shape=(jax....  100 us
    pallas_call x1, Pallas kernels, forward(): pl.pallas_call(functools.partial(forward_kernel, count, capacity), out_sh...  60.5 us
    unnamed x33, local copies, waits for them, and re-layouts  14.2 us

profile of v2, /device:TPU:0, one launch (start us, length us, event | category | flops | bytes accessed | tf_op | source)
XLA Modules:
  0.0 315.2 jit_solution(9007995336563936392)
XLA Ops:
  0.7 0.1 pad.3.clone
  0.7 0.7 copy.28
  1.5 0.7 copy.29
  2.2 0.8 copy.27
  3.0 0.1 maximum_maximum_fusion.pack_shard
  3.1 0.9 copy.30.picks
  4.0 0.0 copy-start
  4.0 1.2 copy-done
  5.2 0.0 copy-start.1
  5.2 1.2 copy-done.1
  6.4 0.0 copy-start.5
  6.4 0.8 copy-done.5
  7.2 0.0 copy-start.6
  7.2 0.7 copy-done.6
  8.0 0.0 copy-start.7
  8.0 0.7 copy-done.7
  8.6 0.0 copy-start.8
  8.6 0.7 copy-done.8
  9.3 0.0 copy-start.9
  9.3 0.7 copy-done.9
  10.0 60.5 %shard_map.196 = (bf16[32,16,2176]{2,1,0:T(8,128)(2,1)}, bf16[1024,1536]{1,0:T(8,128)(2,1)}, bf16[1024,512]{1,0:T(8,128)(2,1)S(1)}, f32[1024,512]{1,0:T(8,128)},...) custom-call(bf16[1024,512]{1,0:T(8,128)(2,1)S(1)} %copy-done, ...), custom_call_target="tpu_custom_call" | custom-call | tf_op jit(solution)/shard_map/pallas_call | solution.py:590
  70.5 0.0 copy-start.2
  70.5 1.0 copy-done.2
  71.5 0.0 copy-start.3
  71.5 0.8 copy-done.3
  72.3 0.0 copy-start.4
  72.3 0.8 copy-done.4
  73.1 1.6 slice.18
  74.6 126.2 %shard_map.197 = (bf16[8,272,512]{2,1,0:T(8,128)(2,1)}, bf16[8,272,512]{2,1,0:T(8,128)(2,1)}, bf16[512,2048]{1,0:T(8,128)(2,1)}, bf16[2048,512]{1,0:T(8,128)(2,1)}, f32[512,128]{1,0:T(8,128)}) custom-call(bf16[8,272,512]{2,1,0:T(8,128)(2,1)} %get-tuple-element.31.sent_rows, bf16[8,272,512]{2,1,0:T(8,128)(2,1)} %get-tuple-element.32.grads, ...), custom_call_target="tpu_custom_call" | custom-call | flops 27380416512 | bytes 16777216 | tf_op jit(solution)/shard_map/pallas_call | solution.py:823
  200.8 0.0 copy-start.11
  200.8 100.2 %shard_map.198 = (bf16[1024,512]{1,0:T(8,128)(2,1)}, f32[1024,512]{1,0:T(8,128)}, f32[16,2176]{1,0:T(8,128)}) custom-call(bf16[1024,512]{1,0:T(8,128)(2,1)} %tokens.3, s32[4,256]{1,0:T(4,128)} %segments.3, s32[4,256]{1,0:T(4,128)} %live.3, bf16[1024,512]{1,0:T(8,128)(2,1)} %out_grad.3, bf16[32,16,2176]{2,1,0:T(8,128)(2,1)} %get-tuple-element.25.weights, ...), custom_call_target="tpu_custom_call" | custom-call | tf_op jit(solution)/shard_map/pallas_call | solution.py:1104
  301.0 1.5 slice_reduce_fusion
  302.5 0.7 slice.23
  303.2 0.7 copy.31
  303.8 1.4 slice.21
  305.2 1.5 slice.20
  306.7 0.0 copy-done.11
  306.7 0.0 copy-start.10
  306.7 2.5 bitcast_convert_fusion.1
  309.3 0.0 copy-done.10
  309.3 0.0 copy-start.13
  309.3 2.6 bitcast_convert_fusion
  311.9 0.0 copy-done.13
  311.9 0.0 copy-start.12
  311.9 1.0 copy.34
  312.9 1.0 copy-done.12
  313.9 1.3 copy.35
  (1 shorter events, 0.0 us)
Async XLA Ops:
  4.0 1.2 copy-start
  5.2 1.2 copy-start.1
  6.4 0.8 copy-start.5
  7.2 0.7 copy-start.6
  8.0 0.7 copy-start.7
  8.6 0.7 copy-start.8
  9.3 0.7 copy-start.9
  70.5 1.0 copy-start.2
  71.5 0.8 copy-start.3
  72.3 0.8 copy-start.4
  200.8 105.9 %copy-start.11 = (bf16[512,2048]{1,0:T(8,128)(2,1)S(1)}, bf16[512,2048]{1,0:T(8,128)(2,1)}, u32[]{:S(2)}) copy-start(bf16[512,2048]{1,0:T(8,128)(2,1)} %get-tuple-element.39) | copy-start | bytes 6291460
  306.7 2.5 copy-start.10
  309.3 2.6 copy-start.13
  311.9 2.0 copy-start.12

commit v3 on v2

--- a/solution.py
+++ b/solution.py
@@ -9,6 +9,10 @@
 
 MESH = pl.DeviceIdType.MESH
 MIB = 1 << 20
+PIECES = 4
+CHUNKS = 2 * PIECES
+EARLY = ((0, 0), (0, 1), (1, 0), (1, 1))
+LATE = ((0, 2), (0, 3), (1, 2), (1, 3))
 
 HEADS = 8
 
@@ -319,19 +323,62 @@
     )
 
 
+def expert_of(me, grp, count):
+    half = count // 2
+    other = lax.rem(lax.div(me, half) + lax.rem(grp, 2), 2)
+    return lax.rem(me, half) + half * other
+
+
+def seat(me, grp, step, count):
+    half = count // 2
+    core = lax.rem(lax.rem(grp, 2) + lax.div(step, half), 2)
+    return {
+        "grp": 2 * lax.div(grp, 2) + core,
+        "ep": partner(me, lax.rem(step, half), count),
+    }
+
+
+def visit(index, count):
+    return lax.div(index, 2) + (count // 2) * lax.rem(index, 2)
+
+
 def greet_all(count, me, grp):
     barrier = pltpu.get_barrier_semaphore()
+    half = count // 2
 
     def greet(step, carry):
-        pl.semaphore_signal(
-            barrier, inc=1, device_id={"ep": partner(me, step, count)}, device_id_type=MESH
-        )
+        device = {"grp": grp, "ep": partner(me, step, count)}
+        pl.semaphore_signal(barrier, inc=1, device_id=device, device_id_type=MESH)
         return carry
 
     lax.fori_loop(1, count, greet, 0)
-    for peer in (core_peer(grp), x_peer(grp)):
-        pl.semaphore_signal(barrier, inc=1, device_id={"grp": peer}, device_id_type=MESH)
-    pl.semaphore_wait(barrier, count + 1)
+
+    def greet_mate(step, carry):
+        device = {"grp": core_peer(grp), "ep": partner(me, step, count)}
+        pl.semaphore_signal(barrier, inc=1, device_id=device, device_id_type=MESH)
+        return carry
+
+    lax.fori_loop(0, half + 1, greet_mate, 0)
+    pl.semaphore_signal(barrier, inc=1, device_id={"grp": x_peer(grp)}, device_id_type=MESH)
+    pl.semaphore_wait(barrier, count + half + 1)
+
+
+def pieces_of(layer_rows):
+    def rows(chunk, side):
+        size = layer_rows[chunk // PIECES] // (2 * PIECES)
+        first = side * PIECES * size + (chunk % PIECES) * size
+        return pl.ds(pl.multiple_of(first, size), size)
+
+    return rows
+
+
+def up_piece(piece, side, side_rows, columns):
+    rows = pl.ds(pl.multiple_of(side * side_rows, side_rows), side_rows)
+    return rows, pl.ds(piece * columns, columns)
+
+
+def down_piece(piece, side, size):
+    return pl.ds(pl.multiple_of(piece * 2 * size + side * size, size), size)
 
 
 def seen(segment_row, live_row, segment_col):
@@ -353,6 +400,8 @@
     joint_shard,
     output_shard,
     pack_shard,
+    own_up,
+    own_down,
     weights,
     joint,
     mixed,
@@ -361,6 +410,8 @@
     logs,
     slots,
     grads,
+    used_up,
+    used_down,
     own_grads,
     normed_two,
     int_columns,
@@ -368,9 +419,13 @@
     x_sems,
     core_sems,
     grad_sems,
+    fetch_sems,
     local_sems,
 ):
     me, grp = lax.axis_index("ep"), lax.axis_index("grp")
+    expert = expert_of(me, grp, count)
+    core, side_x = lax.rem(grp, 2), lax.div(grp, 2)
+    half_ep = count // 2
     row_count, width = tokens.shape
     sequences, length = segments.shape
     block = sent_rows.shape[1]
@@ -388,6 +443,11 @@
         other = partner(me, step, count)
         return remote_copy(place, place, ep_sems.at[0, step], ep_sems.at[1, step], {"ep": other})
 
+    def relay(step):
+        place = shard(grp, partner(me, half_ep, count))
+        sems = ep_sems.at[0, half_ep + step], ep_sems.at[1, half_ep + step]
+        return remote_copy(place, place, *sems, {"ep": partner(me, step, count)})
+
     def to_x(step):
         place = shard(grp, partner(me, step, count))
         return remote_copy(place, place, x_sems.at[0, step], x_sems.at[1, step], {"grp": across})
@@ -403,8 +463,42 @@
             grads.at[step],
             grad_sems.at[0, step],
             grad_sems.at[1, step],
-            {"ep": partner(me, step, count)},
+            seat(me, grp, step, count),
         )
+
+    layers = ((own_up, used_up), (own_down, used_down))
+    rows_at = pieces_of((own_up.shape[0], own_down.shape[0]))
+
+    def fetch(chunk):
+        source, target = layers[chunk // PIECES]
+        place = rows_at(chunk, side_x)
+        sems = fetch_sems.at[0, chunk], fetch_sems.at[1, chunk]
+        device = {"grp": mate, "ep": partner(me, half_ep, count)}
+        return remote_copy(source.at[place], target.at[place], *sems, device)
+
+    def share_fetch(chunk):
+        place = layers[chunk // PIECES][1].at[rows_at(chunk, side_x)]
+        sems = fetch_sems.at[2, chunk], fetch_sems.at[3, chunk]
+        return remote_copy(place, place, *sems, {"grp": across})
+
+    far_steps = [step for step in range(count) if step % half_ep >= half_ep // 2]
+
+    def advance_grads(index):
+        send_grads(far_steps[index]).wait_send()
+        if index + 1 < len(far_steps):
+            send_grads(far_steps[index + 1]).start()
+
+    def advance(chunk):
+        @pl.when(core == 0)
+        def _():
+            fetch(chunk).wait_send()
+            if chunk + 2 < CHUNKS:
+                fetch(chunk + 2).start()
+
+        @pl.when(core == 1)
+        def _():
+            fetch(chunk).wait_recv()
+            share_fetch(chunk).start()
 
     mine = grp * count + me
     fill = [
@@ -427,9 +521,14 @@
         to_ep(step).start()
         return carry
 
-    lax.fori_loop(1, count, first_hop, 0)
+    lax.fori_loop(1, half_ep + 1, first_hop, 0)
     to_x(0).start()
     to_core(grp, 0, 0).start()
+
+    @pl.when(core == 0)
+    def _():
+        fetch(0).start()
+        fetch(1).start()
 
     ints = jnp.concatenate([segments[...], live[...]], axis=0).astype(jnp.float32)
     turned = jnp.transpose(ints)
@@ -466,28 +565,43 @@
     slot_rows = jnp.transpose(both)[0:8].astype(jnp.int32)
     row_one, row_two = slot_rows[0:1], slot_rows[1:2]
 
-    def rows_of(expert, values):
-        index = lax.broadcasted_iota(jnp.int32, (block, row_count), 0) + expert * block
+    def rows_of(number, values):
+        index = lax.broadcasted_iota(jnp.int32, (block, row_count), 0) + number * block
         chosen = flags((index == row_one) | (index == row_two))
         return jnp.dot(chosen, values[...], preferred_element_type=jnp.float32).astype(jnp.bfloat16)
 
-    def spread_grads(step, carry):
-        own_grads[step] = rows_of(partner(me, step, count), out_grad)
-
-        @pl.when(step > 0)
+    def spread_grads(index, carry):
+        step = visit(index, count)
+        own_grads[step] = rows_of(partner(expert, step, count), out_grad)
+
+        @pl.when((step > 0) & (lax.rem(step, half_ep) < half_ep // 2))
         def _():
             send_grads(step).start()
 
         return carry
 
     lax.fori_loop(0, count, spread_grads, 0)
+    send_grads(far_steps[0]).start()
     keep = pltpu.make_async_copy(own_grads.at[0], grads.at[0], local_sems.at[3])
     keep.start()
 
+    to_ep(half_ep).wait_recv()
+
+    def pass_far(step, carry):
+        relay(step).start()
+        return carry
+
+    lax.fori_loop(1, half_ep, pass_far, 0)
+    to_x(half_ep).start()
+    to_core(grp, 0, half_ep).start()
+
     def pass_on(step, carry):
-        to_ep(step).wait_recv()
-        to_x(step).start()
-        to_core(grp, 0, step).start()
+        @pl.when(step != half_ep)
+        def _():
+            to_ep(step).wait_recv()
+            to_x(step).start()
+            to_core(grp, 0, step).start()
+
         return carry
 
     lax.fori_loop(1, count, pass_on, 0)
@@ -505,6 +619,8 @@
         return carry
 
     lax.fori_loop(0, count, arrive, 0)
+    advance(0)
+    advance_grads(0)
 
     devices = weights.shape[0]
     total = devices * weights.shape[1]
@@ -553,15 +669,33 @@
         )
         state[rows, :] = after
         normed_two[rows, :] = normalize(after, gain_two)[0].astype(jnp.bfloat16)
+        for place in range(sequences):
+
+            @pl.when(number == place)
+            def _(place=place):
+                advance(place + 1)
+                if place % 2 == 1:
+                    advance_grads((place + 1) // 2)
+
         return carry
 
     lax.fori_loop(0, sequences, attend, 0)
 
-    def spread_rows(expert, carry):
-        sent_rows[expert] = rows_of(expert, normed_two)
+    def spread_rows(number, carry):
+        sent_rows[number] = rows_of(number, normed_two)
         return carry
 
     lax.fori_loop(0, count, spread_rows, 0)
+
+    for chunk in range(sequences + 1, CHUNKS):
+        advance(chunk)
+    advance_grads(3)
+
+    @pl.when(core == 1)
+    def _():
+        for chunk in range(CHUNKS):
+            share_fetch(chunk).wait()
+
     keep.wait()
     to_x(0).wait_send()
     to_core(grp, 0, 0).wait_send()
@@ -572,19 +706,38 @@
         to_x(step).wait_send()
         to_core(grp, 0, step).wait_send()
         to_core(across, 1, step).wait_send()
-        send_grads(step).wait()
+        send_grads(step).wait_recv()
+
+        @pl.when(lax.rem(step, half_ep) < half_ep // 2)
+        def _():
+            send_grads(step).wait_send()
+
         return carry
 
     lax.fori_loop(1, count, finish, 0)
 
 
 def forward(
-    count, capacity, block, tokens, segments, live, picks, ranks, out_grad, joint, output, pack
+    count,
+    capacity,
+    block,
+    tokens,
+    segments,
+    live,
+    picks,
+    ranks,
+    out_grad,
+    joint,
+    output,
+    pack,
+    up,
+    down,
 ):
     row_count, width = tokens.shape
     devices = width // joint.shape[0]
     all_width = joint.shape[1] + width + 128
     any_space = pl.BlockSpec(memory_space=pl.ANY)
+    hbm = pl.BlockSpec(memory_space=pltpu.HBM)
     vmem = pl.BlockSpec(memory_space=pltpu.VMEM)
     low = jnp.bfloat16
     return pl.pallas_call(
@@ -598,9 +751,11 @@
             jax.ShapeDtypeStruct((row_count, 128), jnp.float32),
             jax.ShapeDtypeStruct((row_count, 128), jnp.int32),
             jax.ShapeDtypeStruct((count, block, width), low),
+            jax.ShapeDtypeStruct(up.shape, low),
+            jax.ShapeDtypeStruct(down.shape, low),
         ),
-        in_specs=[vmem] * 6 + [any_space] * 3,
-        out_specs=(vmem,) * 7 + (any_space,),
+        in_specs=[vmem] * 6 + [any_space] * 3 + [hbm] * 2,
+        out_specs=(vmem,) * 7 + (hbm,) * 3,
         scratch_shapes=[
             pltpu.VMEM((count, block, width), low),
             pltpu.VMEM((row_count, width), low),
@@ -609,25 +764,30 @@
             pltpu.SemaphoreType.DMA((2, count)),
             pltpu.SemaphoreType.DMA((2, 2, count)),
             pltpu.SemaphoreType.DMA((2, count)),
+            pltpu.SemaphoreType.DMA((4, CHUNKS)),
             pltpu.SemaphoreType.DMA((4,)),
         ],
         compiler_params=pltpu.CompilerParams(
             collective_id=2, has_side_effects=True, vmem_limit_bytes=48 * MIB
         ),
-    )(tokens, segments, live, picks, ranks, out_grad, joint, output, pack)
+    )(tokens, segments, live, picks, ranks, out_grad, joint, output, pack, up, down)
 
 
 def middle_kernel(
     count,
     sent_rows,
     grads,
-    up_ref,
-    down_ref,
+    own_up,
+    own_down,
+    used_up,
+    used_down,
     router_ref,
     back_ref,
     out_ret,
-    grad_up_ref,
-    grad_down_ref,
+    part_up,
+    part_down,
+    early_up,
+    early_down,
     grad_router_ref,
     rows,
     gated,
@@ -636,88 +796,140 @@
     logit_grads,
     out_grads,
     turned,
-    part_up,
-    part_down,
-    mate_up,
-    mate_down,
-    half_up,
-    half_down,
-    far_up,
-    far_down,
+    turned_gated,
+    up_ref,
+    down_ref,
+    ret_sums,
+    back_sums,
+    x_up,
+    x_down,
     sems,
-    sum_sems,
+    x_sems,
     local_sem,
 ):
     me, grp = lax.axis_index("ep"), lax.axis_index("grp")
-    mate, across = core_peer(grp), x_peer(grp)
-    core = lax.rem(grp, 2)
+    expert = expert_of(me, grp, count)
     block, width = rows.shape[1:]
     hidden = up_ref.shape[1]
     chunk = 512
+
+    def load(up, down):
+        return (
+            pltpu.make_async_copy(up, up_ref, local_sem.at[2]),
+            pltpu.make_async_copy(down, down_ref, local_sem.at[3]),
+        )
+
+    @pl.when(lax.rem(grp, 2) == 0)
+    def _():
+        for copy in load(own_up, own_down):
+            copy.start()
+
+    @pl.when(lax.rem(grp, 2) == 1)
+    def _():
+        for copy in load(used_up, used_down):
+            copy.start()
+
     greet_all(count, me, grp)
 
     def send_rows(step):
-        other = partner(me, step, count)
+        other = partner(expert, step, count)
+        there = seat(me, grp, step, count)
         return remote_copy(
-            sent_rows.at[other], rows.at[step], sems.at[0, step], sems.at[1, step], {"ep": other}
+            sent_rows.at[other], rows.at[step], sems.at[0, step], sems.at[1, step], there
         )
 
     def send_back(step):
-        other = partner(me, step, count)
+        there = seat(me, grp, step, count)
         return remote_copy(
-            out_grads.at[step], back_ref.at[me], sems.at[2, step], sems.at[3, step], {"ep": other}
+            out_grads.at[step], back_ref.at[expert], sems.at[2, step], sems.at[3, step], there
         )
 
     own = [
-        pltpu.make_async_copy(sent_rows.at[me], rows.at[0], local_sem.at[0]),
-        pltpu.make_async_copy(out_grads.at[0], back_ref.at[me], local_sem.at[1]),
+        pltpu.make_async_copy(sent_rows.at[expert], rows.at[0], local_sem.at[0]),
+        pltpu.make_async_copy(out_grads.at[0], back_ref.at[expert], local_sem.at[1]),
     ]
     own[0].start()
 
-    def start(step, carry):
-        send_rows(step).start()
+    def start(index, carry):
+        send_rows(visit(index, count)).start()
         return carry
 
     lax.fori_loop(1, count, start, 0)
     own[0].wait()
+    for copy in load(used_up, used_down):
+        copy.wait()
     lanes = lax.broadcasted_iota(jnp.int32, (block, router_ref.shape[1]), 1)
 
-    def one_block(step, carry):
-        @pl.when(step > 0)
-        def _():
-            send_rows(step).wait_recv()
-
-        mine = rows[step]
-        cotangent = grads[step].astype(jnp.float32)
-        place = pl.ds(pl.multiple_of(step * block, 16), block)
-        logits = jnp.dot(mine, router_ref[...], preferred_element_type=jnp.float32)
+    across, side_x = x_peer(grp), lax.div(grp, 2)
+    part_hidden = hidden // 2
+    early = len(EARLY)
+
+    def over_x(index):
+        layer, piece = EARLY[index]
+        sems = x_sems.at[0, index], x_sems.at[1, index]
+        if layer == 0:
+            source = part_up.at[up_piece(piece, 1 - side_x, width // 2, chunk)]
+            target = x_up.at[:, pl.ds(piece * chunk, chunk)]
+        else:
+            source = part_down.at[down_piece(piece, 1 - side_x, chunk // 2)]
+            target = x_down.at[pl.ds(piece * chunk // 2, chunk // 2)]
+        return remote_copy(source, target, *sems, {"grp": across})
+
+    def gates_of(values):
+        logits = jnp.dot(values, router_ref[...], preferred_element_type=jnp.float32)
         logits = jnp.where(lanes < count, logits, NEGATIVE)
         weights = jnp.exp(logits - jnp.max(logits, axis=1, keepdims=True))
-        gate_all = weights / jnp.sum(weights, axis=1, keepdims=True)
-        here = (lanes == me).astype(jnp.float32)
-        gate = jnp.sum(gate_all * here, axis=1, keepdims=True)
-        pair = (gate * cotangent).astype(jnp.bfloat16)
-        gated[place, :] = pair
+        return weights / jnp.sum(weights, axis=1, keepdims=True)
+
+    here = (lanes == expert).astype(jnp.float32)
+
+    def through(step, mine, pair, base):
+        place = pl.ds(pl.multiple_of(step * block, 16), block)
         ret = jnp.zeros((block, width), jnp.float32)
         back = jnp.zeros((block, width), jnp.float32)
-        for first in range(0, hidden, chunk):
-            span = slice(first, first + chunk)
+        for first in range(0, part_hidden, chunk):
+            span = slice(base + first, base + first + chunk)
+            kept = slice(first, first + chunk)
             pre = jnp.dot(mine, up_ref[:, span], preferred_element_type=jnp.float32)
             cdf = 0.5 * (1.0 + lax.erf(pre * 0.7071067811865476))
             density = jnp.exp(-0.5 * pre * pre) * 0.3989422804014327
             low = (pre * cdf).astype(jnp.bfloat16)
-            act[place, span] = low
+            act[place, kept] = low
             ret = ret + jnp.dot(low, down_ref[span, :], preferred_element_type=jnp.float32)
             grad_act = times_t(pair, down_ref[span, :])
             slope = (grad_act * (cdf + pre * density)).astype(jnp.bfloat16)
-            grad_pre[place, span] = slope
+            grad_pre[place, kept] = slope
             back = back + times_t(slope, up_ref[:, span])
-        ret = ret.astype(jnp.bfloat16).astype(jnp.float32)
+        return ret, back
+
+    def first_half(index, carry):
+        step = visit(index, count)
+
+        @pl.when(step > 0)
+        def _():
+            send_rows(step).wait_recv()
+
+        mine = rows[step]
+        gate = jnp.sum(gates_of(mine) * here, axis=1, keepdims=True)
+        pair = (gate * grads[step].astype(jnp.float32)).astype(jnp.bfloat16)
+        gated[pl.ds(pl.multiple_of(step * block, 16), block), :] = pair
+        ret_sums[step], back_sums[step] = through(step, mine, pair, 0)
+        return carry
+
+    def second_half(index, carry):
+        step = visit(index, count)
+        mine = rows[step]
+        cotangent = grads[step].astype(jnp.float32)
+        place = pl.ds(pl.multiple_of(step * block, 16), block)
+        gate_all = gates_of(mine)
+        gate = jnp.sum(gate_all * here, axis=1, keepdims=True)
+        ret, back = through(step, mine, gated[place, :], part_hidden)
+        ret = (ret + ret_sums[step]).astype(jnp.bfloat16).astype(jnp.float32)
         out_ret[step] = (gate * ret).astype(jnp.bfloat16)
         gate_grad = jnp.sum(cotangent * ret, axis=1, keepdims=True)
         low_logits = (gate * gate_grad * (here - gate_all)).astype(jnp.bfloat16)
         logit_grads[place, :] = low_logits
-        back = back + times_t(low_logits, router_ref[...])
+        back = back + back_sums[step] + times_t(low_logits, router_ref[...])
         out_grads[step] = back.astype(jnp.bfloat16)
 
         @pl.when(step > 0)
@@ -730,79 +942,51 @@
 
         return carry
 
-    lax.fori_loop(0, count, one_block, 0)
+    def layer_sums(base):
+        def up_chunk(index, carry):
+            span = pl.ds(pl.multiple_of(index * chunk, chunk), chunk)
+            part_up[:, pl.ds(pl.multiple_of(base + index * chunk, chunk), chunk)] = jnp.dot(
+                turned[...], grad_pre[:, span], preferred_element_type=jnp.float32
+            ).astype(jnp.bfloat16)
+            return carry
+
+        def down_chunk(index, carry):
+            span = pl.ds(pl.multiple_of(index * chunk, chunk), chunk)
+            part = jnp.dot(turned_gated[...], act[:, span], preferred_element_type=jnp.float32)
+            part_down[pl.ds(pl.multiple_of(base + index * chunk, chunk), chunk), :] = jnp.transpose(
+                part
+            ).astype(jnp.bfloat16)
+            return carry
+
+        lax.fori_loop(0, part_hidden // chunk, up_chunk, 0)
+        lax.fori_loop(0, part_hidden // chunk, down_chunk, 0)
+
+    lax.fori_loop(0, count, first_half, 0)
     turned[...] = jnp.transpose(rows[...].reshape(count * block, width))
+    turned_gated[...] = jnp.transpose(gated[...])
+    layer_sums(0)
+    for index in range(early):
+        over_x(index).start()
+    lax.fori_loop(0, count, second_half, 0)
+    layer_sums(part_hidden)
     grad_router_ref[...] = jnp.dot(
         turned[...], logit_grads[...], preferred_element_type=jnp.float32
     )
-
-    up_rows, down_rows = half_up.shape[0], half_down.shape[0]
-    groups = (
-        (part_up, mate_up, half_up, far_up, grad_up_ref, up_rows),
-        (part_down, mate_down, half_down, far_down, grad_down_ref, down_rows),
-    )
-
-    def half_of(which, size):
-        return pl.ds(pl.multiple_of(which * size, size), size)
-
-    def to_mate(layer):
-        part, landing, _, _, _, size = groups[layer]
-        sem = sum_sems.at[0, layer], sum_sems.at[1, layer]
-        return remote_copy(part.at[half_of(1 - core, size)], landing, *sem, {"grp": mate})
-
-    def to_across(layer):
-        _, _, half, far, _, _ = groups[layer]
-        sem = sum_sems.at[2, layer], sum_sems.at[3, layer]
-        return remote_copy(half, far, *sem, {"grp": across})
-
-    def to_mate_again(layer):
-        result, size = groups[layer][4:]
-        sem = sum_sems.at[4, layer], sum_sems.at[5, layer]
-        place = result.at[half_of(core, size)]
-        return remote_copy(place, place, *sem, {"grp": mate})
-
-    def add_mate(layer):
-        part, landing, half, _, _, size = groups[layer]
-        to_mate(layer).wait_recv()
-        kept = part[half_of(core, size), :].astype(jnp.float32)
-        half[...] = (kept + landing[...].astype(jnp.float32)).astype(jnp.bfloat16)
-        to_across(layer).start()
-
-    def add_across(layer):
-        _, _, half, far, result, size = groups[layer]
-        to_across(layer).wait_recv()
-        result[half_of(core, size), :] = (
-            half[...].astype(jnp.float32) + far[...].astype(jnp.float32)
-        ).astype(jnp.bfloat16)
-        to_mate_again(layer).start()
-
-    def up_chunk(index, carry):
-        span = pl.ds(pl.multiple_of(index * chunk, chunk), chunk)
-        part_up[:, span] = jnp.dot(
-            turned[...], grad_pre[:, span], preferred_element_type=jnp.float32
-        ).astype(jnp.bfloat16)
-        return carry
-
-    lax.fori_loop(0, hidden // chunk, up_chunk, 0)
-    to_mate(0).start()
-    turned[...] = jnp.transpose(gated[...])
-
-    def down_chunk(index, carry):
-        span = pl.ds(pl.multiple_of(index * chunk, chunk), chunk)
-        part = jnp.dot(turned[...], act[:, span], preferred_element_type=jnp.float32)
-        part_down[span, :] = jnp.transpose(part).astype(jnp.bfloat16)
-        return carry
-
-    lax.fori_loop(0, hidden // chunk, down_chunk, 0)
-    to_mate(1).start()
-    add_mate(0)
-    add_mate(1)
-    add_across(0)
-    add_across(1)
-    for layer in range(2):
-        to_mate(layer).wait_send()
-        to_across(layer).wait_send()
-        to_mate_again(layer).wait()
+    for index in range(early):
+        layer, piece = EARLY[index]
+        over_x(index).wait_recv()
+        if layer == 0:
+            kept = part_up[up_piece(piece, side_x, width // 2, chunk)]
+            span = slice(piece * chunk, (piece + 1) * chunk)
+            added = kept.astype(jnp.float32) + x_up[:, span].astype(jnp.float32)
+            early_up[:, span] = added.astype(jnp.bfloat16)
+        else:
+            kept = part_down[down_piece(piece, side_x, chunk // 2), :]
+            span = slice(piece * chunk // 2, (piece + 1) * chunk // 2)
+            added = kept.astype(jnp.float32) + x_down[span, :].astype(jnp.float32)
+            early_down[span, :] = added.astype(jnp.bfloat16)
+    for index in range(early):
+        over_x(index).wait_send()
 
     def finish(step, carry):
         send_rows(step).wait_send()
@@ -813,10 +997,11 @@
     own[1].wait()
 
 
-def middle(sent_rows, grads, up, down, router):
+def middle(sent_rows, grads, up, down, used_up, used_down, router):
     count, block, width = sent_rows.shape
     hidden = up.shape[1]
     any_space = pl.BlockSpec(memory_space=pl.ANY)
+    hbm = pl.BlockSpec(memory_space=pltpu.HBM)
     vmem = pl.BlockSpec(memory_space=pltpu.VMEM)
     low = jnp.bfloat16
     slots = count * block
@@ -827,29 +1012,30 @@
             jax.ShapeDtypeStruct((count, block, width), low),
             jax.ShapeDtypeStruct((width, hidden), low),
             jax.ShapeDtypeStruct((hidden, width), low),
+            jax.ShapeDtypeStruct((width // 2, hidden // 2), low),
+            jax.ShapeDtypeStruct((hidden // 4, width), low),
             jax.ShapeDtypeStruct((width, 128), jnp.float32),
         ),
-        in_specs=[any_space, vmem, vmem, vmem, vmem],
-        out_specs=(any_space, vmem, vmem, vmem, vmem),
+        in_specs=[any_space, vmem, hbm, hbm, hbm, hbm, vmem],
+        out_specs=(any_space,) + (vmem,) * 6,
         scratch_shapes=[
             pltpu.VMEM((count, block, width), low),
             pltpu.VMEM((slots, width), low),
-            pltpu.VMEM((slots, hidden), low),
-            pltpu.VMEM((slots, hidden), low),
+            pltpu.VMEM((slots, hidden // 2), low),
+            pltpu.VMEM((slots, hidden // 2), low),
             pltpu.VMEM((slots, 128), low),
             pltpu.VMEM((count, block, width), low),
             pltpu.VMEM((width, slots), low),
-            pltpu.VMEM((width, hidden), low),
-            pltpu.VMEM((hidden, width), low),
-            pltpu.VMEM((width // 2, hidden), low),
-            pltpu.VMEM((hidden // 2, width), low),
-            pltpu.VMEM((width // 2, hidden), low),
-            pltpu.VMEM((hidden // 2, width), low),
-            pltpu.VMEM((width // 2, hidden), low),
-            pltpu.VMEM((hidden // 2, width), low),
+            pltpu.VMEM((width, slots), low),
+            pltpu.VMEM(up.shape, low),
+            pltpu.VMEM(down.shape, low),
+            pltpu.VMEM((count, block, width), jnp.float32),
+            pltpu.VMEM((count, block, width), jnp.float32),
+            pltpu.VMEM((width // 2, hidden // 2), low),
+            pltpu.VMEM((hidden // 4, width), low),
             pltpu.SemaphoreType.DMA((4, count)),
-            pltpu.SemaphoreType.DMA((6, 2)),
-            pltpu.SemaphoreType.DMA((2,)),
+            pltpu.SemaphoreType.DMA((2, len(EARLY))),
+            pltpu.SemaphoreType.DMA((4,)),
         ],
         compiler_params=pltpu.CompilerParams(
             collective_id=3, has_side_effects=True, vmem_limit_bytes=60 * MIB
@@ -857,7 +1043,7 @@
         cost_estimate=pl.CostEstimate(
             flops=12 * slots * width * hidden, bytes_accessed=16 * MIB, transcendentals=0
         ),
-    )(sent_rows, grads, up, down, router)
+    )(sent_rows, grads, up, down, used_up, used_down, router)
 
 
 def backward_kernel(
@@ -875,24 +1061,41 @@
     back,
     out_ret,
     grad_router,
+    part_up,
+    part_down,
+    early_up,
+    early_down,
     output,
     tokens_grad,
-    shares,
+    joint_share,
+    output_share,
+    pack_share,
+    sum_up,
+    sum_down,
     returned,
     grad_joint,
     normed_all,
     branch_all,
+    mixed_grads,
+    hidden_pairs,
     part,
     mate_part,
     pair_part,
+    x_part,
     far_part,
-    x_part,
     ep_part,
     turned,
+    x_up,
+    x_down,
+    half_up,
+    half_down,
+    far_up,
+    far_down,
     ret_sems,
     mate_sems,
     x_sems,
     ep_sems,
+    sum_sems,
     local_sems,
 ):
     me, grp = lax.axis_index("ep"), lax.axis_index("grp")
@@ -907,18 +1110,103 @@
     core, side_x = lax.rem(grp, 2), lax.div(grp, 2)
     devices = weights.shape[0]
     total = devices * weights.shape[1]
+    expert = expert_of(me, grp, count)
     greet_all(count, me, grp)
+
+    parts = EARLY + LATE
+    early = len(EARLY)
+    rows_up, size_up = part_up.shape[0] // 2, part_up.shape[1] // PIECES
+    size_down = part_down.shape[0] // (2 * PIECES)
+
+    def whole(index, arrays, side):
+        layer, piece = parts[index]
+        if layer == 0:
+            return arrays[0].at[up_piece(piece, side, rows_up, size_up)]
+        return arrays[1].at[down_piece(piece, side, size_down)]
+
+    def narrow(index, arrays):
+        layer, piece = parts[index]
+        if layer == 0:
+            return arrays[0].at[:, pl.ds((piece % 2) * size_up, size_up)]
+        return arrays[1].at[pl.ds((piece % 2) * size_down, size_down)]
+
+    def summed_x(index):
+        return narrow(index, (early_up, early_down) if index < early else (half_up, half_down))
+
+    def from_foreign(index):
+        return narrow(index, (far_up.at[index // early], far_down.at[index // early]))
+
+    def over_x(index):
+        sems = sum_sems.at[0, index], sum_sems.at[1, index]
+        source = whole(index, (part_up, part_down), 1 - side_x)
+        return remote_copy(source, narrow(index, (x_up, x_down)), *sems, {"grp": across})
+
+    def go_home(index):
+        sems = sum_sems.at[2, index], sum_sems.at[3, index]
+        device = {"grp": mate, "ep": partner(me, count // 2, count)}
+        return remote_copy(summed_x(index), from_foreign(index), *sems, device)
+
+    def spread_x(index):
+        place = whole(index, (sum_up, sum_down), side_x)
+        sems = sum_sems.at[4, index], sum_sems.at[5, index]
+        return remote_copy(place, place, *sems, {"grp": across})
+
+    def spread_core(index, side, first):
+        place = whole(index, (sum_up, sum_down), side)
+        sems = sum_sems.at[first, index], sum_sems.at[first + 1, index]
+        return remote_copy(place, place, *sems, {"grp": mate})
+
+    def own_half(index):
+        return spread_core(index, side_x, 6)
+
+    def other_half(index):
+        return spread_core(index, 1 - side_x, 8)
+
+    def leave(index):
+        @pl.when(core == 1)
+        def _():
+            go_home(index).start()
+
+    def add_x(index):
+        over_x(index).wait_recv()
+        kept = whole(index, (part_up, part_down), side_x)[...].astype(jnp.float32)
+        landed = narrow(index, (x_up, x_down))[...].astype(jnp.float32)
+        summed_x(index)[...] = (kept + landed).astype(jnp.bfloat16)
+        if index + 2 < len(parts):
+            over_x(index + 2).start()
+        leave(index)
+
+    def add_home(index):
+        @pl.when(core == 0)
+        def _():
+            go_home(index).wait_recv()
+            near = summed_x(index)[...].astype(jnp.float32)
+            foreign = from_foreign(index)[...].astype(jnp.float32)
+            whole(index, (sum_up, sum_down), side_x)[...] = (near + foreign).astype(jnp.bfloat16)
+            spread_x(index).start()
+            own_half(index).start()
+
+    def pass_half(index):
+        @pl.when(core == 0)
+        def _():
+            spread_x(index).wait_recv()
+            other_half(index).start()
+
+    for index in range(early):
+        leave(index)
+    over_x(early).start()
+    over_x(early + 1).start()
 
     def send_ret(step):
         return remote_copy(
             out_ret.at[step],
-            returned.at[me],
+            returned.at[expert],
             ret_sems.at[0, step],
             ret_sems.at[1, step],
-            {"ep": partner(me, step, count)},
+            seat(me, grp, step, count),
         )
 
-    keep = pltpu.make_async_copy(out_ret.at[0], returned.at[me], local_sems.at[0])
+    keep = pltpu.make_async_copy(out_ret.at[0], returned.at[expert], local_sems.at[0])
     keep.start()
 
     def start(step, carry):
@@ -926,6 +1214,9 @@
         return carry
 
     lax.fori_loop(1, count, start, 0)
+    pairs = HEADS // 2
+    columns = [(pair * 384, 384) for pair in range(pairs)]
+    columns += [(joint_width, width), (joint_width + width, 128)]
     pack = weights[:, :, joint_width + width :].reshape(total, 128)
     gains = jnp.transpose(pack.astype(jnp.float32))
     gain_one = gains[count : count + 1]
@@ -939,8 +1230,83 @@
         pair = slots[rows, :]
         return flags((index == pair[:, 0:1]) | (index == pair[:, 1:2]))
 
-    def one_sequence(number, carry):
-        grad_one, grad_two = carry
+    def to_mate(chunk, which):
+        first, size = columns[chunk]
+        span = pl.ds(first, size)
+        return remote_copy(
+            part.at[pl.ds((2 * which + 1 - core) * count, count), :, span],
+            mate_part.at[which, :, :, span],
+            mate_sems.at[0, chunk, which],
+            mate_sems.at[1, chunk, which],
+            {"grp": mate},
+        )
+
+    def to_x(chunk):
+        first, size = columns[chunk]
+        span = pl.ds(first, size)
+        sems = x_sems.at[0, chunk], x_sems.at[1, chunk]
+        source = pair_part.at[1 - side_x, :, :, span]
+        return remote_copy(source, x_part.at[:, :, span], *sems, {"grp": across})
+
+    def to_ep(chunk, step):
+        first, size = columns[chunk]
+        span = pl.ds(first, size)
+        other = partner(me, step, count)
+        return remote_copy(
+            far_part.at[other, :, span],
+            ep_part.at[step, :, span],
+            ep_sems.at[0, chunk, step],
+            ep_sems.at[1, chunk, step],
+            {"ep": other},
+        )
+
+    def sum_core(chunk):
+        first, size = columns[chunk]
+        span = slice(first, first + size)
+        for which in range(2):
+            to_mate(chunk, which).wait_recv()
+            owner = 2 * which + core
+            pair_part[which, :, :, span] = (
+                part[pl.ds(owner * count, count), :, span].astype(jnp.float32)
+                + mate_part[which, :, :, span].astype(jnp.float32)
+            ).astype(jnp.bfloat16)
+        to_x(chunk).start()
+
+    def sum_x(chunk):
+        first, size = columns[chunk]
+        span = slice(first, first + size)
+        to_x(chunk).wait_recv()
+        far_part[:, :, span] = (
+            pair_part[side_x, :, :, span].astype(jnp.float32) + x_part[:, :, span].astype(jnp.float32)
+        ).astype(jnp.bfloat16)
+
+        def start(step, carry):
+            to_ep(chunk, step).start()
+            return carry
+
+        lax.fori_loop(1, count, start, 0)
+
+    def sum_ep(chunk):
+        first, size = columns[chunk]
+        span = slice(first, first + size)
+
+        def add(step, added):
+            to_ep(chunk, step).wait_recv()
+            return added + ep_part[step, :, span].astype(jnp.float32)
+
+        share = lax.fori_loop(1, count, add, far_part[me, :, span].astype(jnp.float32))
+        if chunk < pairs:
+            for third in range(3):
+                at = third * width + chunk * 128
+                joint_share[:, at : at + 128] = share[:, third * 128 : third * 128 + 128]
+        elif chunk == pairs:
+            output_share[...] = share
+        else:
+            pack_share[...] = share
+
+    shape = (devices, total // devices)
+
+    def lower_part(number, carry):
         rows = pl.ds(pl.multiple_of(number * length, length), length)
         grad_normed_two = jnp.dot(
             chosen_of(rows),
@@ -949,27 +1315,47 @@
         )
         _, unit, inverse = normalize(state[rows, :], gain_two)
         inner, share = normalize_back(grad_normed_two, gain_two, unit, inverse)
-        grad_two = grad_two + share[None, :]
         grad_state = out_grad[rows, :].astype(jnp.float32) + inner
+        tokens_grad[rows, :] = grad_state
         branch = grad_state.astype(jnp.bfloat16)
         branch_all[rows, :] = branch
-        grad_mixed = times_t(
+        mixed_grads[rows, :] = times_t(
             branch, weights[:, :, joint_width : joint_width + width].reshape(total, width)
         ).astype(jnp.bfloat16)
         allowed = seen(segments[pl.ds(number, 1), :], live[pl.ds(number, 1), :], column(ints, number))
-        log_all = logs[rows, :]
-        for pair in range(HEADS // 2):
-            at = pair * 128
+        hidden_pairs[rows, :] = jnp.where(allowed, 0.0, NEGATIVE)
+        normed = normalize(tokens[rows, :].astype(jnp.float32), gain_one)[0]
+        normed_all[rows, :] = normed.astype(jnp.bfloat16)
+        return carry + share[None, :]
+
+    nothing = jnp.zeros((1, width), jnp.float32)
+    grad_two = lax.fori_loop(0, sequences, lower_part, nothing)
+    turned[...] = jnp.transpose(mixed[...])
+    first, size = columns[pairs]
+    part[:, :, first : first + size] = (
+        jnp.dot(turned[...], branch_all[...], preferred_element_type=jnp.float32)
+        .astype(jnp.bfloat16)
+        .reshape(*shape, size)
+    )
+    to_mate(pairs, 0).start()
+    to_mate(pairs, 1).start()
+    turned[...] = jnp.transpose(normed_all[...])
+
+    for pair in range(pairs):
+        at = pair * 128
+
+        def attend(number, carry, pair=pair, at=at):
+            rows = pl.ds(pl.multiple_of(number * length, length), length)
             query = joint[rows, at : at + 128]
             key = joint[rows, width + at : width + at + 128]
             value = joint[rows, 2 * width + at : 2 * width + at + 128]
-            grad_out = grad_mixed[:, at : at + 128]
+            grad_out = mixed_grads[rows, at : at + 128]
+            unseen = hidden_pairs[rows, :]
             results = []
             for side in range(2):
                 scores = times_t(query * halves[side], key) * factor
-                head = 2 * pair + side
-                masked = jnp.where(allowed, scores, NEGATIVE)
-                probs = jnp.exp(masked - log_all[:, head : head + 1])
+                log_all = logs[rows, 2 * pair + side : 2 * pair + side + 1]
+                probs = jnp.exp(scores + unseen - log_all)
                 grad_value = outer(probs.astype(jnp.bfloat16), grad_out)
                 grad_probs = times_t(grad_out * halves[side], value)
                 delta = jnp.sum(probs * grad_probs, axis=-1, keepdims=True)
@@ -981,80 +1367,59 @@
                 grad_joint[rows, third * width + at : third * width + at + 128] = jnp.where(
                     half, results[0][third], results[1][third]
                 ).astype(jnp.bfloat16)
+            return carry
+
+        lax.fori_loop(0, sequences, attend, 0, unroll=4)
+        first, size = columns[pair]
+        mine = jnp.concatenate(
+            [grad_joint[:, third * width + at : third * width + at + 128] for third in range(3)], axis=1
+        )
+        part[:, :, first : first + size] = (
+            jnp.dot(turned[...], mine, preferred_element_type=jnp.float32)
+            .astype(jnp.bfloat16)
+            .reshape(*shape, size)
+        )
+        to_mate(pair, 0).start()
+        to_mate(pair, 1).start()
+        sum_core(pairs if pair == 0 else pair - 1)
+        if pair == 0:
+            add_x(early)
+            add_x(early + 1)
+        elif pair == 1:
+            sum_x(pairs)
+        else:
+            sum_x(pair - 2)
+        if pair == 2:
+            for index in range(early):
+                add_home(index)
+            add_x(early + 2)
+            add_x(early + 3)
+            sum_ep(pairs)
+
+    def upper_part(number, carry):
+        rows = pl.ds(pl.multiple_of(number * length, length), length)
         grad_normed = times_t(
             grad_joint[rows, :], weights[:, :, :joint_width].reshape(total, joint_width)
         )
-        normed, unit, inverse = normalize(tokens[rows, :].astype(jnp.float32), gain_one)
-        normed_all[rows, :] = normed.astype(jnp.bfloat16)
+        _, unit, inverse = normalize(tokens[rows, :].astype(jnp.float32), gain_one)
         inner, share = normalize_back(grad_normed, gain_one, unit, inverse)
-        grad_one = grad_one + share[None, :]
-        tokens_grad[rows, :] = grad_state + inner
-        return grad_one, grad_two
-
-    nothing = jnp.zeros((1, width), jnp.float32)
-    grad_one, grad_two = lax.fori_loop(0, sequences, one_sequence, (nothing, nothing))
-
-    shape = (devices, total // devices)
-    turned[...] = jnp.transpose(mixed[...])
-    part[:, :, joint_width : joint_width + width] = (
-        jnp.dot(turned[...], branch_all[...], preferred_element_type=jnp.float32)
-        .astype(jnp.bfloat16)
-        .reshape(*shape, width)
-    )
+        tokens_grad[rows, :] = tokens_grad[rows, :] + inner
+        return carry + share[None, :]
+
+    grad_one = lax.fori_loop(0, sequences, upper_part, nothing)
     lines = lax.broadcasted_iota(jnp.int32, (128, width), 0)
     gain_lines = jnp.where(
         lines == count, grad_one, jnp.where(lines == count + 1, grad_two, 0.0)
     )
-    part[:, :, joint_width + width :] = (
+    first, size = columns[pairs + 1]
+    part[:, :, first : first + size] = (
         (grad_router[...] + jnp.transpose(gain_lines)).astype(jnp.bfloat16).reshape(*shape, 128)
     )
-    turned[...] = jnp.transpose(normed_all[...])
-    for third in range(3):
-        span = slice(third * width, (third + 1) * width)
-        part[:, :, span] = (
-            jnp.dot(turned[...], grad_joint[:, span], preferred_element_type=jnp.float32)
-            .astype(jnp.bfloat16)
-            .reshape(*shape, width)
-        )
-
-    def to_mate(which):
-        owner = 2 * which + 1 - core
-        return remote_copy(
-            part.at[pl.ds(owner * count, count)],
-            mate_part.at[which],
-            mate_sems.at[0, which],
-            mate_sems.at[1, which],
-            {"grp": mate},
-        )
-
-    to_x = remote_copy(pair_part, x_part, x_sems.at[0], x_sems.at[1], {"grp": across})
-
-    def to_ep(step):
-        other = partner(me, step, count)
-        return remote_copy(
-            far_part.at[other], ep_part.at[step], ep_sems.at[0, step], ep_sems.at[1, step], {"ep": other}
-        )
-
-    def summed(which, landing):
-        owner = 2 * which + core
-        return part[pl.ds(owner * count, count)].astype(jnp.float32) + landing.astype(jnp.float32)
-
-    to_mate(1 - side_x).start()
-    to_mate(side_x).start()
-    to_mate(1 - side_x).wait_recv()
-    pair_part[...] = summed(1 - side_x, mate_part[1 - side_x]).astype(jnp.bfloat16)
-    to_x.start()
-    to_mate(side_x).wait_recv()
-    to_x.wait_recv()
-    far_part[...] = (summed(side_x, mate_part[side_x]) + x_part[...].astype(jnp.float32)).astype(
-        jnp.bfloat16
-    )
-
-    def to_all(step, carry):
-        to_ep(step).start()
-        return carry
-
-    lax.fori_loop(1, count, to_all, 0)
+    to_mate(pairs + 1, 0).start()
+    to_mate(pairs + 1, 1).start()
+    sum_core(pairs - 1)
+    sum_core(pairs + 1)
+    sum_x(pairs - 2)
     keep.wait()
 
     def from_all(step, carry):
@@ -1074,25 +1439,68 @@
         return carry
 
     lax.fori_loop(0, sequences, combine, 0)
-
-    def add_share(step, added):
-        to_ep(step).wait_recv()
-        return added + ep_part[step].astype(jnp.float32)
-
-    shares[...] = lax.fori_loop(1, count, add_share, far_part[me].astype(jnp.float32))
-    to_mate(0).wait_send()
-    to_mate(1).wait_send()
-    to_x.wait_send()
-
-    def finish(step, carry):
-        to_ep(step).wait_send()
-        return carry
-
-    lax.fori_loop(1, count, finish, 0)
+    sum_x(pairs - 1)
+    sum_x(pairs + 1)
+    for index in range(early):
+        pass_half(index)
+    add_home(early)
+    add_home(early + 1)
+    for chunk in range(pairs):
+        sum_ep(chunk)
+    sum_ep(pairs + 1)
+    add_home(early + 2)
+    pass_half(early)
+    pass_half(early + 1)
+    add_home(early + 3)
+    pass_half(early + 2)
+    pass_half(early + 3)
+
+    @pl.when(core == 0)
+    def _():
+        for chunk in range(CHUNKS):
+            spread_x(chunk).wait_send()
+            own_half(chunk).wait_send()
+            other_half(chunk).wait_send()
+
+    @pl.when(core == 1)
+    def _():
+        for chunk in range(CHUNKS):
+            go_home(chunk).wait_send()
+            own_half(chunk).wait_recv()
+            other_half(chunk).wait_recv()
+
+    for index in range(early, len(parts)):
+        over_x(index).wait_send()
+    for chunk in range(len(columns)):
+        to_mate(chunk, 0).wait_send()
+        to_mate(chunk, 1).wait_send()
+        to_x(chunk).wait_send()
+
+        def finish(step, carry, chunk=chunk):
+            to_ep(chunk, step).wait_send()
+            return carry
+
+        lax.fori_loop(1, count, finish, 0)
 
 
 def backward(
-    tokens, segments, live, out_grad, weights, joint, mixed, state, logs, slots, back, ret, router
+    tokens,
+    segments,
+    live,
+    out_grad,
+    weights,
+    joint,
+    mixed,
+    state,
+    logs,
+    slots,
+    back,
+    ret,
+    router,
+    part_up,
+    part_down,
+    early_up,
+    early_down,
 ):
     row_count, width = tokens.shape
     count = back.shape[0]
@@ -1106,32 +1514,63 @@
         out_shape=(
             jax.ShapeDtypeStruct((row_count, width), low),
             jax.ShapeDtypeStruct((row_count, width), jnp.float32),
-            jax.ShapeDtypeStruct((shard_rows, all_width), jnp.float32),
+            jax.ShapeDtypeStruct((shard_rows, joint.shape[1]), jnp.float32),
+            jax.ShapeDtypeStruct((shard_rows, width), jnp.float32),
+            jax.ShapeDtypeStruct((shard_rows, 128), jnp.float32),
+            jax.ShapeDtypeStruct(part_up.shape, low),
+            jax.ShapeDtypeStruct(part_down.shape, low),
         ),
-        in_specs=[vmem] * 11 + [any_space, vmem],
-        out_specs=(vmem,) * 3,
+        in_specs=[vmem] * 11 + [any_space] + [vmem] * 5,
+        out_specs=(vmem,) * 7,
         scratch_shapes=[
             pltpu.VMEM(back.shape, low),
             pltpu.VMEM(joint.shape, low),
             pltpu.VMEM((row_count, width), low),
             pltpu.VMEM((row_count, width), low),
+            pltpu.VMEM((row_count, width), low),
+            pltpu.VMEM((row_count, segments.shape[1]), jnp.float32),
             pltpu.VMEM(weights.shape, low),
+            pltpu.VMEM((2,) + quarter, low),
             pltpu.VMEM((2,) + quarter, low),
             pltpu.VMEM(quarter, low),
             pltpu.VMEM(quarter, low),
             pltpu.VMEM(quarter, low),
-            pltpu.VMEM(quarter, low),
             pltpu.VMEM((width, row_count), low),
+            pltpu.VMEM(early_up.shape, low),
+            pltpu.VMEM(early_down.shape, low),
+            pltpu.VMEM(early_up.shape, low),
+            pltpu.VMEM(early_down.shape, low),
+            pltpu.VMEM((2,) + early_up.shape, low),
+            pltpu.VMEM((2,) + early_down.shape, low),
             pltpu.SemaphoreType.DMA((2, count)),
-            pltpu.SemaphoreType.DMA((2, 2)),
-            pltpu.SemaphoreType.DMA((2,)),
-            pltpu.SemaphoreType.DMA((2, count)),
+            pltpu.SemaphoreType.DMA((2, HEADS // 2 + 2, 2)),
+            pltpu.SemaphoreType.DMA((2, HEADS // 2 + 2)),
+            pltpu.SemaphoreType.DMA((2, HEADS // 2 + 2, count)),
+            pltpu.SemaphoreType.DMA((10, CHUNKS)),
             pltpu.SemaphoreType.DMA((1,)),
         ],
         compiler_params=pltpu.CompilerParams(
-            collective_id=4, has_side_effects=True, vmem_limit_bytes=56 * MIB
+            collective_id=4, has_side_effects=True, vmem_limit_bytes=60 * MIB
         ),
-    )(tokens, segments, live, out_grad, weights, joint, mixed, state, logs, slots, back, ret, router)
+    )(
+        tokens,
+        segments,
+        live,
+        out_grad,
+        weights,
+        joint,
+        mixed,
+        state,
+        logs,
+        slots,
+        back,
+        ret,
+        router,
+        part_up,
+        part_down,
+        early_up,
+        early_down,
+    )
 
 
 def per_device_fused(
@@ -1163,7 +1602,7 @@
         ],
         axis=1,
     )
-    weights, joint, mixed, state, sent_rows, logs, slots, grads = forward(
+    weights, joint, mixed, state, sent_rows, logs, slots, grads, used_up, used_down = forward(
         experts,
         capacity,
         block,
@@ -1176,12 +1615,14 @@
         joint_weight,
         output_weight,
         pack,
+        expert_up[0],
+        expert_down[0],
     )
     router = weights[:, :, joint.shape[1] + width :].reshape(width, 128)
-    back, ret, grad_up, grad_down, grad_router = middle(
-        sent_rows, grads, expert_up[0], expert_down[0], router
-    )
-    output, tokens_grad, shares = backward(
+    back, ret, part_up, part_down, early_up, early_down, grad_router = middle(
+        sent_rows, grads, expert_up[0], expert_down[0], used_up, used_down, router
+    )
+    output, tokens_grad, grad_joint, grad_output, grad_pack, grad_up, grad_down = backward(
         tokens,
         segments,
         patch_mask,
@@ -1195,16 +1636,19 @@
         back,
         ret,
         grad_router,
-    )
-    start = joint.shape[1] + width
+        part_up,
+        part_down,
+        early_up,
+        early_down,
+    )
     return (
         output,
         tokens_grad,
-        shares[:, start + experts],
-        shares[:, : joint.shape[1]],
-        shares[:, joint.shape[1] : start],
-        shares[:, start + experts + 1],
-        shares[:, start : start + experts],
+        grad_pack[:, experts],
+        grad_joint,
+        grad_output,
+        grad_pack[:, experts + 1],
+        grad_pack[:, :experts],
         grad_up.astype(jnp.float32)[None],
         grad_down.astype(jnp.float32)[None],
     )

time: 316 us -> 281 us (0.89)
  Pallas kernels: 287 us -> 252 us
    pallas_call x1, Pallas kernels: 126 us -> 82.7 us  [middle(): pl.pallas_call(functools.partial(middle_kernel, count), out_shape=(jax.Sh...]
    pallas_call x1, Pallas kernels: 60.5 us -> 73.8 us  [forward(): pl.pallas_call(functools.partial(forward_kernel, count, capacity), out_sh...]
    pallas_call x1, Pallas kernels: 100 us -> 95.3 us  [backward(): pl.pallas_call(functools.partial(backward_kernel, count), out_shape=(jax....]
    slice x4 -> x1, local copies, waits for them, and re-layouts: 5.08 us -> 1.47 us  [per_device_fused(): grad_pack[:, experts + 1]]
    unnamed x33 -> x37, local copies, waits for them, and re-layouts: 14.2 us -> 16.2 us
where the time goes in v3:
time: 281 us; the launch traced here: 280 us
  Pallas kernels  252 us (90%)
  local copies, waits for them, and re-layouts  20.8 us (7%)
  other arithmetic  6.97 us (2%)
    pallas_call x1, Pallas kernels, backward(): pl.pallas_call(functools.partial(backward_kernel, count), out_shape=(jax....  95.3 us
    pallas_call x1, Pallas kernels, middle(): pl.pallas_call(functools.partial(middle_kernel, count), out_shape=(jax.Sh...  82.7 us
    pallas_call x1, Pallas kernels, forward(): pl.pallas_call(functools.partial(forward_kernel, count, capacity), out_sh...  73.8 us
    unnamed x37, local copies, waits for them, and re-layouts  16.2 us

profile of v3, /device:TPU:0, one launch (start us, length us, event | category | flops | bytes accessed | tf_op | source)
XLA Modules:
  0.0 280.2 jit_solution(9770642652493675274)
XLA Ops:
  0.7 0.1 pad.3.clone
  0.7 0.7 copy.28
  1.5 0.7 copy.29
  2.2 0.8 copy.27
  3.0 0.1 maximum_maximum_fusion.pack_shard
  3.1 0.9 copy.30.picks
  4.0 0.0 copy-start
  4.0 1.2 copy-done
  5.2 0.0 copy-start.1
  5.2 1.2 copy-done.1
  6.4 0.0 copy-start.5
  6.4 0.8 copy-done.5
  7.2 0.0 copy-start.6
  7.2 0.7 copy-done.6
  8.0 0.0 copy-start.7
  8.0 0.7 copy-done.7
  8.6 0.0 copy-start.8
  8.6 0.7 copy-done.8
  9.3 0.0 copy-start.9
  9.3 0.7 copy-done.9
  10.0 73.8 %shard_map.196 = (bf16[32,16,2176]{2,1,0:T(8,128)(2,1)}, bf16[1024,1536]{1,0:T(8,128)(2,1)}, bf16[1024,512]{1,0:T(8,128)(2,1)S(1)}, f32[1024,512]{1,0:T(8,128)},...) custom-call(bf16[1024,512]{1,0:T(8,128)(2,1)S(1)} %copy-done, ...), custom_call_target="tpu_custom_call" | custom-call | tf_op jit(solution)/shard_map/pallas_call | solution.py:743
  83.8 0.0 copy-start.2
  83.8 1.0 copy-done.2
  84.8 0.0 copy-start.3
  84.8 0.8 copy-done.3
  85.6 0.0 copy-start.4
  85.6 0.8 copy-done.4
  86.4 1.6 slice.12
  87.9 82.7 %shard_map.197 = (bf16[8,272,512]{2,1,0:T(8,128)(2,1)}, bf16[8,272,512]{2,1,0:T(8,128)(2,1)}, bf16[512,2048]{1,0:T(8,128)(2,1)}, bf16[2048,512]{1,0:T(8,128)(2,1...) custom-call(bf16[8,272,512]{2,1,0:T(8,128)(2,1)} %get-tuple-element.39.sent_rows, ...), custom_call_target="tpu_custom_call" | custom-call | flops 27380416512 | bytes 16777216 | tf_op jit(solution)/shard_map/pallas_call | solution.py:1008
  170.6 95.3 %shard_map.198 = (bf16[1024,512]{1,0:T(8,128)(2,1)}, f32[1024,512]{1,0:T(8,128)}, f32[16,1536]{1,0:T(8,128)}, f32[16,512]{1,0:T(8,128)}, f32[16,128]{1,0:T(8,128...) custom-call(bf16[1024,512]{1,0:T(8,128)(2,1)} %tokens.3, s32[4,256]{1,0:T(4,128)} %segments.3, s32[4,256]{1,0:T(4,128)} %live.3, ...), custom_call_target="tpu_custom_call" | custom-call | tf_op jit(solution)/shard_map/pallas_call | solution.py:1512
  265.9 1.5 slice_reduce_fusion
  267.4 1.4 copy.31
  268.8 0.0 copy-start.10
  268.8 4.3 %bitcast_convert_fusion.1 = f32[1,512,2048]{2,1,0:T(8,128)} fusion(bf16[512,2048]{1,0:T(8,128)(2,1)} %get-tuple-element.55), kind=kLoop, calls=%fused_computation.1 | loop fusion | flops 1048576 | bytes 6291456 | tf_op jit(solution)/shard_map/broadcast_in_dim | solution.py:1652
  273.0 0.0 copy-done.10
  273.0 0.0 copy-start.12
  273.0 2.6 bitcast_convert_fusion
  275.7 0.0 copy-done.12
  275.7 0.0 copy-start.11
  275.7 1.0 copy.36
  276.6 1.0 copy-done.11
  277.6 0.0 copy-start.13
  277.6 0.0 copy-start.14
  277.6 1.3 copy.37
  278.9 0.0 copy-done.13
  278.9 0.6 copy.38
  279.6 0.0 copy-done.14
  279.6 0.6 copy.39
  (1 shorter events, 0.0 us)
Async XLA Ops:
  4.0 1.2 copy-start
  5.2 1.2 copy-start.1
  6.4 0.8 copy-start.5
  7.2 0.7 copy-start.6
  8.0 0.7 copy-start.7
  8.6 0.7 copy-start.8
  9.3 0.7 copy-start.9
  83.8 1.0 copy-start.2
  84.8 0.8 copy-start.3
  85.6 0.8 copy-start.4
  268.8 4.3 %copy-start.10 = (bf16[2048,512]{1,0:T(8,128)(2,1)S(1)}, bf16[2048,512]{1,0:T(8,128)(2,1)}, u32[]{:S(2)}) copy-start(bf16[2048,512]{1,0:T(8,128)(2,1)} %get-tuple-element.56) | copy-start | bytes 6291460
  273.0 2.6 copy-start.12
  275.7 2.0 copy-start.11
  277.6 1.3 copy-start.13
  277.6 2.0 copy-start.14

commit v4 on v3

--- a/solution.py
+++ b/solution.py
@@ -391,17 +391,31 @@
 def forward_kernel(
     count,
     capacity,
-    tokens,
+    tokens_in,
     segments,
     live,
     picks,
     ranks,
-    out_grad,
+    out_grad_in,
     joint_shard,
     output_shard,
-    pack_shard,
+    gains_shard,
+    router_shard,
     own_up,
     own_down,
+    weights_out,
+    joint_out,
+    mixed_out,
+    state_out,
+    rows_out,
+    logs_out,
+    slots_out,
+    router_out,
+    grads,
+    used_up,
+    used_down,
+    tokens,
+    out_grad,
     weights,
     joint,
     mixed,
@@ -409,9 +423,6 @@
     sent_rows,
     logs,
     slots,
-    grads,
-    used_up,
-    used_down,
     own_grads,
     normed_two,
     int_columns,
@@ -421,6 +432,7 @@
     grad_sems,
     fetch_sems,
     local_sems,
+    move_sems,
 ):
     me, grp = lax.axis_index("ep"), lax.axis_index("grp")
     expert = expert_of(me, grp, count)
@@ -429,6 +441,24 @@
     row_count, width = tokens.shape
     sequences, length = segments.shape
     block = sent_rows.shape[1]
+    moves = {
+        name: pltpu.make_async_copy(source, target, move_sems.at[place])
+        for place, (name, source, target) in enumerate(
+            (
+                ("out_grad", out_grad_in, out_grad),
+                ("tokens", tokens_in, tokens),
+                ("slots", slots, slots_out),
+                ("weights", weights, weights_out),
+                ("joint", joint, joint_out),
+                ("mixed", mixed, mixed_out),
+                ("state", state, state_out),
+                ("logs", logs, logs_out),
+                ("rows", sent_rows, rows_out),
+            )
+        )
+    }
+    moves["out_grad"].start()
+    moves["tokens"].start()
     joint_width = joint.shape[1]
     head_size = width // HEADS
     factor = head_size ** (-0.5)
@@ -508,12 +538,23 @@
         pltpu.make_async_copy(
             output_shard, weights.at[mine, :, pl.ds(joint_width, width)], local_sems.at[1]
         ),
-        pltpu.make_async_copy(
-            pack_shard, weights.at[mine, :, pl.ds(joint_width + width, 128)], local_sems.at[2]
-        ),
     ]
     for copy in fill:
         copy.start()
+    shard_rows = weights.shape[1]
+    stacked = jnp.concatenate(
+        [
+            router_shard[...].astype(jnp.float32),
+            gains_shard[...].astype(jnp.float32),
+            jnp.zeros((16 - count - 2, shard_rows), jnp.float32),
+        ],
+        axis=0,
+    ).astype(jnp.bfloat16)
+    tile = (16, 128)
+    diagonal = flags(
+        lax.broadcasted_iota(jnp.int32, tile, 0) == lax.broadcasted_iota(jnp.int32, tile, 1)
+    )
+    weights[mine, :, joint_width + width :] = outer(stacked, diagonal).astype(jnp.bfloat16)
     for copy in fill:
         copy.wait()
 
@@ -537,9 +578,14 @@
         [turned[:, sequences + i : sequences + i + 1] for i in range(sequences)], axis=0
     )
     rank_row = ranks[...].astype(jnp.float32)
-    rank_col = jnp.transpose(jnp.broadcast_to(rank_row, (8, row_count)))[:, 0:1]
+    lines = jnp.concatenate(
+        [rank_row, picks[...].astype(jnp.float32), jnp.zeros((5, row_count), jnp.float32)], axis=0
+    )
+    token_columns = jnp.transpose(lines)
+    rank_col = token_columns[:, 0:1]
     earlier = flags(rank_row < rank_col)
-    first, second = picks[:, 0:1], picks[:, 1:2]
+    first = token_columns[:, 1:2].astype(jnp.int32)
+    second = token_columns[:, 2:3].astype(jnp.int32)
     lanes = lax.broadcasted_iota(jnp.int32, (row_count, 128), 1)
     one = jnp.where(lanes == first, 1.0, 0.0)
     two = jnp.where(lanes == second + count, 1.0, 0.0)
@@ -562,6 +608,8 @@
     )
     both = jnp.where(lanes == 0, slot_one, jnp.where(lanes == 1, slot_two, nowhere))
     slots[...] = both.astype(jnp.int32)
+    moves["slots"].start()
+    moves["out_grad"].wait()
     slot_rows = jnp.transpose(both)[0:8].astype(jnp.int32)
     row_one, row_two = slot_rows[0:1], slot_rows[1:2]
 
@@ -622,9 +670,12 @@
     advance(0)
     advance_grads(0)
 
+    moves["weights"].start()
+    moves["tokens"].wait()
     devices = weights.shape[0]
     total = devices * weights.shape[1]
     pack = weights[:, :, joint_width + width :].reshape(total, 128)
+    router_out[...] = pack
     gains = jnp.transpose(pack.astype(jnp.float32))
     gain_one = gains[count : count + 1]
     gain_two = gains[count + 1 : count + 2]
@@ -680,12 +731,15 @@
         return carry
 
     lax.fori_loop(0, sequences, attend, 0)
+    for name in ("joint", "mixed", "state", "logs"):
+        moves[name].start()
 
     def spread_rows(number, carry):
         sent_rows[number] = rows_of(number, normed_two)
         return carry
 
     lax.fori_loop(0, count, spread_rows, 0)
+    moves["rows"].start()
 
     for chunk in range(sequences + 1, CHUNKS):
         advance(chunk)
@@ -696,6 +750,8 @@
         for chunk in range(CHUNKS):
             share_fetch(chunk).wait()
 
+    for name in ("slots", "weights", "joint", "mixed", "state", "logs", "rows"):
+        moves[name].wait()
     keep.wait()
     to_x(0).wait_send()
     to_core(grp, 0, 0).wait_send()
@@ -729,14 +785,14 @@
     out_grad,
     joint,
     output,
-    pack,
+    gains,
+    router,
     up,
     down,
 ):
     row_count, width = tokens.shape
     devices = width // joint.shape[0]
     all_width = joint.shape[1] + width + 128
-    any_space = pl.BlockSpec(memory_space=pl.ANY)
     hbm = pl.BlockSpec(memory_space=pltpu.HBM)
     vmem = pl.BlockSpec(memory_space=pltpu.VMEM)
     low = jnp.bfloat16
@@ -750,13 +806,23 @@
             jax.ShapeDtypeStruct((count, block, width), low),
             jax.ShapeDtypeStruct((row_count, 128), jnp.float32),
             jax.ShapeDtypeStruct((row_count, 128), jnp.int32),
+            jax.ShapeDtypeStruct((width, 128), low),
             jax.ShapeDtypeStruct((count, block, width), low),
             jax.ShapeDtypeStruct(up.shape, low),
             jax.ShapeDtypeStruct(down.shape, low),
         ),
-        in_specs=[vmem] * 6 + [any_space] * 3 + [hbm] * 2,
-        out_specs=(vmem,) * 7 + (hbm,) * 3,
+        in_specs=[hbm] + [vmem] * 4 + [hbm] * 3 + [vmem] * 2 + [hbm] * 2,
+        out_specs=(hbm,) * 7 + (vmem,) + (hbm,) * 3,
         scratch_shapes=[
+            pltpu.VMEM(tokens.shape, low),
+            pltpu.VMEM(out_grad.shape, low),
+            pltpu.VMEM((devices, joint.shape[0], all_width), low),
+            pltpu.VMEM((row_count, joint.shape[1]), low),
+            pltpu.VMEM((row_count, width), low),
+            pltpu.VMEM((row_count, width), jnp.float32),
+            pltpu.VMEM((count, block, width), low),
+            pltpu.VMEM((row_count, 128), jnp.float32),
+            pltpu.VMEM((row_count, 128), jnp.int32),
             pltpu.VMEM((count, block, width), low),
             pltpu.VMEM((row_count, width), low),
             pltpu.VMEM((segments.shape[1], 2 * segments.shape[0]), jnp.int32),
@@ -766,17 +832,31 @@
             pltpu.SemaphoreType.DMA((2, count)),
             pltpu.SemaphoreType.DMA((4, CHUNKS)),
             pltpu.SemaphoreType.DMA((4,)),
+            pltpu.SemaphoreType.DMA((9,)),
         ],
         compiler_params=pltpu.CompilerParams(
-            collective_id=2, has_side_effects=True, vmem_limit_bytes=48 * MIB
+            collective_id=2, has_side_effects=True, vmem_limit_bytes=63 * MIB
         ),
-    )(tokens, segments, live, picks, ranks, out_grad, joint, output, pack, up, down)
+    )(
+        tokens,
+        segments,
+        live,
+        picks,
+        ranks,
+        out_grad,
+        joint,
+        output,
+        gains,
+        router,
+        up,
+        down,
+    )
 
 
 def middle_kernel(
     count,
     sent_rows,
-    grads,
+    grads_in,
     own_up,
     own_down,
     used_up,
@@ -789,6 +869,7 @@
     early_up,
     early_down,
     grad_router_ref,
+    grads,
     rows,
     gated,
     act,
@@ -813,6 +894,9 @@
     hidden = up_ref.shape[1]
     chunk = 512
 
+    bring = pltpu.make_async_copy(grads_in, grads, local_sem.at[4])
+    bring.start()
+
     def load(up, down):
         return (
             pltpu.make_async_copy(up, up_ref, local_sem.at[2]),
@@ -858,6 +942,7 @@
     own[0].wait()
     for copy in load(used_up, used_down):
         copy.wait()
+    bring.wait()
     lanes = lax.broadcasted_iota(jnp.int32, (block, router_ref.shape[1]), 1)
 
     across, side_x = x_peer(grp), lax.div(grp, 2)
@@ -1016,9 +1101,10 @@
             jax.ShapeDtypeStruct((hidden // 4, width), low),
             jax.ShapeDtypeStruct((width, 128), jnp.float32),
         ),
-        in_specs=[any_space, vmem, hbm, hbm, hbm, hbm, vmem],
+        in_specs=[hbm] * 6 + [vmem],
         out_specs=(any_space,) + (vmem,) * 6,
         scratch_shapes=[
+            pltpu.VMEM((count, block, width), low),
             pltpu.VMEM((count, block, width), low),
             pltpu.VMEM((slots, width), low),
             pltpu.VMEM((slots, hidden // 2), low),
@@ -1035,10 +1121,10 @@
             pltpu.VMEM((hidden // 4, width), low),
             pltpu.SemaphoreType.DMA((4, count)),
             pltpu.SemaphoreType.DMA((2, len(EARLY))),
-            pltpu.SemaphoreType.DMA((4,)),
+            pltpu.SemaphoreType.DMA((5,)),
         ],
         compiler_params=pltpu.CompilerParams(
-            collective_id=3, has_side_effects=True, vmem_limit_bytes=60 * MIB
+            collective_id=3, has_side_effects=True, vmem_limit_bytes=63 * MIB
         ),
         cost_estimate=pl.CostEstimate(
             flops=12 * slots * width * hidden, bytes_accessed=16 * MIB, transcendentals=0
@@ -1048,9 +1134,31 @@
 
 def backward_kernel(
     count,
-    tokens,
+    tokens_in,
     segments,
     live,
+    out_grad_in,
+    weights_in,
+    joint_in,
+    mixed_in,
+    state_in,
+    logs_in,
+    slots_in,
+    back_in,
+    out_ret,
+    grad_router,
+    part_up_in,
+    part_down_in,
+    early_up_in,
+    early_down_in,
+    output,
+    tokens_grad,
+    joint_share,
+    output_share,
+    pack_share,
+    sum_up,
+    sum_down,
+    tokens,
     out_grad,
     weights,
     joint,
@@ -1059,19 +1167,10 @@
     logs,
     slots,
     back,
-    out_ret,
-    grad_router,
     part_up,
     part_down,
     early_up,
     early_down,
-    output,
-    tokens_grad,
-    joint_share,
-    output_share,
-    pack_share,
-    sum_up,
-    sum_down,
     returned,
     grad_joint,
     normed_all,
@@ -1097,7 +1196,30 @@
     ep_sems,
     sum_sems,
     local_sems,
+    bring_sems,
 ):
+    bring = [
+        pltpu.make_async_copy(source, target, bring_sems.at[place])
+        for place, (source, target) in enumerate(
+            (
+                (weights_in, weights),
+                (slots_in, slots),
+                (back_in, back),
+                (state_in, state),
+                (out_grad_in, out_grad),
+                (tokens_in, tokens),
+                (mixed_in, mixed),
+                (joint_in, joint),
+                (logs_in, logs),
+                (part_up_in, part_up),
+                (part_down_in, part_down),
+                (early_up_in, early_up),
+                (early_down_in, early_down),
+            )
+        )
+    ]
+    for copy in bring:
+        copy.start()
     me, grp = lax.axis_index("ep"), lax.axis_index("grp")
     row_count, width = tokens.shape
     sequences, length = segments.shape
@@ -1138,13 +1260,14 @@
 
     def over_x(index):
         sems = sum_sems.at[0, index], sum_sems.at[1, index]
-        source = whole(index, (part_up, part_down), 1 - side_x)
+        source = whole(index, (part_up_in, part_down_in), 1 - side_x)
         return remote_copy(source, narrow(index, (x_up, x_down)), *sems, {"grp": across})
 
     def go_home(index):
         sems = sum_sems.at[2, index], sum_sems.at[3, index]
         device = {"grp": mate, "ep": partner(me, count // 2, count)}
-        return remote_copy(summed_x(index), from_foreign(index), *sems, device)
+        source = narrow(index, (early_up_in, early_down_in)) if index < early else summed_x(index)
+        return remote_copy(source, from_foreign(index), *sems, device)
 
     def spread_x(index):
         place = whole(index, (sum_up, sum_down), side_x)
@@ -1217,6 +1340,8 @@
     pairs = HEADS // 2
     columns = [(pair * 384, 384) for pair in range(pairs)]
     columns += [(joint_width, width), (joint_width + width, 128)]
+    for copy in bring[:6]:
+        copy.wait()
     pack = weights[:, :, joint_width + width :].reshape(total, 128)
     gains = jnp.transpose(pack.astype(jnp.float32))
     gain_one = gains[count : count + 1]
@@ -1330,6 +1455,8 @@
 
     nothing = jnp.zeros((1, width), jnp.float32)
     grad_two = lax.fori_loop(0, sequences, lower_part, nothing)
+    for copy in bring[6:]:
+        copy.wait()
     turned[...] = jnp.transpose(mixed[...])
     first, size = columns[pairs]
     part[:, :, first : first + size] = (
@@ -1505,7 +1632,7 @@
     row_count, width = tokens.shape
     count = back.shape[0]
     devices, shard_rows, all_width = weights.shape
-    any_space = pl.BlockSpec(memory_space=pl.ANY)
+    hbm = pl.BlockSpec(memory_space=pltpu.HBM)
     vmem = pl.BlockSpec(memory_space=pltpu.VMEM)
     low = jnp.bfloat16
     quarter = (count, shard_rows, all_width)
@@ -1520,9 +1647,27 @@
             jax.ShapeDtypeStruct(part_up.shape, low),
             jax.ShapeDtypeStruct(part_down.shape, low),
         ),
-        in_specs=[vmem] * 11 + [any_space] + [vmem] * 5,
+        in_specs=[hbm, vmem, vmem] + [hbm] * 9 + [vmem] + [hbm] * 4,
         out_specs=(vmem,) * 7,
         scratch_shapes=[
+            pltpu.VMEM(array.shape, array.dtype)
+            for array in (
+                tokens,
+                out_grad,
+                weights,
+                joint,
+                mixed,
+                state,
+                logs,
+                slots,
+                back,
+                part_up,
+                part_down,
+                early_up,
+                early_down,
+            )
+        ]
+        + [
             pltpu.VMEM(back.shape, low),
             pltpu.VMEM(joint.shape, low),
             pltpu.VMEM((row_count, width), low),
@@ -1548,9 +1693,10 @@
             pltpu.SemaphoreType.DMA((2, HEADS // 2 + 2, count)),
             pltpu.SemaphoreType.DMA((10, CHUNKS)),
             pltpu.SemaphoreType.DMA((1,)),
+            pltpu.SemaphoreType.DMA((13,)),
         ],
         compiler_params=pltpu.CompilerParams(
-            collective_id=4, has_side_effects=True, vmem_limit_bytes=60 * MIB
+            collective_id=4, has_side_effects=True, vmem_limit_bytes=63 * MIB
         ),
     )(
         tokens,
@@ -1592,33 +1738,23 @@
     experts = router_weight.shape[1]
     capacity = (21 * choices.shape[1] * row_count + 20 * experts - 1) // (20 * experts)
     block = -(-capacity // 16) * 16
-    shard_rows = first_gain.shape[0]
-    pack = jnp.concatenate(
-        [
-            router_weight,
-            first_gain[:, None],
-            second_gain[:, None],
-            jnp.zeros((shard_rows, 128 - experts - 2), jnp.bfloat16),
-        ],
-        axis=1,
-    )
-    weights, joint, mixed, state, sent_rows, logs, slots, grads, used_up, used_down = forward(
+    weights, joint, mixed, state, sent_rows, logs, slots, router, grads, used_up, used_down = forward(
         experts,
         capacity,
         block,
         tokens,
         segments,
         patch_mask,
-        choices,
+        choices.T,
         priority,
         out_grad,
         joint_weight,
         output_weight,
-        pack,
+        jnp.stack([first_gain, second_gain]),
+        router_weight.T,
         expert_up[0],
         expert_down[0],
     )
-    router = weights[:, :, joint.shape[1] + width :].reshape(width, 128)
     back, ret, part_up, part_down, early_up, early_down, grad_router = middle(
         sent_rows, grads, expert_up[0], expert_down[0], used_up, used_down, router
     )

time: 281 us -> 261 us (0.929)
  local copies, waits for them, and re-layouts: 20.8 us -> 7.39 us
  Pallas kernels: 252 us -> 244 us
    unnamed x37 -> x15, local copies, waits for them, and re-layouts: 16.2 us -> 5.91 us
    pallas_call x1, Pallas kernels: 95.3 us -> 89.8 us  [backward(): pl.pallas_call(functools.partial(backward_kernel, count), out_shape=(jax....]
where the time goes in v4:
time: 261 us; the launch traced here: 260 us
  Pallas kernels  244 us (93%)
  other arithmetic  8.08 us (3%)
  local copies, waits for them, and re-layouts  7.39 us (3%)
    pallas_call x1, Pallas kernels, backward(): pl.pallas_call(functools.partial(backward_kernel, count), out_shape=(jax....  89.8 us
    pallas_call x1, Pallas kernels, middle(): pl.pallas_call(functools.partial(middle_kernel, count), out_shape=(jax.Sh...  81.8 us
    pallas_call x1, Pallas kernels, forward(): pl.pallas_call(functools.partial(forward_kernel, count, capacity), out_sh...  72.5 us
    unnamed x15, local copies, waits for them, and re-layouts  5.91 us

profile of v4, /device:TPU:0, one launch (start us, length us, event | category | flops | bytes accessed | tf_op | source)
XLA Modules:
  0.0 260.2 jit_solution(6909561216492003996)
XLA Ops:
  0.6 1.2 pad_maximum_fusion.gains_shard
  1.8 72.5 %shard_map.196 = (bf16[32,16,2176]{2,1,0:T(8,128)(2,1)}, bf16[1024,1536]{1,0:T(8,128)(2,1)}, bf16[1024,512]{1,0:T(8,128)(2,1)}, f32[1024,512]{1,0:T(8,128)}, bf1...) custom-call(bf16[1024,512]{1,0:T(8,128)(2,1)} %tokens_in.3, ...), custom_call_target="tpu_custom_call" | custom-call | tf_op jit(solution)/shard_map/pallas_call | solution.py:799
  74.3 81.8 %shard_map.197 = (bf16[8,272,512]{2,1,0:T(8,128)(2,1)}, bf16[8,272,512]{2,1,0:T(8,128)(2,1)}, bf16[512,2048]{1,0:T(8,128)(2,1)}, bf16[2048,512]{1,0:T(8,128)(2,1...) custom-call(bf16[8,272,512]{2,1,0:T(8,128)(2,1)} %get-tuple-element.40.sent_rows, ...), custom_call_target="tpu_custom_call" | custom-call | flops 27380416512 | bytes 16777216 | tf_op jit(solution)/shard_map/pallas_call | solution.py:1093
  156.1 89.8 %shard_map.198 = (bf16[1024,512]{1,0:T(8,128)(2,1)}, f32[1024,512]{1,0:T(8,128)}, f32[16,1536]{1,0:T(8,128)}, f32[16,512]{1,0:T(8,128)}, f32[16,128]{1,0:T(8,128...) custom-call(bf16[1024,512]{1,0:T(8,128)(2,1)} %tokens_in.3, s32[4,256]{1,0:T(4,128)} %segments.3, s32[4,256]{1,0:T(4,128)} %live.3, ...), custom_call_target="tpu_custom_call" | custom-call | tf_op jit(solution)/shard_map/pallas_call | solution.py:1639
  245.9 1.5 slice_reduce_fusion
  247.4 1.4 copy.23
  248.8 0.0 copy-start
  248.8 4.3 %bitcast_convert_fusion.1 = f32[1,512,2048]{2,1,0:T(8,128)} fusion(bf16[512,2048]{1,0:T(8,128)(2,1)} %get-tuple-element.57), kind=kLoop, calls=%fused_computation.1 | loop fusion | flops 1048576 | bytes 6291456 | tf_op jit(solution)/shard_map/broadcast_in_dim | solution.py:1788
  253.0 0.0 copy-done
  253.0 0.0 copy-start.2
  253.0 2.6 %bitcast_convert_fusion = f32[1,2048,512]{2,1,0:T(8,128)} fusion(bf16[2048,512]{1,0:T(8,128)(2,1)S(1)} %copy-done), kind=kLoop, calls=%fused_computation | loop fusion | flops 1048576 | bytes 6291456 | tf_op jit(solution)/shard_map/broadcast_in_dim | solution.py:1789
  255.6 0.0 copy-done.2
  255.7 0.0 copy-start.1
  255.7 1.0 copy.28
  256.6 1.0 copy-done.1
  257.6 0.0 copy-start.3
  257.6 0.0 copy-start.4
  257.6 1.3 copy.29
  258.9 0.0 copy-done.3
  258.9 0.6 copy.30
  259.6 0.0 copy-done.4
  259.6 0.6 copy.31
Async XLA Ops:
  248.8 4.3 %copy-start = (bf16[2048,512]{1,0:T(8,128)(2,1)S(1)}, bf16[2048,512]{1,0:T(8,128)(2,1)}, u32[]{:S(2)}) copy-start(bf16[2048,512]{1,0:T(8,128)(2,1)} %get-tuple-element.58) | copy-start | bytes 6291460
  253.0 2.6 %copy-start.2 = (bf16[1024,512]{1,0:T(8,128)(2,1)S(1)}, bf16[1024,512]{1,0:T(8,128)(2,1)}, u32[]{:S(2)}) copy-start(bf16[1024,512]{1,0:T(8,128)(2,1)} %get-tuple-element.88) | copy-start | bytes 3145732
  255.7 2.0 copy-start.1
  257.6 1.3 copy-start.3
  257.6 2.0 copy-start.4

commit v5 on v4

--- a/solution.py
+++ b/solution.py
@@ -12,6 +12,7 @@
 PIECES = 4
 CHUNKS = 2 * PIECES
 EARLY = ((0, 0), (0, 1), (1, 0), (1, 1))
+SETTLED = 2
 LATE = ((0, 2), (0, 3), (1, 2), (1, 3))
 
 HEADS = 8
@@ -884,6 +885,8 @@
     back_sums,
     x_up,
     x_down,
+    half_up,
+    far_up,
     sems,
     x_sems,
     local_sem,
@@ -959,6 +962,31 @@
             source = part_down.at[down_piece(piece, 1 - side_x, chunk // 2)]
             target = x_down.at[pl.ds(piece * chunk // 2, chunk // 2)]
         return remote_copy(source, target, *sems, {"grp": across})
+
+    def go_home(index):
+        place = pl.ds(EARLY[index][1] * chunk, chunk)
+        sems = x_sems.at[2, index], x_sems.at[3, index]
+        device = {"grp": core_peer(grp), "ep": partner(me, count // 2, count)}
+        return remote_copy(half_up.at[:, place], far_up.at[:, place], *sems, device)
+
+    def add_x(index):
+        layer, piece = EARLY[index]
+        over_x(index).wait_recv()
+        if layer == 0:
+            kept = part_up[up_piece(piece, side_x, width // 2, chunk)]
+            span = slice(piece * chunk, (piece + 1) * chunk)
+            added = kept.astype(jnp.float32) + x_up[:, span].astype(jnp.float32)
+            half_up[:, span] = added.astype(jnp.bfloat16)
+
+            @pl.when(lax.rem(grp, 2) == 1)
+            def _():
+                go_home(index).start()
+
+        else:
+            kept = part_down[down_piece(piece, side_x, chunk // 2), :]
+            span = slice(piece * chunk // 2, (piece + 1) * chunk // 2)
+            added = kept.astype(jnp.float32) + x_down[span, :].astype(jnp.float32)
+            early_down[span, :] = added.astype(jnp.bfloat16)
 
     def gates_of(values):
         logits = jnp.dot(values, router_ref[...], preferred_element_type=jnp.float32)
@@ -1025,6 +1053,13 @@
         def _():
             own[1].start()
 
+        @pl.when(index == count // 2)
+        def _():
+            for part in range(SETTLED):
+                add_x(part)
+            for part in range(SETTLED, early):
+                over_x(part).start()
+
         return carry
 
     def layer_sums(base):
@@ -1050,26 +1085,29 @@
     turned[...] = jnp.transpose(rows[...].reshape(count * block, width))
     turned_gated[...] = jnp.transpose(gated[...])
     layer_sums(0)
-    for index in range(early):
+    for index in range(SETTLED):
         over_x(index).start()
     lax.fori_loop(0, count, second_half, 0)
     layer_sums(part_hidden)
     grad_router_ref[...] = jnp.dot(
         turned[...], logit_grads[...], preferred_element_type=jnp.float32
     )
-    for index in range(early):
-        layer, piece = EARLY[index]
-        over_x(index).wait_recv()
-        if layer == 0:
-            kept = part_up[up_piece(piece, side_x, width // 2, chunk)]
-            span = slice(piece * chunk, (piece + 1) * chunk)
-            added = kept.astype(jnp.float32) + x_up[:, span].astype(jnp.float32)
-            early_up[:, span] = added.astype(jnp.bfloat16)
-        else:
-            kept = part_down[down_piece(piece, side_x, chunk // 2), :]
-            span = slice(piece * chunk // 2, (piece + 1) * chunk // 2)
-            added = kept.astype(jnp.float32) + x_down[span, :].astype(jnp.float32)
-            early_down[span, :] = added.astype(jnp.bfloat16)
+    for index in range(SETTLED, early):
+        add_x(index)
+
+    @pl.when(lax.rem(grp, 2) == 0)
+    def _():
+        for index in range(SETTLED):
+            go_home(index).wait_recv()
+        early_up[...] = (half_up[...].astype(jnp.float32) + far_up[...].astype(jnp.float32)).astype(
+            jnp.bfloat16
+        )
+
+    @pl.when(lax.rem(grp, 2) == 1)
+    def _():
+        for index in range(SETTLED):
+            go_home(index).wait_send()
+
     for index in range(early):
         over_x(index).wait_send()
 
@@ -1119,8 +1157,10 @@
             pltpu.VMEM((count, block, width), jnp.float32),
             pltpu.VMEM((width // 2, hidden // 2), low),
             pltpu.VMEM((hidden // 4, width), low),
+            pltpu.VMEM((width // 2, hidden // 2), low),
+            pltpu.VMEM((width // 2, hidden // 2), low),
             pltpu.SemaphoreType.DMA((4, count)),
-            pltpu.SemaphoreType.DMA((2, len(EARLY))),
+            pltpu.SemaphoreType.DMA((4, len(EARLY))),
             pltpu.SemaphoreType.DMA((5,)),
         ],
         compiler_params=pltpu.CompilerParams(
@@ -1151,8 +1191,8 @@
     part_down_in,
     early_up_in,
     early_down_in,
-    output,
-    tokens_grad,
+    output_out,
+    tokens_grad_out,
     joint_share,
     output_share,
     pack_share,
@@ -1171,6 +1211,8 @@
     part_down,
     early_up,
     early_down,
+    output,
+    tokens_grad,
     returned,
     grad_joint,
     normed_all,
@@ -1299,6 +1341,10 @@
             over_x(index + 2).start()
         leave(index)
 
+    def spread(index):
+        spread_x(index).start()
+        own_half(index).start()
+
     def add_home(index):
         @pl.when(core == 0)
         def _():
@@ -1306,8 +1352,7 @@
             near = summed_x(index)[...].astype(jnp.float32)
             foreign = from_foreign(index)[...].astype(jnp.float32)
             whole(index, (sum_up, sum_down), side_x)[...] = (near + foreign).astype(jnp.bfloat16)
-            spread_x(index).start()
-            own_half(index).start()
+            spread(index)
 
     def pass_half(index):
         @pl.when(core == 0)
@@ -1315,7 +1360,7 @@
             spread_x(index).wait_recv()
             other_half(index).start()
 
-    for index in range(early):
+    for index in range(SETTLED, early):
         leave(index)
     over_x(early).start()
     over_x(early + 1).start()
@@ -1457,6 +1502,13 @@
     grad_two = lax.fori_loop(0, sequences, lower_part, nothing)
     for copy in bring[6:]:
         copy.wait()
+
+    @pl.when(core == 0)
+    def _():
+        for index in range(SETTLED):
+            whole(index, (sum_up, sum_down), side_x)[...] = summed_x(index)[...]
+            spread(index)
+
     turned[...] = jnp.transpose(mixed[...])
     first, size = columns[pairs]
     part[:, :, first : first + size] = (
@@ -1517,7 +1569,7 @@
         else:
             sum_x(pair - 2)
         if pair == 2:
-            for index in range(early):
+            for index in range(SETTLED, early):
                 add_home(index)
             add_x(early + 2)
             add_x(early + 3)
@@ -1534,6 +1586,11 @@
         return carry + share[None, :]
 
     grad_one = lax.fori_loop(0, sequences, upper_part, nothing)
+    leaving = (
+        pltpu.make_async_copy(tokens_grad, tokens_grad_out, bring_sems.at[len(bring)]),
+        pltpu.make_async_copy(output, output_out, bring_sems.at[len(bring) + 1]),
+    )
+    leaving[0].start()
     lines = lax.broadcasted_iota(jnp.int32, (128, width), 0)
     gain_lines = jnp.where(
         lines == count, grad_one, jnp.where(lines == count + 1, grad_two, 0.0)
@@ -1544,9 +1601,17 @@
     )
     to_mate(pairs + 1, 0).start()
     to_mate(pairs + 1, 1).start()
+    for index in range(SETTLED):
+        pass_half(index)
     sum_core(pairs - 1)
     sum_core(pairs + 1)
     sum_x(pairs - 2)
+    add_home(early)
+    add_home(early + 1)
+    sum_x(pairs - 1)
+    sum_x(pairs + 1)
+    for index in range(SETTLED, early):
+        pass_half(index)
     keep.wait()
 
     def from_all(step, carry):
@@ -1566,19 +1631,14 @@
         return carry
 
     lax.fori_loop(0, sequences, combine, 0)
-    sum_x(pairs - 1)
-    sum_x(pairs + 1)
-    for index in range(early):
-        pass_half(index)
-    add_home(early)
-    add_home(early + 1)
-    for chunk in range(pairs):
-        sum_ep(chunk)
-    sum_ep(pairs + 1)
+    leaving[1].start()
     add_home(early + 2)
     pass_half(early)
     pass_half(early + 1)
     add_home(early + 3)
+    for chunk in range(pairs):
+        sum_ep(chunk)
+    sum_ep(pairs + 1)
     pass_half(early + 2)
     pass_half(early + 3)
 
@@ -1591,11 +1651,14 @@
 
     @pl.when(core == 1)
     def _():
+        for index in range(SETTLED, CHUNKS):
+            go_home(index).wait_send()
         for chunk in range(CHUNKS):
-            go_home(chunk).wait_send()
             own_half(chunk).wait_recv()
             other_half(chunk).wait_recv()
 
+    for copy in leaving:
+        copy.wait()
     for index in range(early, len(parts)):
         over_x(index).wait_send()
     for chunk in range(len(columns)):
@@ -1648,7 +1711,7 @@
             jax.ShapeDtypeStruct(part_down.shape, low),
         ),
         in_specs=[hbm, vmem, vmem] + [hbm] * 9 + [vmem] + [hbm] * 4,
-        out_specs=(vmem,) * 7,
+        out_specs=(hbm,) * 2 + (vmem,) * 5,
         scratch_shapes=[
             pltpu.VMEM(array.shape, array.dtype)
             for array in (
@@ -1668,6 +1731,8 @@
             )
         ]
         + [
+            pltpu.VMEM((row_count, width), low),
+            pltpu.VMEM((row_count, width), jnp.float32),
             pltpu.VMEM(back.shape, low),
             pltpu.VMEM(joint.shape, low),
             pltpu.VMEM((row_count, width), low),
@@ -1693,7 +1758,7 @@
             pltpu.SemaphoreType.DMA((2, HEADS // 2 + 2, count)),
             pltpu.SemaphoreType.DMA((10, CHUNKS)),
             pltpu.SemaphoreType.DMA((1,)),
-            pltpu.SemaphoreType.DMA((13,)),
+            pltpu.SemaphoreType.DMA((15,)),
         ],
         compiler_params=pltpu.CompilerParams(
             collective_id=4, has_side_effects=True, vmem_limit_bytes=63 * MIB
@@ -1717,6 +1782,88 @@
         early_up,
         early_down,
     )
+
+
+def finish_kernel(
+    copied_in,
+    pack,
+    summed_in,
+    copied_out,
+    pack_out,
+    summed_out,
+    copied,
+    narrow,
+    wide,
+    in_sems,
+    out_sems,
+    piece_sems,
+):
+    arrive = [
+        pltpu.make_async_copy(source, target, in_sems.at[place])
+        for place, (source, target) in enumerate(zip(copied_in, copied))
+    ]
+    leave = [
+        pltpu.make_async_copy(source, target, out_sems.at[place])
+        for place, (source, target) in enumerate(zip(copied, copied_out))
+    ]
+
+    def piece(layer, number):
+        size = narrow[layer].shape[0] // PIECES
+        rows = pl.ds(number * size, size)
+        return (
+            pltpu.make_async_copy(
+                summed_in[layer].at[rows], narrow[layer].at[rows], piece_sems.at[0, layer, number]
+            ),
+            pltpu.make_async_copy(
+                wide[layer].at[rows], summed_out[layer].at[rows], piece_sems.at[1, layer, number]
+            ),
+            rows,
+        )
+
+    pieces = [piece(layer, number) for number in range(PIECES) for layer in range(2)]
+    for number, part in enumerate(pieces):
+        part[0].start()
+        if number < len(arrive):
+            arrive[number].start()
+    shard_rows = pack.shape[0]
+    tall = jnp.concatenate([pack[...], jnp.zeros((128 - shard_rows, 128), jnp.float32)], axis=0)
+    pack_out[...] = jnp.transpose(tall)[:16, :shard_rows]
+    for number, (load, store, rows) in enumerate(pieces):
+        load.wait()
+        wide[number % 2][rows, :] = narrow[number % 2][rows, :].astype(jnp.float32)
+        store.start()
+        if number < len(arrive):
+            arrive[number].wait()
+            leave[number].start()
+    for copy in leave:
+        copy.wait()
+    for _, store, _ in pieces:
+        store.wait()
+
+
+def finish(copied, pack, summed):
+    hbm = pl.BlockSpec(memory_space=pltpu.HBM)
+    vmem = pl.BlockSpec(memory_space=pltpu.VMEM)
+    wide = [jax.ShapeDtypeStruct(array.shape, jnp.float32) for array in summed]
+    return pl.pallas_call(
+        finish_kernel,
+        out_shape=(
+            [jax.ShapeDtypeStruct(array.shape, array.dtype) for array in copied],
+            jax.ShapeDtypeStruct((16, pack.shape[0]), jnp.float32),
+            wide,
+        ),
+        in_specs=[[hbm] * len(copied), vmem, [hbm] * 2],
+        out_specs=([hbm] * len(copied), vmem, [hbm] * 2),
+        scratch_shapes=[
+            [pltpu.VMEM(array.shape, array.dtype) for array in copied],
+            [pltpu.VMEM(array.shape, array.dtype) for array in summed],
+            [pltpu.VMEM(array.shape, jnp.float32) for array in summed],
+            pltpu.SemaphoreType.DMA((len(copied),)),
+            pltpu.SemaphoreType.DMA((len(copied),)),
+            pltpu.SemaphoreType.DMA((2, 2, PIECES)),
+        ],
+        compiler_params=pltpu.CompilerParams(vmem_limit_bytes=63 * MIB),
+    )(copied, pack, summed)
 
 
 def per_device_fused(
@@ -1777,16 +1924,19 @@
         early_up,
         early_down,
     )
+    (output, tokens_grad, grad_joint, grad_output), lines, (grad_up, grad_down) = finish(
+        [output, tokens_grad, grad_joint, grad_output], grad_pack, [grad_up, grad_down]
+    )
     return (
         output,
         tokens_grad,
-        grad_pack[:, experts],
+        lines[experts],
         grad_joint,
         grad_output,
-        grad_pack[:, experts + 1],
-        grad_pack[:, :experts],
-        grad_up.astype(jnp.float32)[None],
-        grad_down.astype(jnp.float32)[None],
+        lines[experts + 1],
+        lines[:experts].T,
+        grad_up[None],
+        grad_down[None],
     )
 
 

time: 261 us -> 249 us (0.954)
  other arithmetic: 8.08 us -> 1.19 us
  local copies, waits for them, and re-layouts: 7.39 us -> 2.54 us
    pallas_call x1, Pallas kernels: 89.8 us -> 79.2 us  [backward(): pl.pallas_call(functools.partial(backward_kernel, count), out_shape=(jax....]
    pallas_call x0 -> x1, Pallas kernels: none -> 8.48 us  [finish(): pl.pallas_call(finish_kernel, out_shape=([jax.ShapeDtypeStruct(array.shap...]
    broadcast_in_dim x2 -> x0, other arithmetic: 6.89 us -> none  [the longest x1 4.28 us: per_device_fused(): grad_up.astype(jnp.float32)[None]]
    unnamed x15 -> x0, local copies, waits for them, and re-layouts: 5.91 us -> none
where the time goes in v5:
time: 249 us
  Pallas kernels  245 us (98%)
  local copies, waits for them, and re-layouts  2.54 us (1%)
    pallas_call x1, Pallas kernels, middle(): pl.pallas_call(functools.partial(middle_kernel, count), out_shape=(jax.Sh...  84.3 us
    pallas_call x1, Pallas kernels, backward(): pl.pallas_call(functools.partial(backward_kernel, count), out_shape=(jax....  79.2 us
    pallas_call x1, Pallas kernels, forward(): pl.pallas_call(functools.partial(forward_kernel, count, capacity), out_sh...  72.5 us
    pallas_call x1, Pallas kernels, finish(): pl.pallas_call(finish_kernel, out_shape=([jax.ShapeDtypeStruct(array.shap...  8.48 us

profile of v5, /device:TPU:0, one launch (start us, length us, event | category | flops | bytes accessed | tf_op | source)
XLA Modules:
  0.0 248.9 jit_solution(14943593344876137604)
XLA Ops:
  0.6 1.2 pad_maximum_fusion.gains_shard
  1.8 72.5 %shard_map.196 = (bf16[32,16,2176]{2,1,0:T(8,128)(2,1)}, bf16[1024,1536]{1,0:T(8,128)(2,1)}, bf16[1024,512]{1,0:T(8,128)(2,1)}, f32[1024,512]{1,0:T(8,128)}, bf1...) custom-call(bf16[1024,512]{1,0:T(8,128)(2,1)} %tokens_in.3, ...), custom_call_target="tpu_custom_call" | custom-call | tf_op jit(solution)/shard_map/pallas_call | solution.py:800
  74.3 84.3 %shard_map.197 = (bf16[8,272,512]{2,1,0:T(8,128)(2,1)}, bf16[8,272,512]{2,1,0:T(8,128)(2,1)}, bf16[512,2048]{1,0:T(8,128)(2,1)}, bf16[2048,512]{1,0:T(8,128)(2,1...) custom-call(bf16[8,272,512]{2,1,0:T(8,128)(2,1)} %get-tuple-element.47.sent_rows, ...), custom_call_target="tpu_custom_call" | custom-call | flops 27380416512 | bytes 16777216 | tf_op jit(solution)/shard_map/pallas_call | solution.py:1131
  158.7 79.2 %shard_map.198 = (bf16[1024,512]{1,0:T(8,128)(2,1)}, f32[1024,512]{1,0:T(8,128)}, f32[16,1536]{1,0:T(8,128)}, f32[16,512]{1,0:T(8,128)}, f32[16,128]{1,0:T(8,128...) custom-call(bf16[1024,512]{1,0:T(8,128)(2,1)} %tokens_in.3, s32[4,256]{1,0:T(4,128)} %segments.3, s32[4,256]{1,0:T(4,128)} %live.3, ...), custom_call_target="tpu_custom_call" | custom-call | tf_op jit(solution)/shard_map/pallas_call | solution.py:1702
  237.9 8.5 %shard_map.199 = (bf16[1024,512]{1,0:T(8,128)(2,1)}, f32[1024,512]{1,0:T(8,128)}, f32[16,1536]{1,0:T(8,128)}, f32[16,512]{1,0:T(8,128)}, f32[16,16]{1,0:T(8,128)...) custom-call(bf16[1024,512]{1,0:T(8,128)(2,1)} %get-tuple-element.59.copied_in_0_, ...), custom_call_target="tpu_custom_call" | custom-call | tf_op jit(solution)/shard_map/pallas_call | solution.py:1848
  246.4 1.3 slice_bitcast_fusion.1
  247.7 1.3 slice_bitcast_fusion

commit v6 on v5

--- a/solution.py
+++ b/solution.py
@@ -523,8 +523,8 @@
         @pl.when(core == 0)
         def _():
             fetch(chunk).wait_send()
-            if chunk + 2 < CHUNKS:
-                fetch(chunk + 2).start()
+            if chunk + 3 < CHUNKS:
+                fetch(chunk + 3).start()
 
         @pl.when(core == 1)
         def _():
@@ -571,6 +571,7 @@
     def _():
         fetch(0).start()
         fetch(1).start()
+        fetch(2).start()
 
     ints = jnp.concatenate([segments[...], live[...]], axis=0).astype(jnp.float32)
     turned = jnp.transpose(ints)
@@ -1030,7 +1031,7 @@
         return carry
 
     def second_half(index, carry):
-        step = visit(index, count)
+        step = visit(count - 1 - index, count)
         mine = rows[step]
         cotangent = grads[step].astype(jnp.float32)
         place = pl.ds(pl.multiple_of(step * block, 16), block)

time: 249 us -> 239 us (0.960)
  Pallas kernels: 245 us -> 234 us
    pallas_call x1, Pallas kernels: 84.3 us -> 79.5 us  [middle(): pl.pallas_call(functools.partial(middle_kernel, count), out_shape=(jax.Sh...]
    pallas_call x1, Pallas kernels: 79.2 us -> 74.8 us  [backward(): pl.pallas_call(functools.partial(backward_kernel, count), out_shape=(jax....]
where the time goes in v6:
time: 239 us
  Pallas kernels  234 us (98%)
  local copies, waits for them, and re-layouts  2.54 us (1%)
    pallas_call x1, Pallas kernels, middle(): pl.pallas_call(functools.partial(middle_kernel, count), out_shape=(jax.Sh...  79.5 us
    pallas_call x1, Pallas kernels, backward(): pl.pallas_call(functools.partial(backward_kernel, count), out_shape=(jax....  74.8 us
    pallas_call x1, Pallas kernels, forward(): pl.pallas_call(functools.partial(forward_kernel, count, capacity), out_sh...  71.3 us
    pallas_call x1, Pallas kernels, finish(): pl.pallas_call(finish_kernel, out_shape=([jax.ShapeDtypeStruct(array.shap...  8.48 us

profile of v6, /device:TPU:0, one launch (start us, length us, event | category | flops | bytes accessed | tf_op | source)
XLA Modules:
  0.0 238.5 jit_solution(7003282105408472327)
XLA Ops:
  0.6 1.2 pad_maximum_fusion.gains_shard
  1.8 71.3 %shard_map.196 = (bf16[32,16,2176]{2,1,0:T(8,128)(2,1)}, bf16[1024,1536]{1,0:T(8,128)(2,1)}, bf16[1024,512]{1,0:T(8,128)(2,1)}, f32[1024,512]{1,0:T(8,128)}, bf1...) custom-call(bf16[1024,512]{1,0:T(8,128)(2,1)} %tokens_in.3, ...), custom_call_target="tpu_custom_call" | custom-call | tf_op jit(solution)/shard_map/pallas_call | solution.py:801
  73.2 79.5 %shard_map.197 = (bf16[8,272,512]{2,1,0:T(8,128)(2,1)}, bf16[8,272,512]{2,1,0:T(8,128)(2,1)}, bf16[512,2048]{1,0:T(8,128)(2,1)}, bf16[2048,512]{1,0:T(8,128)(2,1...) custom-call(bf16[8,272,512]{2,1,0:T(8,128)(2,1)} %get-tuple-element.47.sent_rows, ...), custom_call_target="tpu_custom_call" | custom-call | flops 27380416512 | bytes 16777216 | tf_op jit(solution)/shard_map/pallas_call | solution.py:1132
  152.7 74.8 %shard_map.198 = (bf16[1024,512]{1,0:T(8,128)(2,1)}, f32[1024,512]{1,0:T(8,128)}, f32[16,1536]{1,0:T(8,128)}, f32[16,512]{1,0:T(8,128)}, f32[16,128]{1,0:T(8,128...) custom-call(bf16[1024,512]{1,0:T(8,128)(2,1)} %tokens_in.3, s32[4,256]{1,0:T(4,128)} %segments.3, s32[4,256]{1,0:T(4,128)} %live.3, ...), custom_call_target="tpu_custom_call" | custom-call | tf_op jit(solution)/shard_map/pallas_call | solution.py:1703
  227.5 8.5 %shard_map.199 = (bf16[1024,512]{1,0:T(8,128)(2,1)}, f32[1024,512]{1,0:T(8,128)}, f32[16,1536]{1,0:T(8,128)}, f32[16,512]{1,0:T(8,128)}, f32[16,16]{1,0:T(8,128)...) custom-call(bf16[1024,512]{1,0:T(8,128)(2,1)} %get-tuple-element.59.copied_in_0_, ...), custom_call_target="tpu_custom_call" | custom-call | tf_op jit(solution)/shard_map/pallas_call | solution.py:1849
  236.0 1.3 slice_bitcast_fusion.1
  237.3 1.3 slice_bitcast_fusion

commit v7 on v6

--- a/solution.py
+++ b/solution.py
@@ -1378,11 +1378,13 @@
     keep = pltpu.make_async_copy(out_ret.at[0], returned.at[expert], local_sems.at[0])
     keep.start()
 
-    def start(step, carry):
-        send_ret(step).start()
-        return carry
-
-    lax.fori_loop(1, count, start, 0)
+    half_ep = count // 2
+    far_steps = [step for step in range(count) if step % half_ep >= half_ep // 2]
+    for step in range(1, count):
+        if step not in far_steps:
+            send_ret(step).start()
+    send_ret(far_steps[0]).start()
+    send_ret(far_steps[1]).start()
     pairs = HEADS // 2
     columns = [(pair * 384, 384) for pair in range(pairs)]
     columns += [(joint_width, width), (joint_width + width, 128)]
@@ -1575,6 +1577,9 @@
             add_x(early + 2)
             add_x(early + 3)
             sum_ep(pairs)
+        if pair == 1:
+            send_ret(far_steps[2]).start()
+            send_ret(far_steps[3]).start()
 
     def upper_part(number, carry):
         rows = pl.ds(pl.multiple_of(number * length, length), length)

time: 239 us -> 235 us (0.983)
  Pallas kernels: 234 us -> 230 us
    pallas_call x1, Pallas kernels: 74.8 us -> 70.6 us  [backward(): pl.pallas_call(functools.partial(backward_kernel, count), out_shape=(jax....]
where the time goes in v7:
time: 235 us; the launch traced here: 234 us
  Pallas kernels  230 us (98%)
  local copies, waits for them, and re-layouts  2.54 us (1%)
    pallas_call x1, Pallas kernels, middle(): pl.pallas_call(functools.partial(middle_kernel, count), out_shape=(jax.Sh...  79.5 us
    pallas_call x1, Pallas kernels, forward(): pl.pallas_call(functools.partial(forward_kernel, count, capacity), out_sh...  71.3 us
    pallas_call x1, Pallas kernels, backward(): pl.pallas_call(functools.partial(backward_kernel, count), out_shape=(jax....  70.6 us
    pallas_call x1, Pallas kernels, finish(): pl.pallas_call(finish_kernel, out_shape=([jax.ShapeDtypeStruct(array.shap...  8.48 us

profile of v7, /device:TPU:0, one launch (start us, length us, event | category | flops | bytes accessed | tf_op | source)
XLA Modules:
  0.0 234.3 jit_solution(6517144666408370239)
XLA Ops:
  0.6 1.2 pad_maximum_fusion.gains_shard
  1.8 71.3 %shard_map.196 = (bf16[32,16,2176]{2,1,0:T(8,128)(2,1)}, bf16[1024,1536]{1,0:T(8,128)(2,1)}, bf16[1024,512]{1,0:T(8,128)(2,1)}, f32[1024,512]{1,0:T(8,128)}, bf1...) custom-call(bf16[1024,512]{1,0:T(8,128)(2,1)} %tokens_in.3, ...), custom_call_target="tpu_custom_call" | custom-call | tf_op jit(solution)/shard_map/pallas_call | solution.py:801
  73.2 79.5 %shard_map.197 = (bf16[8,272,512]{2,1,0:T(8,128)(2,1)}, bf16[8,272,512]{2,1,0:T(8,128)(2,1)}, bf16[512,2048]{1,0:T(8,128)(2,1)}, bf16[2048,512]{1,0:T(8,128)(2,1...) custom-call(bf16[8,272,512]{2,1,0:T(8,128)(2,1)} %get-tuple-element.47.sent_rows, ...), custom_call_target="tpu_custom_call" | custom-call | flops 27380416512 | bytes 16777216 | tf_op jit(solution)/shard_map/pallas_call | solution.py:1132
  152.7 70.6 %shard_map.198 = (bf16[1024,512]{1,0:T(8,128)(2,1)}, f32[1024,512]{1,0:T(8,128)}, f32[16,1536]{1,0:T(8,128)}, f32[16,512]{1,0:T(8,128)}, f32[16,128]{1,0:T(8,128...) custom-call(bf16[1024,512]{1,0:T(8,128)(2,1)} %tokens_in.3, s32[4,256]{1,0:T(4,128)} %segments.3, s32[4,256]{1,0:T(4,128)} %live.3, ...), custom_call_target="tpu_custom_call" | custom-call | tf_op jit(solution)/shard_map/pallas_call | solution.py:1708
  223.3 8.5 %shard_map.199 = (bf16[1024,512]{1,0:T(8,128)(2,1)}, f32[1024,512]{1,0:T(8,128)}, f32[16,1536]{1,0:T(8,128)}, f32[16,512]{1,0:T(8,128)}, f32[16,16]{1,0:T(8,128)...) custom-call(bf16[1024,512]{1,0:T(8,128)(2,1)} %get-tuple-element.59.copied_in_0_, ...), custom_call_target="tpu_custom_call" | custom-call | tf_op jit(solution)/shard_map/pallas_call | solution.py:1854
  231.7 1.3 slice_bitcast_fusion.1
  233.0 1.3 slice_bitcast_fusion
